TPU v7x, 256 devices: a whole 4x4x8 slice. The times are simulated.
256 devices in a mesh: member: 16 (over z_lo, x), grid: 16 (over z_hi, y, core).
Axes of the slice: x: 4, y: 4, z: 8 (z_hi: 2, z_lo: 4; z = z_hi * 4 + z_lo), core: 2. Of those that a mesh axis runs over, the one named last changes fastest.
Arguments:
- slabs: bfloat16 [16, 4096, 256], P('member', 'grid'), may hold values from -6 to 6
- loader: int32 [1], replicated, may hold values from 0 to 15
- hidden_jitter: bfloat16 [16, 2048, 16], P('member', 'grid'), may hold values from -3 to 3
- w_noise: bfloat16 [16, 1024], replicated, may hold values from -1.5 to 1.5
- w_enc: bfloat16 [128, 1024], replicated, may hold values from -0.10986328 to 0.10986328
- enc_offset: int32 [2048, 8], P('grid'), may hold values from -128 to 128
- enc_weight: float32 [2048, 8], P('grid'), may hold values from -1 to 1
- w_qkv: bfloat16 [1024, 1536], replicated, may hold values from -0.1875 to 0.1875
- window_offset: int32 [2048], P('grid'), may hold values from -64 to 0
- w_out: bfloat16 [512, 1024], replicated, may hold values from -0.25 to 0.25
- unpacker_linear_map: bfloat16 [1024, 128], replicated, may hold values from -0.1875 to 0.1875
- dec_offset: int32 [4096, 3], P('grid'), may hold values from -64 to 64
- unpacker_arc_scales: float32 [4096, 3], P('grid'), may hold values from 0.2 to 1
Outputs:
- grad_noise: float32 [16, 1024], P(None, ('member', 'grid'))
- grad_enc: float32 [128, 1024], P(None, ('member', 'grid'))
- grad_qkv: float32 [1024, 1536], P(('member', 'grid'))
- grad_out: float32 [512, 1024], P(None, ('member', 'grid'))
- unpacker_map_sensitivity: float32 [1024, 128], P(('member', 'grid'))
All inputs are finite; a program needn't handle non-finite values.
Results may differ from a plain program's by a relative error of at most 0.0075.
Values may be sent and summed in bfloat16 or wider, within the bound.
No kernel may reach another device: no remote copies, remote signals or barrier semaphores. Data moves between devices by JAX's collectives and lax.ppermute only.
A program may use at most 128 MiB of HBM per device.

v0:
```python
import jax
import jax.numpy as jnp
from jax import lax
from jax.sharding import Mesh
from jax.sharding import PartitionSpec as P

HEAD_DIM = 64
RIM_G = 128
RIM_H = 64
WIN = 64

EPS = 1e-06
DELTA_SQ = 0.01

MEMBER = ("zl", "x")
GRID = ("zh", "y", "core")
F32 = jnp.float32
BF16 = jnp.bfloat16
HIGHEST = lax.Precision.HIGHEST


def rms_factor(values):
    return lax.rsqrt(jnp.mean(values * values, axis=-1, keepdims=True) + EPS)


def rms_back(values, factor, gradient):
    inner = jnp.mean(gradient * values, axis=-1, keepdims=True)
    return factor * gradient - values * (factor * factor * factor) * inner


def silu_slope(pre):
    sigma = jax.nn.sigmoid(pre)
    return sigma * (1.0 + pre * (1.0 - sigma))


def eased_sensitivity(diff):
    return diff * lax.rsqrt(diff * diff + DELTA_SQ)


def dot(left, right, dims, **options):
    return lax.dot_general(left, right, (dims, ((), ())), preferred_element_type=F32, **options)


NN = ((1,), (0,))
TN = ((0,), (0,))
NT = ((1,), (1,))


def two_terms(values):
    high = lax.reduce_precision(values, 8, 7)
    return high.astype(BF16), (values - high).astype(BF16)


def three_terms(values):
    high = lax.reduce_precision(values, 8, 7)
    middle = lax.reduce_precision(values - high, 8, 7)
    return [high.astype(BF16), middle.astype(BF16), (values - high - middle).astype(BF16)]


def swap(values, axes):
    return lax.all_to_all(values, axes, split_axis=0, concat_axis=0, tiled=True)


def shifted(values, step):
    count = lax.axis_size(GRID)
    return lax.ppermute(values, GRID, [(i, (i + step) % count) for i in range(count)])


def per_device(
    slabs,
    loader,
    hidden_jitter,
    w_noise,
    w_enc,
    enc_offset,
    enc_weight,
    w_qkv,
    window_offset,
    w_out,
    unpacker_linear_map,
    dec_offset,
    unpacker_arc_scales,
):
    members = lax.axis_size(MEMBER)
    shards = lax.axis_size(GRID)
    channels, width = w_enc.shape
    attn = w_out.shape[0]
    heads = attn // HEAD_DIM
    points = slabs.shape[1]
    nodes = enc_offset.shape[0]
    per_node = points // nodes
    sub = points // members
    noise = w_noise.shape[0]
    k_enc = enc_offset.shape[1]
    k_dec = dec_offset.shape[1]
    inv_root = HEAD_DIM ** (-0.5)

    pieces = swap(slabs[0].reshape(members, sub, 2 * channels), MEMBER)
    piece = lax.dynamic_index_in_dim(pieces, loader[0], 0, keepdims=False)
    truth = piece[:, channels:].astype(F32)

    packed = jnp.concatenate(
        [enc_offset.astype(BF16)]
        + three_terms(enc_weight)
        + [window_offset[:, None].astype(BF16)]
        + [dec_offset.reshape(nodes, per_node * k_dec).astype(BF16)]
        + three_terms(unpacker_arc_scales.reshape(nodes, per_node * k_dec)),
        axis=1,
    )
    packed = jnp.pad(packed, ((0, 0), (0, channels - packed.shape[1])))
    share = nodes // members
    member = lax.axis_index(MEMBER)
    shard = lax.axis_index(GRID)
    jitter_rows = nodes * noise // channels
    chunk = jnp.concatenate(
        [
            piece[:, :channels],
            hidden_jitter[0].reshape(jitter_rows, channels),
            lax.dynamic_slice_in_dim(packed, member * share, share, 0),
        ],
        axis=0,
    )
    got = swap(jnp.broadcast_to(chunk[None], (shards,) + chunk.shape), GRID)
    far2, low, mid, high, far1 = (
        lax.dynamic_index_in_dim(got, (shard + o) % shards, 0, keepdims=False)
        for o in (-2, -1, 0, 1, 2)
    )
    at = sub + jitter_rows
    far = jnp.where(member >= members // 2, far2[:sub], far1[:sub])
    payload = jnp.concatenate(
        [low[:sub], mid[:sub], high[:sub], far, low[at:], mid[at:], high[at:]], axis=0
    )
    got = swap(jnp.broadcast_to(payload[None], (members,) + payload.shape), MEMBER)
    x_parts = [
        got[:, i * sub : (i + 1) * sub].reshape(points, channels) for i in range(3)
    ]
    x_own = x_parts[1]
    far = got[:, 3 * sub : 4 * sub]
    x_all = jnp.concatenate(
        [far[members // 2 :].reshape(-1, channels)]
        + x_parts
        + [far[: members // 2].reshape(-1, channels)],
        axis=0,
    )
    packed = got[:, 4 * sub :].reshape(members, 3, share, channels)
    packed = packed.transpose(1, 0, 2, 3).reshape(3 * nodes, channels)
    jitter_all = jnp.concatenate([low[sub:at], mid[sub:at], high[sub:at]], axis=0)
    jitter_all = jitter_all.reshape(3 * nodes, noise)
    packed = packed.astype(F32)

    def column(start, count):
        return packed[:, start : start + count]

    def summed(start, count):
        return sum(column(start + i * count, count) for i in range(1, 3)) + column(start, count)

    enc_offset_all = column(0, k_enc).astype(jnp.int32)
    enc_weight_all = summed(k_enc, k_enc)
    at = 4 * k_enc
    window_all = column(at, 1).astype(jnp.int32)
    at += 1
    each = per_node * k_dec
    dec_offset_all = column(at, each).astype(jnp.int32).reshape(3 * points, k_dec)
    dec_scale_all = summed(at + each, each).reshape(3 * points, k_dec)

    reach = points + 2 * RIM_G
    pre_enc = dot(x_all, w_enc, NN)
    messages = jax.nn.silu(pre_enc).astype(BF16)
    home = (jnp.arange(3 * nodes, dtype=jnp.int32) % nodes) * per_node
    source = home[:, None] + enc_offset_all + RIM_G
    span = lax.broadcasted_iota(jnp.int32, (3 * nodes, reach), 1)
    spread = jnp.zeros((3 * nodes, reach), F32)
    for k in range(k_enc):
        spread = spread + jnp.where(
            source[:, k : k + 1] == span, enc_weight_all[:, k : k + 1], 0.0
        )
    spread_high, spread_low = two_terms(spread)
    pooled = []
    for s in range(3):
        rows = slice(s * nodes, (s + 1) * nodes)
        near = messages[s * points : s * points + reach]
        pooled.append(dot(spread_high[rows], near, NN) + dot(spread_low[rows], near, NN))
    pooled = jnp.concatenate(pooled, axis=0)
    factor0 = rms_factor(pooled)
    state0 = pooled * factor0 + dot(jitter_all, w_noise, NN)
    factor1 = rms_factor(state0)
    normed = (state0 * factor1).astype(BF16)
    mixed = dot(normed, w_qkv, NN).reshape(3 * nodes, 3, heads, HEAD_DIM)

    own = slice(nodes, 2 * nodes)
    asked = slice(nodes - WIN, 2 * nodes + WIN)
    n_asked = nodes + 2 * WIN
    own_asked = slice(WIN, WIN + nodes)
    queries = mixed[asked, 0]
    key_raw = mixed[:, 1]
    query_factor = rms_factor(queries)
    key_factor = rms_factor(key_raw)
    query_norm = (queries * query_factor).astype(BF16)
    key_norm = (key_raw * key_factor).astype(BF16)
    value_rows = mixed[:, 2].astype(BF16)
    relative = (
        jnp.arange(3 * nodes, dtype=jnp.int32)[None, :]
        - WIN
        - jnp.arange(n_asked, dtype=jnp.int32)[:, None]
    )
    offsets = window_all[asked]
    allowed = ((relative >= offsets) & (relative < offsets + WIN)).astype(F32)
    scores = (
        jnp.einsum("qhd,khd->hqk", query_norm, key_norm, preferred_element_type=F32) * inv_root
    )
    weights_exp = jnp.exp(scores) * allowed[None]
    prob = (weights_exp / jnp.sum(weights_exp, axis=-1, keepdims=True)).astype(BF16)
    attended = jnp.einsum("hqk,khd->qhd", prob, value_rows, preferred_element_type=F32)
    attended = attended.astype(BF16).reshape(n_asked, attn)
    state1 = state0[asked] + dot(attended, w_out, NN)
    factor2 = rms_factor(state1)
    dnorm = (state1 * factor2).astype(BF16)

    projected = dot(dnorm, unpacker_linear_map, NN)
    homeh = jnp.arange(3 * points, dtype=jnp.int32) // per_node - nodes + RIM_H
    dec_source = homeh[:, None] + dec_offset_all
    dec_span = lax.broadcasted_iota(jnp.int32, (3 * points, n_asked), 1)
    arcs = jnp.zeros((3 * points, n_asked), F32)
    for k in range(k_dec):
        arcs = arcs + jnp.where(
            dec_source[:, k : k + 1] == dec_span, dec_scale_all[:, k : k + 1], 0.0
        )
    restored = dot(arcs[points : 2 * points], projected, NN, precision=HIGHEST)
    forecast = x_own.astype(F32) + restored

    cells = swap(forecast.reshape(members, sub, channels), MEMBER)
    loss_scale = float(members * points * shards * channels) ** (-0.5)
    fair = jnp.sum(eased_sensitivity(cells[:, None] - cells[None, :]), axis=1)
    sensitivity = (
        eased_sensitivity(cells - truth[None]) / members - fair / (members * (members - 1))
    ) * loss_scale
    grad_forecast = swap(sensitivity.astype(BF16), MEMBER).reshape(points, channels)
    grad_forecast = jnp.concatenate(
        [shifted(grad_forecast, 1), grad_forecast, shifted(grad_forecast, -1)], axis=0
    ).astype(F32)

    zl, x = (lax.axis_size(a) for a in MEMBER)
    zh, y, core = (lax.axis_size(a) for a in GRID)
    rows = width // (members * shards)
    order = jnp.arange(width, dtype=jnp.int32).reshape(core, x, y, zl, zh, rows)
    c_i, x_i, y_i, zl_i, zh_i, r_i = (
        lax.broadcasted_iota(jnp.int32, order.shape, d) for d in range(6)
    )
    target = ((((zl_i * x + x_i) * zh + zh_i) * y + y_i) * core + c_i) * rows + r_i
    target = target.reshape(1, width)
    reorder = (lax.broadcasted_iota(jnp.int32, (width, width), 0) == target).astype(BF16)

    def reordered(values):
        return dot(values, reorder, NN).astype(BF16)

    grad_projected = dot(arcs, grad_forecast, TN, precision=HIGHEST)
    gp_high, gp_low = two_terms(grad_projected)
    dnorm_r = reordered(dnorm[own_asked])
    dec_term = dot(dnorm_r, gp_high[own_asked], TN) + dot(dnorm_r, gp_low[own_asked], TN)
    grad_dnorm = dot(gp_high, unpacker_linear_map, NT) + dot(gp_low, unpacker_linear_map, NT)
    grad_state1 = rms_back(state1, factor2, grad_dnorm)
    grad_state1_b = grad_state1.astype(BF16)
    out_term = dot(reordered(grad_state1_b[own_asked]), attended[own_asked], TN)
    grad_attended = dot(grad_state1_b, w_out, NT).astype(BF16).reshape(n_asked, heads, HEAD_DIM)
    grad_probs = jnp.einsum("qhd,khd->hqk", grad_attended, value_rows, preferred_element_type=F32)
    prob_wide = prob.astype(F32)
    grad_scores = (
        prob_wide * (grad_probs - jnp.sum(prob_wide * grad_probs, axis=-1, keepdims=True))
    ).astype(BF16)
    grad_qnorm = (
        jnp.einsum(
            "hqk,khd->qhd", grad_scores[:, own_asked], key_norm, preferred_element_type=F32
        )
        * inv_root
    )
    grad_knorm = (
        jnp.einsum("hqk,qhd->khd", grad_scores[:, :, own], query_norm, preferred_element_type=F32)
        * inv_root
    )
    grad_values = jnp.einsum(
        "hqk,qhd->khd", prob[:, :, own], grad_attended, preferred_element_type=F32
    )
    grad_queries = rms_back(queries[own_asked], query_factor[own_asked], grad_qnorm)
    grad_keys = rms_back(key_raw[own], key_factor[own], grad_knorm)
    grad_mixed = (
        jnp.stack([grad_queries, grad_keys, grad_values], axis=1)
        .reshape(nodes, 3 * attn)
        .astype(BF16)
    )
    qkv_term = dot(reordered(normed[own]), grad_mixed, TN)
    grad_normed = dot(grad_mixed, w_qkv, NT)
    grad_state0 = grad_state1[own_asked] + rms_back(state0[own], factor1[own], grad_normed)
    grad_state0_r = reordered(grad_state0.astype(BF16))
    jitter_own = jnp.pad(hidden_jitter[0], ((0, 0), (0, 128 - noise)))
    noise_term = dot(grad_state0_r, jitter_own, TN)
    grad_pooled = rms_back(pooled[own], factor0[own], grad_state0)
    grad_messages = dot(spread[own], grad_pooled, TN, precision=HIGHEST)
    near = slice(points, points + reach)
    grad_pre = grad_messages * silu_slope(pre_enc[near])
    enc_term = dot(x_all[near].astype(F32), grad_pre, TN, precision=HIGHEST)
    enc_term = dot(reorder, enc_term.astype(BF16), ((0,), (1,)))

    parts = (qkv_term, out_term, enc_term, dec_term, noise_term)
    total = jnp.concatenate([part.astype(BF16) for part in parts], axis=1)
    lanes = total.shape[1]
    total = total.reshape(core, width // core, lanes)
    side = lax.axis_index("core")
    kept = lax.dynamic_index_in_dim(total, side, 0, keepdims=False)
    sent = lax.dynamic_index_in_dim(total, 1 - side, 0, keepdims=False)
    total = kept.astype(F32) + lax.ppermute(sent, "core", [(0, 1), (1, 0)]).astype(F32)
    total = swap(total.astype(BF16).reshape(x * y, -1, lanes), ("x", "y"))
    total = jnp.sum(total.astype(F32), axis=0)
    total = swap(total.astype(BF16).reshape(zl * zh, rows, lanes), ("zl", "zh"))
    total = jnp.sum(total.astype(F32), axis=0)
    cuts = []
    at = 0
    for part in parts:
        cuts.append(total[:, at : at + part.shape[1]])
        at += part.shape[1]
    grad_qkv, grad_out, grad_enc, grad_map, grad_noise = cuts
    return (grad_noise[:, :noise].T, grad_enc.T, grad_qkv, grad_out.T, grad_map)


def solution(mesh):
    member, grid = mesh.shape["member"], mesh.shape["grid"]
    inner = 4 if member == 16 else 2
    fine = Mesh(
        mesh.devices.reshape(member // inner, inner, 2, grid // 4, 2), MEMBER + GRID
    )
    in_specs = (
        P(MEMBER, GRID, None),
        P(),
        P(MEMBER, GRID, None),
        P(),
        P(),
        P(GRID, None),
        P(GRID, None),
        P(),
        P(GRID),
        P(),
        P(),
        P(GRID, None),
        P(GRID, None),
    )
    both = MEMBER + GRID
    out_specs = (P(None, both), P(None, both), P(both, None), P(None, both), P(both, None))
    return jax.shard_map(
        per_device, mesh=fine, in_specs=in_specs, out_specs=out_specs, check_vma=False
    )
```

profile of v0, /device:TPU:32, one launch (start us, length us, event | category | flops | bytes accessed | tf_op | source)
XLA Modules:
  0.0 240.0 jit_solution(7884230046379174082)
XLA Ops:
  0.6 8.8 %all-to-all-start = ((bf16[16,16,256]{2,1,0:T(8,128)(2,1)}), bf16[16,16,256]{2,1,0:T(8,128)(2,1)S(1)}, u32[]{:S(2)}, u32[]{:S(2)}) async-start(bf16[16,16,256]{2,1,0:T(8,128)(2,1)} %bitcast.221), calls=%async_computation | async-start | bytes 262144 | tf_op jit(solution)/shard_map/all_to_all | solution.py:61
  17.6 8.5 %all-to-all-start.1 = ((bf16[16,40,128]{2,1,0:T(8,128)(2,1)}), bf16[16,40,128]{2,1,0:T(8,128)(2,1)S(1)}, u32[]{:S(2)}, u32[]{:S(2)}) async-start(bf16[16,40,128]{2,1,0:T(8,128)(2,1)} %broadcast_in_dim.133), calls=%async_computation.1 | async-start | bytes 327680 | tf_op jit(solution)/shard_map/all_to_all | solution.py:61
  26.2 12.6 %all-to-all-done.1 = bf16[16,40,128]{2,1,0:T(8,128)(2,1)S(1)} async-done(((bf16[16,40,128]{2,1,0:T(8,128)(2,1)}), bf16[16,40,128]{2,1,0:T(8,128)(2,1)S(1)}, u32[]{:S(2)}, u32[]{:S(2)}) %all-to-all-start.1) | async-done | bytes 163872 | tf_op jit(solution)/shard_map/all_to_all | solution.py:61
  39.7 5.8 %all-to-all-start.2 = ((bf16[16,88,128]{2,1,0:T(8,128)(2,1)}), bf16[16,88,128]{2,1,0:T(8,128)(2,1)S(1)}, u32[]{:S(2)}, u32[]{:S(2)}) async-start(bf16[16,88,128]{2,1,0:T(8,128)(2,1)} %broadcast_in_dim.134), calls=%async_computation.2 | async-start | bytes 720896 | tf_op jit(solution)/shard_map/all_to_all | solution.py:61
  46.3 1.7 reshape.383
  50.0 6.9 %all-to-all-done.2 = bf16[16,88,128]{2,1,0:T(8,128)(2,1)S(1)} async-done(((bf16[16,88,128]{2,1,0:T(8,128)(2,1)}), bf16[16,88,128]{2,1,0:T(8,128)(2,1)S(1)}, u32[]{:S(2)}, u32[]{:S(2)}) %all-to-all-start.2) | async-done | bytes 360480 | tf_op jit(solution)/shard_map/all_to_all | solution.py:61
  60.8 3.2 %multiply_convert_fusion = (bf16[1024,1024]{1,0:T(8,128)(2,1)S(1)}, f32[1024,1024]{1,0:T(8,128)}) fusion(bf16[1024,128]{1,0:T(8,128)(2,1)S(1)} %constant_dynamic-update-slice_fusion.7, bf16[128,1024]{1,0:T(8,128)(2,1)S(1)} %copy-done.54), kind=kOutput, calls=%fused_computation.9 | convolution fusion | flops 273678336 | bytes 6815744 | tf_op jit(solution)/shard_map/dot_general | solution.py:41
  64.1 2.2 select_add_fusion.1
  70.8 1.9 fusion.144
  72.9 1.2 copy-done.1
  76.7 1.2 slice_reduce_fusion.5
  81.2 2.5 %fusion.9 = (f32[8,256]{1,0:T(8,128)S(1)}, f32[8,256,384]{2,1,0:T(8,128)S(1)}) fusion(f32[256,384]{1,0:T(8,128)S(1)} %fusion.73, f32[384,3,8,64]{0,3,2,1:T(8,128)} %bitcast.194, f32[384,8]{0,1:T(8,128)S(1)} %add_rsqrt_fusion, f32[256,8]{0,1:T(8,128)S(1)} %add_rsqrt_fusion.1), kind=kOutput, calls=%fused_computation.19 | convolution fusion | flops 103675904 | bytes 4878336 | tf_op jit(solution)/shard_map/qhd,khd->hqk/dot_general | solution.py:209
  84.3 2.4 convolution_convert_fusion.2
  91.3 5.1 %all-to-all-start.3 = ((f32[16,16,128]{2,1,0:T(8,128)}), f32[16,16,128]{2,1,0:T(8,128)S(1)}, u32[]{:S(2)}, u32[]{:S(2)}) async-start(f32[16,16,128]{2,1,0:T(8,128)} %bitcast.216), calls=%async_computation.3 | async-start | bytes 262144 | tf_op jit(solution)/shard_map/all_to_all | solution.py:61
  96.4 1.4 multiply_bitcast_fusion
  97.8 2.6 %fusion.46 = bf16[128,1024]{1,0:T(8,128)(2,1)} fusion(s32[1024]{0:T(1024)} %reshape.383, bf16[256,1024]{1,0:T(8,128)(2,1)} %copy-done.13), kind=kOutput, calls=%fused_computation.63 | convolution fusion | flops 269615104 | bytes 528384 | tf_op jit(solution)/shard_map/dot_general | solution.py:41
  100.4 3.0 %all-to-all-done.3 = f32[16,16,128]{2,1,0:T(8,128)S(1)} async-done(((f32[16,16,128]{2,1,0:T(8,128)}), f32[16,16,128]{2,1,0:T(8,128)S(1)}, u32[]{:S(2)}, u32[]{:S(2)}) %all-to-all-start.3) | async-done | bytes 131104 | tf_op jit(solution)/shard_map/all_to_all | solution.py:61
  103.8 1.4 multiply_convert_fusion.5
  105.1 5.4 %all-to-all-start.4 = ((bf16[16,16,128]{2,1,0:T(8,128)(2,1)}), bf16[16,16,128]{2,1,0:T(8,128)(2,1)S(1)}, u32[]{:S(2)}, u32[]{:S(2)}) async-start(bf16[16,16,128]{2,1,0:T(8,128)(2,1)} %multiply_convert_fusion.5), calls=%async_computation.4 | async-start | bytes 131072 | tf_op jit(solution)/shard_map/all_to_all | solution.py:61
  110.5 1.3 fusion.129
  111.8 5.4 %all-to-all-done.4 = bf16[16,16,128]{2,1,0:T(8,128)(2,1)S(1)} async-done(((bf16[16,16,128]{2,1,0:T(8,128)(2,1)}), bf16[16,16,128]{2,1,0:T(8,128)(2,1)S(1)}, u32[]{:S(2)}, u32[]{:S(2)}) %all-to-all-start.4) | async-done | bytes 65568 | tf_op jit(solution)/shard_map/all_to_all | solution.py:61
  117.7 1.2 fusion.128
  118.9 1.2 slice.420
  120.2 1.2 slice.422
  121.3 1.7 slice.498
  123.0 4.6 %collective-permute-done = bf16[256,128]{1,0:T(8,128)(2,1)S(1)} collective-permute-done((bf16[256,128]{1,0:T(8,128)(2,1)S(1)}, bf16[256,128]{1,0:T(8,128)(2,1)S(1)}, u32[]{:S(2)}, u32[]{:S(2)}) %collective-permute-start) | collective-permute-done | bytes 65568 | tf_op jit(solution)/shard_map/ppermute | solution.py:66
  127.6 2.2 fusion.96
  130.9 1.3 fusion.140
  133.0 1.2 convolution_convert_fusion.4
  135.3 1.9 fusion.49
  137.2 4.6 %fusion.8 = bf16[8,256,384]{2,1,0:T(8,128)(2,1)} fusion(bf16[8,256,384]{2,1,0:T(8,128)(2,1)} %copy-done.2, bf16[256,8,64]{0,2,1:T(8,128)(2,1)S(1)} %bitcast.208, f32[384,3,8,64]{0,3,2,1:T(8,128)} %bitcast.196), kind=kOutput, calls=%fused_computation.14 | convolution fusion | flops 206047616 | bytes 6029312 | tf_op jit(solution)/shard_map/sub | solution.py:268
  141.8 1.6 convolution_bitcast_fusion
  143.4 2.0 multiply_reduce_fusion.9
  146.8 3.0 %multiply_reduce_fusion.6 = (f32[128]{0:T(128)S(1)}, f32[128,1024]{1,0:T(8,128)}) fusion(f32[384,1024]{1,0:T(8,128)} %copy-done.5, bf16[128,1536]{0,1:T(8,128)(2,1)S(1)} %bitcast.211, bf16[1024,1536]{1,0:T(8,128)(2,1)S(1)} %copy-done), kind=kOutput, calls=%fused_computation.118 | convolution fusion | flops 402915200 | bytes 4588032 | tf_op jit(solution)/shard_map/dot_general | solution.py:41
  149.8 4.5 %fusion.7 = bf16[1024,2432]{1,0:T(8,128)(2,1)} fusion(bf16[128,1536]{0,1:T(8,128)(2,1)S(1)} %bitcast.212, s32[1024]{0:T(1024)S(1)} %copy-done.47, bf16[384,1024]{1,0:T(8,128)(2,1)} %copy-done.18), kind=kOutput, calls=%fused_computation.13 | convolution fusion | flops 673841152 | bytes 3805184 | tf_op jit(solution)/shard_map/dot_general | solution.py:41
  154.3 2.1 fusion.109
  156.4 1.9 multiply_reduce_fusion.5
  158.4 3.1 %fusion.64 = f32[512,1024]{1,0:T(8,128)S(1)} fusion(f32[128,1024]{1,0:T(8,128)S(1)} %copy-done.8, f32[128,1024]{1,0:T(8,128)S(1)} %get-tuple-element.32, f32[384,512]{1,0:T(8,128)} %get-tuple-element.51, f32[128]{0:T(128)S(1)} %broadcast_multiply_fusion.3, f32[128]{0:T(128)S(1)} %copy-done.52, f32[128]{0:T(128)S(1)} %copy-done.53), kind=kOutput, calls=%fused_computation.112 | convolution fusion | flops 805830656 | bytes 3409408 | tf_op jit(solution)/shard_map/dot_general | solution.py:41
  161.5 2.3 fusion.35
  163.8 3.3 %fusion.32 = bf16[1024,2432]{1,0:T(8,128)(2,1)} fusion(bf16[1024,2432]{1,0:T(8,128)(2,1)} %fusion.7, bf16[128,512]{0,1:T(8,128)(2,1)} %bitcast.222, s32[1024]{0:T(1024)S(1)} %copy-done.47, bf16[256,1024]{1,0:T(8,128)(2,1)} %copy-done.14), kind=kOutput, calls=%fused_computation.48 | convolution fusion | flops 404357120 | bytes 1445888 | tf_op jit(solution)/shard_map/dot_general | solution.py:41
  167.1 2.8 %fusion.41 = bf16[1024,2432]{1,0:T(8,128)(2,1)} fusion(bf16[1024,2432]{1,0:T(8,128)(2,1)} %fusion.32, bf16[128,1024]{1,0:T(8,128)(2,1)} %fusion.35, s32[1024]{0:T(1024)S(1)} %copy-done.47), kind=kOutput, calls=%fused_computation.60 | convolution fusion | flops 270663680 | bytes 528384 | tf_op jit(solution)/shard_map/dot_general | solution.py:41
  171.0 2.9 %fusion.48 = bf16[1024,2432]{1,0:T(8,128)(2,1)} fusion(bf16[1024,2432]{1,0:T(8,128)(2,1)} %fusion.34, s32[1024]{0:T(1024)S(1)} %copy-done.47, f32[128,1024]{1,0:T(8,128)} %copy-done.15, bf16[128,16]{0,1:T(8,128)(2,1)S(1)} %bitcast.228), kind=kOutput, calls=%fused_computation.66 | convolution fusion | flops 303431680 | bytes 794624 | tf_op jit(solution)/shard_map/dot_general | solution.py:41
  173.9 3.4 %dynamic-slice_bitcast_fusion = bf16[512,2432]{1,0:T(8,128)(2,1)} fusion(bf16[2,512,2432]{2,1,0:T(8,128)(2,1)} %bitcast.205, s32[]{:T(128)S(6)} %select_n.147), kind=kLoop, calls=%fused_computation.20 | loop fusion | bytes 4980740 | tf_op jit(solution)/shard_map/jit(dynamic_index_in_dim)/squeeze | solution.py:309
  177.3 5.1 %collective-permute-done.2 = bf16[512,2432]{1,0:T(8,128)(2,1)} collective-permute-done((bf16[512,2432]{1,0:T(8,128)(2,1)}, bf16[512,2432]{1,0:T(8,128)(2,1)}, u32[]{:S(2)}, u32[]{:S(2)}) %collective-permute-start.2) | collective-permute-done | bytes 2490400 | tf_op jit(solution)/shard_map/ppermute | solution.py:310
  182.3 3.0 %fusion.1 = bf16[512,2432]{1,0:T(8,128)(2,1)S(1)} fusion(bf16[512,2432]{1,0:T(8,128)(2,1)} %collective-permute-done.2, bf16[2,512,2432]{2,1,0:T(8,128)(2,1)} %bitcast.206, s32[]{:T(128)S(6)} %select_n.146), kind=kLoop, calls=%fused_computation.2 | loop fusion | flops 4980736 | bytes 7471108 | tf_op jit(solution)/shard_map/convert_element_type | solution.py:311
  185.4 36.2 %all_to_all.35 = bf16[16,32,2432]{2,1,0:T(8,128)(2,1)} all-to-all(bf16[16,32,2432]{2,1,0:T(8,128)(2,1)S(1)} %bitcast.204), channel_id=1, replica_groups=mesh['zl'=4,'x'=4,'zh'=2,'y'=4,'core'=2] {'x','y'}, dimensions={0} | all-to-all | bytes 4980736 | tf_op jit(solution)/shard_map/all_to_all | solution.py:61
  221.5 2.1 reduce_sum.151
  223.7 13.9 %all_to_all.36 = bf16[8,4,2432]{2,1,0:T(4,128)(2,1)S(1)} all-to-all(bf16[8,4,2432]{2,1,0:T(4,128)(2,1)S(1)} %reshape.373), channel_id=1, replica_groups=mesh['zl'=4,'x'=4,'zh'=2,'y'=4,'core'=2] {'zl','zh'}, dimensions={0} | all-to-all | bytes 311296 | tf_op jit(solution)/shard_map/all_to_all | solution.py:61
  (214 shorter events, 39.4 us)
Async XLA Ops:
  0.6 70.2 %copy-start = (bf16[1024,1536]{1,0:T(8,128)(2,1)S(1)}, bf16[1024,1536]{1,0:T(8,128)(2,1)}, u32[]{:S(2)}) copy-start(bf16[1024,1536]{1,0:T(8,128)(2,1)} %param.20) | copy-start | bytes 9437188
  0.6 15.7 %all-to-all-start = ((bf16[16,16,256]{2,1,0:T(8,128)(2,1)}), bf16[16,16,256]{2,1,0:T(8,128)(2,1)S(1)}, u32[]{:S(2)}, u32[]{:S(2)}) async-start(bf16[16,16,256]{2,1,0:T(8,128)(2,1)} %bitcast.221), calls=%async_computation | async-start | bytes 262144 | tf_op jit(solution)/shard_map/all_to_all | solution.py:61
  17.6 21.2 %all-to-all-start.1 = ((bf16[16,40,128]{2,1,0:T(8,128)(2,1)}), bf16[16,40,128]{2,1,0:T(8,128)(2,1)S(1)}, u32[]{:S(2)}, u32[]{:S(2)}) async-start(bf16[16,40,128]{2,1,0:T(8,128)(2,1)} %broadcast_in_dim.133), calls=%async_computation.1 | async-start | bytes 327680 | tf_op jit(solution)/shard_map/all_to_all | solution.py:61
  39.7 17.2 %all-to-all-start.2 = ((bf16[16,88,128]{2,1,0:T(8,128)(2,1)}), bf16[16,88,128]{2,1,0:T(8,128)(2,1)S(1)}, u32[]{:S(2)}, u32[]{:S(2)}) async-start(bf16[16,88,128]{2,1,0:T(8,128)(2,1)} %broadcast_in_dim.134), calls=%async_computation.2 | async-start | bytes 720896 | tf_op jit(solution)/shard_map/all_to_all | solution.py:61
  58.3 2.6 %copy-start.54 = (bf16[128,1024]{1,0:T(8,128)(2,1)S(1)}, bf16[128,1024]{1,0:T(8,128)(2,1)}, u32[]{:S(2)}) copy-start(bf16[128,1024]{1,0:T(8,128)(2,1)} %param.17) | copy-start | bytes 786436
  67.9 1.5 copy-start.7
  70.8 1.9 copy-start.18
  79.6 10.0 %copy-start.36 = (f32[768]{0:T(1024)}, f32[768]{0:T(1024)S(1)}, u32[]{:S(2)}) copy-start(f32[768]{0:T(1024)S(1)} %get-tuple-element.10) | copy-start | bytes 9220
  79.6 10.0 %copy-start.37 = (f32[768]{0:T(1024)}, f32[768]{0:T(1024)S(1)}, u32[]{:S(2)}) copy-start(f32[768]{0:T(1024)S(1)} %get-tuple-element.11) | copy-start | bytes 9220
  79.6 10.0 %copy-start.38 = (f32[768]{0:T(1024)}, f32[768]{0:T(1024)S(1)}, u32[]{:S(2)}) copy-start(f32[768]{0:T(1024)S(1)} %get-tuple-element.12) | copy-start | bytes 9220
  79.6 4.0 %copy-start.31 = (f32[256,8]{0,1:T(8,128)}, f32[256,8]{0,1:T(8,128)S(1)}, u32[]{:S(2)}) copy-start(f32[256,8]{0,1:T(8,128)S(1)} %add_rsqrt_fusion.1) | copy-start | bytes 24580
  84.3 3.1 %copy-start.2 = (bf16[8,256,384]{2,1,0:T(8,128)(2,1)}, bf16[8,256,384]{2,1,0:T(8,128)(2,1)S(1)}, u32[]{:S(2)}) copy-start(bf16[8,256,384]{2,1,0:T(8,128)(2,1)S(1)} %divide_convert_fusion) | copy-start | bytes 4718596
  84.3 2.4 copy-start.6
  84.3 2.5 %copy-start.9 = (bf16[512,1024]{1,0:T(8,128)(2,1)S(1)}, bf16[512,1024]{1,0:T(8,128)(2,1)}, u32[]{:S(2)}) copy-start(bf16[512,1024]{1,0:T(8,128)(2,1)} %param.22) | copy-start | bytes 3145732
  86.7 1.8 copy-start.16
  86.8 2.5 %copy-start.11 = (bf16[1024,128]{1,0:T(8,128)(2,1)S(1)}, bf16[1024,128]{1,0:T(8,128)(2,1)}, u32[]{:S(2)}) copy-start(bf16[1024,128]{1,0:T(8,128)(2,1)} %param.23) | copy-start | bytes 786436
  86.8 2.8 %copy-start.34 = (s32[768]{0:T(1024)S(1)}, s32[768]{0:T(1024)}, u32[]{:S(2)}) copy-start(s32[768]{0:T(1024)} %get-tuple-element.8) | copy-start | bytes 9220
  86.8 2.8 %copy-start.35 = (s32[768]{0:T(1024)S(1)}, s32[768]{0:T(1024)}, u32[]{:S(2)}) copy-start(s32[768]{0:T(1024)} %get-tuple-element.9) | copy-start | bytes 9220
  87.4 2.9 %copy-start.20 = (bf16[16,16,128]{2,1,0:T(8,128)(2,1)S(1)}, bf16[16,16,128]{2,1,0:T(8,128)(2,1)}, u32[]{:S(2)}) copy-start(bf16[16,16,128]{2,1,0:T(8,128)(2,1)} %copy-done.19) | copy-start | bytes 196612
  87.9 3.4 %copy-start.43 = (f32[256]{0:T(256)}, f32[256]{0:T(256)S(1)}, u32[]{:S(2)}) copy-start(f32[256]{0:T(256)S(1)} %get-tuple-element.67) | copy-start | bytes 3076
  91.3 12.0 %all-to-all-start.3 = ((f32[16,16,128]{2,1,0:T(8,128)}), f32[16,16,128]{2,1,0:T(8,128)S(1)}, u32[]{:S(2)}, u32[]{:S(2)}) async-start(f32[16,16,128]{2,1,0:T(8,128)} %bitcast.216), calls=%async_computation.3 | async-start | bytes 262144 | tf_op jit(solution)/shard_map/all_to_all | solution.py:61
  105.1 12.1 %all-to-all-start.4 = ((bf16[16,16,128]{2,1,0:T(8,128)(2,1)}), bf16[16,16,128]{2,1,0:T(8,128)(2,1)S(1)}, u32[]{:S(2)}, u32[]{:S(2)}) async-start(bf16[16,16,128]{2,1,0:T(8,128)(2,1)} %multiply_convert_fusion.5), calls=%async_computation.4 | async-start | bytes 131072 | tf_op jit(solution)/shard_map/all_to_all | solution.py:61
  117.2 13.2 %copy-start.4 = (f32[256,1024]{1,0:T(8,128)S(1)}, f32[256,1024]{1,0:T(8,128)}, u32[]{:S(2)}) copy-start(f32[256,1024]{1,0:T(8,128)} %copy-done.3) | copy-start | bytes 3145732
  117.2 5.8 %collective-permute-start.1 = (bf16[256,128]{1,0:T(8,128)(2,1)S(1)}, bf16[256,128]{1,0:T(8,128)(2,1)S(1)}, u32[]{:S(2)}, u32[]{:S(2)}) collective-permute-start(bf16[256,128]{1,0:T(8,128)(2,1)S(1)} %bitcast.225), channel_id=1, source_target_pairs={{0,15},{1,0},{2,1},{3,2},{4,3},{5,4},{6,5},{7,6},{8,7},{9,8},{10,9... | collective-permute-start | bytes 196616 | tf_op jit(solution)/shard_map/ppermute | solution.py:66
  117.2 10.4 %collective-permute-start = (bf16[256,128]{1,0:T(8,128)(2,1)S(1)}, bf16[256,128]{1,0:T(8,128)(2,1)S(1)}, u32[]{:S(2)}, u32[]{:S(2)}) collective-permute-start(bf16[256,128]{1,0:T(8,128)(2,1)S(1)} %bitcast.226), channel_id=1, source_target_pairs={{0,1},{1,2},{2,3},{3,4},{4,5},{5,6},{6,7},{7,8},{8,9},{9,10},{10,1... | collective-permute-start | bytes 196616 | tf_op jit(solution)/shard_map/ppermute | solution.py:66
  130.8 2.1 copy-start.10
  137.2 4.6 %copy-start.32 = (f32[256,8]{0,1:T(8,128)S(1)}, f32[256,8]{0,1:T(8,128)}, u32[]{:S(2)}) copy-start(f32[256,8]{0,1:T(8,128)} %copy-done.31) | copy-start | bytes 24580
  141.8 3.7 %copy-start.39 = (f32[128,8]{0,1:T(8,128)S(1)}, f32[128,8]{0,1:T(8,128)}, u32[]{:S(2)}) copy-start(f32[128,8]{0,1:T(8,128)} %get-tuple-element.54) | copy-start | bytes 12292
  141.8 3.7 %copy-start.40 = (f32[128,8]{0,1:T(8,128)S(1)}, f32[128,8]{0,1:T(8,128)}, u32[]{:S(2)}) copy-start(f32[128,8]{0,1:T(8,128)} %get-tuple-element.55) | copy-start | bytes 12292
  141.8 3.7 %copy-start.41 = (f32[128,8]{0,1:T(8,128)S(1)}, f32[128,8]{0,1:T(8,128)}, u32[]{:S(2)}) copy-start(f32[128,8]{0,1:T(8,128)} %get-tuple-element.83) | copy-start | bytes 12292
  141.8 3.7 %copy-start.42 = (f32[128,8]{0,1:T(8,128)S(1)}, f32[128,8]{0,1:T(8,128)}, u32[]{:S(2)}) copy-start(f32[128,8]{0,1:T(8,128)} %get-tuple-element.84) | copy-start | bytes 12292
  141.8 4.9 %copy-start.22 = (bf16[128,1,8,64]{0,3,2,1:T(8,128)(2,1)S(1)}, bf16[128,1,8,64]{0,3,2,1:T(8,128)(2,1)}, u32[]{:S(2)}) copy-start(bf16[128,1,8,64]{0,3,2,1:T(8,128)(2,1)} %fusion.49) | copy-start | bytes 393220
  146.7 3.0 %copy-start.47 = (s32[1024]{0:T(1024)S(1)}, s32[1024]{0:T(1024)}, u32[]{:S(2)}) copy-start(s32[1024]{0:T(1024)} %reshape.383) | copy-start | bytes 12292
  149.7 6.6 %copy-start.50 = (f32[128]{0:T(128)S(1)}, f32[128]{0:T(128)}, u32[]{:S(2)}) copy-start(f32[128]{0:T(128)} %fusion.128) | copy-start | bytes 1540
  149.7 6.6 %copy-start.51 = (f32[128]{0:T(128)S(1)}, f32[128]{0:T(128)}, u32[]{:S(2)}) copy-start(f32[128]{0:T(128)} %slice.422) | copy-start | bytes 1540
  154.3 4.1 %copy-start.8 = (f32[128,1024]{1,0:T(8,128)S(1)}, f32[128,1024]{1,0:T(8,128)}, u32[]{:S(2)}) copy-start(f32[128,1024]{1,0:T(8,128)} %copy-done.7) | copy-start | bytes 1572868
  154.3 4.1 %copy-start.52 = (f32[128]{0:T(128)S(1)}, f32[128]{0:T(128)}, u32[]{:S(2)}) copy-start(f32[128]{0:T(128)} %fusion.129) | copy-start | bytes 1540
  154.3 4.1 %copy-start.53 = (f32[128]{0:T(128)S(1)}, f32[128]{0:T(128)}, u32[]{:S(2)}) copy-start(f32[128]{0:T(128)} %slice.420) | copy-start | bytes 1540
  156.4 5.1 %copy-start.56 = (f32[1024,1024]{1,0:T(8,128)S(1)}, f32[1024,1024]{1,0:T(8,128)}, u32[]{:S(2)}) copy-start(f32[1024,1024]{1,0:T(8,128)} %get-tuple-element.69) | copy-start | bytes 12582916
  158.3 3.2 %copy-start.15 = (f32[128,1024]{1,0:T(8,128)}, f32[128,1024]{1,0:T(8,128)S(1)}, u32[]{:S(2)}) copy-start(f32[128,1024]{1,0:T(8,128)S(1)} %get-tuple-element.32) | copy-start | bytes 1572868
  158.3 3.2 %copy-start.21 = (bf16[16,16,128]{2,1,0:T(8,128)(2,1)S(1)}, bf16[16,16,128]{2,1,0:T(8,128)(2,1)}, u32[]{:S(2)}) copy-start(bf16[16,16,128]{2,1,0:T(8,128)(2,1)} %copy-done.19) | copy-start | bytes 196612
  158.3 3.2 %copy-start.24 = (bf16[16,16,128]{2,1,0:T(8,128)(2,1)S(1)}, bf16[16,16,128]{2,1,0:T(8,128)(2,1)}, u32[]{:S(2)}) copy-start(bf16[16,16,128]{2,1,0:T(8,128)(2,1)} %copy-done.23) | copy-start | bytes 196612
  158.3 3.2 %copy-start.26 = (bf16[16,16,128]{2,1,0:T(8,128)(2,1)S(1)}, bf16[16,16,128]{2,1,0:T(8,128)(2,1)}, u32[]{:S(2)}) copy-start(bf16[16,16,128]{2,1,0:T(8,128)(2,1)} %copy-done.25) | copy-start | bytes 196612
  163.8 6.1 %copy-start.17 = (bf16[128,1024]{1,0:T(8,128)(2,1)S(1)}, bf16[128,1024]{1,0:T(8,128)(2,1)}, u32[]{:S(2)}) copy-start(bf16[128,1024]{1,0:T(8,128)(2,1)} %fusion.46) | copy-start | bytes 786436
  163.8 6.1 %copy-start.29 = (bf16[256,128]{1,0:T(8,128)(2,1)S(1)}, bf16[256,128]{1,0:T(8,128)(2,1)}, u32[]{:S(2)}) copy-start(bf16[256,128]{1,0:T(8,128)(2,1)} %copy-done.28) | copy-start | bytes 196612
  167.1 2.8 %copy-start.12 = (f32[1024,128]{1,0:T(8,128)S(1)}, f32[1024,128]{1,0:T(8,128)}, u32[]{:S(2)}) copy-start(f32[1024,128]{1,0:T(8,128)} %fusion.109) | copy-start | bytes 1572868
  167.1 3.8 %copy-start.46 = (bf16[1,128,16]{1,2,0:T(8,128)(2,1)S(1)}, bf16[1,128,16]{1,2,0:T(8,128)(2,1)}, u32[]{:S(2)}) copy-start(bf16[1,128,16]{1,2,0:T(8,128)(2,1)} %param.15) | copy-start | bytes 12292
  177.3 5.1 %collective-permute-start.2 = (bf16[512,2432]{1,0:T(8,128)(2,1)}, bf16[512,2432]{1,0:T(8,128)(2,1)}, u32[]{:S(2)}, u32[]{:S(2)}) collective-permute-start(bf16[512,2432]{1,0:T(8,128)(2,1)} %dynamic-slice_bitcast_fusion), channel_id=1, source_target_pairs={{0,1},{1,0},{2,3},{3,2},{4,5},{5,4},{6,7},{7,6},{8,9},{9,8},{10,11... | collective-permute-start | bytes 7471112 | tf_op jit(solution)/shard_map/ppermute | solution.py:310
  (17 other events, 15.4 us)
where the time goes:
time: 242 us; the launch traced here: 240 us
  matrix products  55.8 us (23%)
  blocking collectives  50.1 us (21%)
  waiting for transfers between devices  38.2 us (16%)
  starting transfers between devices  34.1 us (14%)
  local copies, waits for them, and re-layouts  30.2 us (12%)
  other arithmetic  29.3 us (12%)
    all_to_all x2, blocking collectives, swap(): return lax.all_to_all(values, axes, split_axis=0, concat_axis=0, tiled=True)  50.1 us
    dot_general x26, matrix products, dot(): lax.dot_general(left, right, (dims, ((), ())), preferred_element_type=F32...  40.9 us
    all_to_all x5, starting transfers between devices, swap(): return lax.all_to_all(values, axes, split_axis=0, concat_axis=0, tiled=True)  33.6 us
    all_to_all x5, waiting for transfers between devices, swap(): return lax.all_to_all(values, axes, split_axis=0, concat_axis=0, tiled=True)  28.6 us
    unnamed x125, local copies, waits for them, and re-layouts  7.82 us
    ppermute x1, waiting for transfers between devices, per_device(): lax.ppermute(sent, 'core', [(0, 1), (1, 0)]).astype(F32)  5.06 us
  transfers between devices with their start and end apart: 8, of which 7 were waited for; matrix products, arithmetic and copies ran while one was open for 9% of the time, Pallas kernels for 0%

commit v1 on v0

v1 whole, which is shorter than its diff:
```python
import functools

import jax
import jax.numpy as jnp
from jax import lax
from jax.experimental import pallas as pl
from jax.experimental.pallas import tpu as pltpu
from jax.sharding import Mesh
from jax.sharding import PartitionSpec as P

HEAD_DIM = 64
RIM_G = 128
RIM_H = 64
WIN = 64

EPS = 1e-06
DELTA_SQ = 0.01

MEMBER = ("zl", "x")
GRID = ("zh", "y", "core")
F32 = jnp.float32
BF16 = jnp.bfloat16
INTERPRET = False
NODES = 128
POINTS = 256
ASKED = NODES + 2 * WIN


def rms_factor(values):
    return lax.rsqrt(jnp.mean(values * values, axis=-1, keepdims=True) + EPS)


def rms_back(values, factor, gradient):
    inner = jnp.mean(gradient * values, axis=-1, keepdims=True)
    return factor * gradient - values * (factor * factor * factor) * inner


def silu_slope(pre):
    sigma = jax.nn.sigmoid(pre)
    return sigma * (1.0 + pre * (1.0 - sigma))


def eased_sensitivity(diff):
    return diff * lax.rsqrt(diff * diff + DELTA_SQ)


def dot(left, right, dims, **options):
    return lax.dot_general(left, right, (dims, ((), ())), preferred_element_type=F32, **options)


NN = ((1,), (0,))
TN = ((0,), (0,))
NT = ((1,), (1,))


def two_terms(values):
    high = lax.reduce_precision(values, 8, 7)
    return high.astype(BF16), (values - high).astype(BF16)


def three_terms(values):
    high = lax.reduce_precision(values, 8, 7)
    middle = lax.reduce_precision(values - high, 8, 7)
    return [high.astype(BF16), middle.astype(BF16), (values - high - middle).astype(BF16)]


def swap(values, axes):
    return lax.all_to_all(values, axes, split_axis=0, concat_axis=0, tiled=True)


def shifted(values, step):
    count = lax.axis_size(GRID)
    return lax.ppermute(values, GRID, [(i, (i + step) % count) for i in range(count)])


def split2(values):
    high = values.astype(BF16)
    return high, (values - high.astype(F32)).astype(BF16)


def same_head(attn):
    row = lax.broadcasted_iota(jnp.int32, (attn, attn), 0) // HEAD_DIM
    column = lax.broadcasted_iota(jnp.int32, (attn, attn), 1) // HEAD_DIM
    return jnp.where(row == column, 1.0, 0.0).astype(BF16)


def head_mean(values, heads):
    high, low = split2(values)
    return (dot(high, heads, NN) + dot(low, heads, NN)) * (1.0 / HEAD_DIM)


def head_masks():
    lane = lax.broadcasted_iota(jnp.int32, (1, 2 * HEAD_DIM), 1)
    return (lane < HEAD_DIM, lane >= HEAD_DIM)


def masked(mask, values):
    return jnp.where(mask, values, jnp.zeros_like(values))


def spread_matrix(facts, k_enc, reach):
    span = lax.broadcasted_iota(jnp.int32, (NODES, reach), 1)
    home = lax.broadcasted_iota(jnp.int32, (NODES, 1), 0) * (POINTS // NODES) + RIM_G
    spread = jnp.zeros((NODES, reach), F32)
    for k in range(k_enc):
        source = facts[:, k : k + 1].astype(jnp.int32) + home
        spread = spread + jnp.where(source == span, facts[:, k_enc + k : k_enc + k + 1], 0.0)
    return split2(spread)


def interleave(parity, shape, point_dim):
    point = lax.broadcasted_iota(jnp.int32, shape, point_dim)
    node = lax.broadcasted_iota(jnp.int32, shape, 1 - point_dim)
    return jnp.where(point == 2 * node + parity, 1.0, 0.0).astype(BF16)


def forward_kernel(k_enc, k_dec, *refs):
    x_ref, facts_ref, jitter_ref, wn_ref, we_ref, wq_ref, wo_ref, u_ref = refs[:8]
    (forecast_ref, pooled_ref, state0_ref, normed_ref, raw_ref, qn_ref, kn_ref, v_ref) = refs[8:16]
    prob_ref, att_ref, state1_ref, dnorm_ref, msg_ref, all0_ref, proj_ref = refs[16:]
    attn = wo_ref.shape[0]
    reach = POINTS + 2 * RIM_G
    inv_root = HEAD_DIM ** (-0.5)

    def message_rows(i, carry):
        rows = pl.ds(pl.multiple_of(i * 128, 128), 128)
        pre = dot(x_ref[rows, :], we_ref[...], NN)
        msg_ref[rows, :] = (pre * jax.nn.sigmoid(pre)).astype(BF16)
        return carry

    lax.fori_loop(0, x_ref.shape[0] // 128, message_rows, 0)
    heads = same_head(attn)
    for s in range(3):
        rows = slice(s * NODES, (s + 1) * NODES)
        high, low = spread_matrix(facts_ref[rows, :], k_enc, reach)
        near = msg_ref[s * POINTS : s * POINTS + reach, :]
        pooled = dot(high, near, NN) + dot(low, near, NN)
        state0 = pooled * rms_factor(pooled) + dot(jitter_ref[rows, :], wn_ref[...], NN)
        all0_ref[rows, :] = state0
        normed = (state0 * rms_factor(state0)).astype(BF16)
        mixed = dot(normed, wq_ref[...], NN)
        queries, keys = mixed[:, :attn], mixed[:, attn : 2 * attn]
        qn_ref[rows, :] = (
            queries * lax.rsqrt(head_mean(queries * queries, heads) + EPS)
        ).astype(BF16)
        kn_ref[rows, :] = (keys * lax.rsqrt(head_mean(keys * keys, heads) + EPS)).astype(BF16)
        v_ref[rows, :] = mixed[:, 2 * attn :].astype(BF16)
        if s == 1:
            pooled_ref[...] = pooled
            state0_ref[...] = state0
            normed_ref[...] = normed
            raw_ref[...] = mixed[:, : 2 * attn]

    masks = head_masks()
    span = 2 * NODES
    relative = (
        lax.broadcasted_iota(jnp.int32, (NODES, span), 1)
        - lax.broadcasted_iota(jnp.int32, (NODES, span), 0)
        - WIN
    )
    for b in range(2):
        asked = slice(WIN + b * NODES, WIN + (b + 1) * NODES)
        known = slice(b * NODES, b * NODES + span)
        rows = slice(b * NODES, (b + 1) * NODES)
        offsets = facts_ref[asked, 2 * k_enc : 2 * k_enc + 1].astype(jnp.int32)
        allowed = (relative >= offsets) & (relative < offsets + WIN)
        for pair in range(attn // 128):
            lanes = slice(pair * 128, (pair + 1) * 128)
            query, key, value = qn_ref[asked, lanes], kn_ref[known, lanes], v_ref[known, lanes]
            out = jnp.zeros((NODES, 128), F32)
            for h in range(2):
                scores = dot(masked(masks[h], query), key, NT) * inv_root
                weights = jnp.where(allowed, jnp.exp(scores), 0.0)
                prob = (weights / jnp.sum(weights, axis=-1, keepdims=True)).astype(BF16)
                prob_ref[(b * attn // 128 + pair) * 2 + h] = prob
                out = out + dot(prob, masked(masks[h], value), NN)
            att_ref[rows, lanes] = out.astype(BF16)
        state1 = all0_ref[asked, :] + dot(att_ref[rows, :], wo_ref[...], NN)
        state1_ref[rows, :] = state1
        dnorm = (state1 * rms_factor(state1)).astype(BF16)
        dnorm_ref[rows, :] = dnorm
        proj_ref[rows, :] = dot(dnorm, u_ref[...], NN)

    proj_high, proj_low = split2(proj_ref[...])
    facts = facts_ref[NODES : 2 * NODES, :]
    span = lax.broadcasted_iota(jnp.int32, (NODES, ASKED), 1)
    home = lax.broadcasted_iota(jnp.int32, (NODES, 1), 0) + RIM_H
    forecast = x_ref[POINTS + RIM_G : 2 * POINTS + RIM_G, :].astype(F32)
    for parity in range(2):
        arcs = jnp.zeros((NODES, ASKED), F32)
        for k in range(k_dec):
            at = 2 * k_enc + 1 + parity * k_dec + k
            source = facts[:, at : at + 1].astype(jnp.int32) + home
            scale = facts[:, at + 2 * k_dec : at + 2 * k_dec + 1]
            arcs = arcs + jnp.where(source == span, scale, 0.0)
        high, low = split2(arcs)
        rest = dot(high, proj_high, NN) + dot(high, proj_low, NN) + dot(low, proj_high, NN)
        place = interleave(parity, (POINTS, NODES), 0)
        high, low = split2(rest)
        forecast = forecast + dot(place, high, NN) + dot(place, low, NN)
    forecast_ref[...] = forecast


def backward_kernel(k_enc, k_dec, *refs):
    (low_ref, mid_ref, high_ref, facts_ref, turned_ref, x_ref, jitter_ref, wet_ref) = refs[:8]
    (wq_ref, wo_ref, u_ref, order_ref, pooled_ref, state0_ref, normed_ref, raw_ref) = refs[8:16]
    (qn_ref, kn_ref, v_ref, prob_ref, att_ref, state1_ref, dnorm_ref) = refs[16:23]
    kept_ref, sent_ref, grad1_ref, g1b_ref, ga_ref, gq_ref, gk_ref, gv_ref, mixed_ref = refs[23:]
    attn, width = wo_ref.shape
    reach = POINTS + 2 * RIM_G
    inv_root = HEAD_DIM ** (-0.5)
    own = slice(NODES, 2 * NODES)
    own_asked = slice(WIN, WIN + NODES)
    quarter = width // 4

    def store(r, start, values):
        ref = kept_ref if r < 2 else sent_ref
        at = (r % 2) * quarter
        ref[at : at + quarter, start : start + values.shape[1]] = values.astype(BF16)

    def turned(r, values):
        return dot(order_ref[r * quarter : (r + 1) * quarter, :], values, NT).astype(BF16)

    grad_proj = jnp.zeros((ASKED, low_ref.shape[1]), F32)
    span = lax.broadcasted_iota(jnp.int32, (ASKED, NODES), 0)
    node = lax.broadcasted_iota(jnp.int32, (1, NODES), 1)
    for s, ref in enumerate((low_ref, mid_ref, high_ref)):
        lanes = slice(s * NODES, (s + 1) * NODES)
        for parity in range(2):
            arcs = jnp.zeros((ASKED, NODES), F32)
            for k in range(k_dec):
                at = 2 * k_enc + 1 + parity * k_dec + k
                source = turned_ref[at : at + 1, lanes].astype(jnp.int32) + node
                source = source + (s * NODES - NODES + RIM_H)
                scale = turned_ref[at + 2 * k_dec : at + 2 * k_dec + 1, lanes]
                arcs = arcs + jnp.where(source == span, scale, 0.0)
            grad = dot(interleave(parity, (NODES, POINTS), 1), ref[...], NN).astype(BF16)
            high, low = split2(arcs)
            grad_proj = grad_proj + dot(high, grad, NN) + dot(low, grad, NN)
    proj_high, proj_low = split2(grad_proj)
    for b in range(2):
        rows = slice(b * NODES, (b + 1) * NODES)
        state1 = state1_ref[rows, :]
        grad = dot(proj_high[rows], u_ref[...], NT) + dot(proj_low[rows], u_ref[...], NT)
        grad = rms_back(state1, rms_factor(state1), grad)
        grad1_ref[rows, :] = grad
        g1b_ref[rows, :] = grad.astype(BF16)
        ga_ref[rows, :] = dot(g1b_ref[rows, :], wo_ref[...], NT).astype(BF16)
    for r in range(4):
        dnorm = turned(r, dnorm_ref[own_asked, :])
        store(
            r,
            4 * attn + 128,
            dot(dnorm, proj_high[own_asked], NN) + dot(dnorm, proj_low[own_asked], NN),
        )
        store(r, 3 * attn, dot(turned(r, g1b_ref[own_asked, :]), att_ref[own_asked, :], NN))

    masks = head_masks()
    for pair in range(attn // 128):
        lanes = slice(pair * 128, (pair + 1) * 128)
        grad_key = jnp.zeros((NODES, 128), F32)
        grad_value = jnp.zeros((NODES, 128), F32)
        for b in range(2):
            asked = slice(WIN + b * NODES, WIN + (b + 1) * NODES)
            known = slice(b * NODES, b * NODES + 2 * NODES)
            mine = slice(NODES, 2 * NODES) if b == 0 else slice(0, NODES)
            half = slice(WIN, NODES) if b == 0 else slice(0, WIN)
            query, key, value = qn_ref[asked, lanes], kn_ref[known, lanes], v_ref[known, lanes]
            grad_out = ga_ref[b * NODES : (b + 1) * NODES, lanes]
            grad_query = jnp.zeros((WIN, 128), F32)
            for h in range(2):
                grad_head = masked(masks[h], grad_out)
                grad_prob = dot(grad_head, value, NT)
                prob = prob_ref[(b * attn // 128 + pair) * 2 + h]
                wide = prob.astype(F32)
                inner = jnp.sum(wide * grad_prob, axis=-1, keepdims=True)
                grad_scores = (wide * (grad_prob - inner)).astype(BF16)
                grad_query = grad_query + dot(grad_scores[half, :], masked(masks[h], key), NN)
                grad_key = grad_key + dot(grad_scores[:, mine], masked(masks[h], query), TN)
                grad_value = grad_value + dot(prob[:, mine], grad_head, TN)
            gq_ref[b * WIN : (b + 1) * WIN, lanes] = grad_query * inv_root
        gk_ref[:, lanes] = grad_key * inv_root
        gv_ref[:, lanes] = grad_value
    heads = same_head(attn)
    for i, ref in enumerate((gq_ref, gk_ref)):
        values = raw_ref[:, i * attn : (i + 1) * attn]
        grad = ref[...]
        factor = lax.rsqrt(head_mean(values * values, heads) + EPS)
        inner = head_mean(grad * values, heads)
        grad = factor * grad - values * (factor * factor * factor) * inner
        mixed_ref[:, i * attn : (i + 1) * attn] = grad.astype(BF16)
    mixed_ref[:, 2 * attn :] = gv_ref[...].astype(BF16)

    grad_normed = dot(mixed_ref[...], wq_ref[...], NT)
    state0 = state0_ref[...]
    grad0 = grad1_ref[own_asked, :] + rms_back(state0, rms_factor(state0), grad_normed)
    grad0_b = grad0.astype(BF16)
    pooled = pooled_ref[...]
    pool_high, pool_low = split2(rms_back(pooled, rms_factor(pooled), grad0))
    high, low = spread_matrix(facts_ref[own, :], k_enc, reach)
    for r in range(4):
        store(r, 0, dot(turned(r, normed_ref[...]), mixed_ref[...], NN))
        store(r, 4 * attn + 256, dot(turned(r, grad0_b), jitter_ref[...], NN))
        first = turned(r, pool_high)
        grad = dot(first, high, NN) + dot(first, low, NN) + dot(turned(r, pool_low), high, NN)
        pre = dot(wet_ref[r * quarter : (r + 1) * quarter, :], x_ref[...], NT)
        grad_high, grad_low = split2(grad * silu_slope(pre))
        store(r, 4 * attn, dot(grad_high, x_ref[...], NN) + dot(grad_low, x_ref[...], NN))


def call(kernel, args, outs, scratch, name):
    return pl.pallas_call(
        kernel,
        out_shape=[jax.ShapeDtypeStruct(*out) for out in outs],
        scratch_shapes=[pltpu.VMEM(*one) for one in scratch],
        compiler_params=pltpu.CompilerParams(vmem_limit_bytes=48 << 20),
        interpret=INTERPRET,
        name=name,
    )(*args)


def per_device(
    slabs,
    loader,
    hidden_jitter,
    w_noise,
    w_enc,
    enc_offset,
    enc_weight,
    w_qkv,
    window_offset,
    w_out,
    unpacker_linear_map,
    dec_offset,
    unpacker_arc_scales,
):
    members = lax.axis_size(MEMBER)
    shards = lax.axis_size(GRID)
    channels, width = w_enc.shape
    attn = w_out.shape[0]
    heads = attn // HEAD_DIM
    points = slabs.shape[1]
    nodes = enc_offset.shape[0]
    per_node = points // nodes
    sub = points // members
    noise = w_noise.shape[0]
    k_enc = enc_offset.shape[1]
    k_dec = dec_offset.shape[1]
    inv_root = HEAD_DIM ** (-0.5)

    pieces = swap(slabs[0].reshape(members, sub, 2 * channels), MEMBER)
    piece = lax.dynamic_index_in_dim(pieces, loader[0], 0, keepdims=False)
    truth = piece[:, channels:].astype(F32)

    packed = jnp.concatenate(
        [enc_offset.astype(BF16)]
        + three_terms(enc_weight)
        + [window_offset[:, None].astype(BF16)]
        + [dec_offset.reshape(nodes, per_node * k_dec).astype(BF16)]
        + three_terms(unpacker_arc_scales.reshape(nodes, per_node * k_dec)),
        axis=1,
    )
    packed = jnp.pad(packed, ((0, 0), (0, channels - packed.shape[1])))
    share = nodes // members
    member = lax.axis_index(MEMBER)
    shard = lax.axis_index(GRID)
    jitter_rows = nodes * noise // channels
    chunk = jnp.concatenate(
        [
            piece[:, :channels],
            hidden_jitter[0].reshape(jitter_rows, channels),
            lax.dynamic_slice_in_dim(packed, member * share, share, 0),
        ],
        axis=0,
    )
    got = swap(jnp.broadcast_to(chunk[None], (shards,) + chunk.shape), GRID)
    far2, low, mid, high, far1 = (
        lax.dynamic_index_in_dim(got, (shard + o) % shards, 0, keepdims=False)
        for o in (-2, -1, 0, 1, 2)
    )
    at = sub + jitter_rows
    far = jnp.where(member >= members // 2, far2[:sub], far1[:sub])
    payload = jnp.concatenate(
        [low[:sub], mid[:sub], high[:sub], far, low[at:], mid[at:], high[at:]], axis=0
    )
    got = swap(jnp.broadcast_to(payload[None], (members,) + payload.shape), MEMBER)
    x_parts = [
        got[:, i * sub : (i + 1) * sub].reshape(points, channels) for i in range(3)
    ]
    x_own = x_parts[1]
    far = got[:, 3 * sub : 4 * sub]
    x_all = jnp.concatenate(
        [far[members // 2 :].reshape(-1, channels)]
        + x_parts
        + [far[: members // 2].reshape(-1, channels)],
        axis=0,
    )
    packed = got[:, 4 * sub :].reshape(members, 3, share, channels)
    packed = packed.transpose(1, 0, 2, 3).reshape(3 * nodes, channels)
    jitter_all = jnp.concatenate([low[sub:at], mid[sub:at], high[sub:at]], axis=0)
    jitter_all = jnp.pad(jitter_all.reshape(3 * nodes, noise), ((0, 0), (0, channels - noise)))
    packed = packed.astype(F32)

    def column(start, count):
        return packed[:, start : start + count]

    def summed(start, count):
        return sum(column(start + i * count, count) for i in range(1, 3)) + column(start, count)

    each = per_node * k_dec
    at = 4 * k_enc
    facts = jnp.concatenate(
        [
            column(0, k_enc),
            summed(k_enc, k_enc),
            column(at, 1),
            column(at + 1, each),
            summed(at + 1 + each, each),
        ],
        axis=1,
    )
    facts = jnp.pad(facts, ((0, 0), (0, channels - facts.shape[1])))
    w_noise = jnp.pad(w_noise, ((0, channels - noise), (0, 0)))
    residuals = [
        ((nodes, width), F32),
        ((nodes, width), F32),
        ((nodes, width), BF16),
        ((nodes, 2 * attn), F32),
        ((3 * nodes, attn), BF16),
        ((3 * nodes, attn), BF16),
        ((3 * nodes, attn), BF16),
        ((2 * attn // HEAD_DIM, nodes, 2 * nodes), BF16),
        ((ASKED, attn), BF16),
        ((ASKED, width), F32),
        ((ASKED, width), BF16),
    ]
    forecast, *saved = call(
        functools.partial(forward_kernel, k_enc, k_dec),
        (x_all, facts, jitter_all, w_noise, w_enc, w_qkv, w_out, unpacker_linear_map),
        [((points, channels), F32)] + residuals,
        [
            ((4 * points, width), BF16),
            ((3 * nodes, width), F32),
            ((ASKED, channels), F32),
        ],
        "forward",
    )

    cells = swap(forecast.reshape(members, sub, channels), MEMBER)
    loss_scale = float(members * points * shards * channels) ** (-0.5)
    fair = jnp.sum(eased_sensitivity(cells[:, None] - cells[None, :]), axis=1)
    sensitivity = (
        eased_sensitivity(cells - truth[None]) / members - fair / (members * (members - 1))
    ) * loss_scale
    grad_forecast = swap(sensitivity.astype(BF16), MEMBER).reshape(points, channels)
    grad_low, grad_high = shifted(grad_forecast, 1), shifted(grad_forecast, -1)

    zl, x = (lax.axis_size(a) for a in MEMBER)
    zh, y, core = (lax.axis_size(a) for a in GRID)
    rows = width // (members * shards)
    order = jnp.arange(width, dtype=jnp.int32).reshape(core, x, y, zl, zh, rows)
    c_i, x_i, y_i, zl_i, zh_i, r_i = (
        lax.broadcasted_iota(jnp.int32, order.shape, d) for d in range(6)
    )
    c_i = c_i ^ lax.axis_index("core")
    target = ((((zl_i * x + x_i) * zh + zh_i) * y + y_i) * core + c_i) * rows + r_i
    target = target.reshape(width, 1)
    reorder = (lax.broadcasted_iota(jnp.int32, (width, width), 1) == target).astype(BF16)
    w_enc_turned = dot(reorder, w_enc, NT).astype(BF16)
    lanes = 4 * attn + 3 * channels
    kept, sent = call(
        functools.partial(backward_kernel, k_enc, k_dec),
        (
            grad_low,
            grad_forecast,
            grad_high,
            facts,
            facts.T,
            x_all[points : 3 * points],
            jitter_all[nodes : 2 * nodes],
            w_enc_turned,
            w_qkv,
            w_out,
            unpacker_linear_map,
            reorder,
            *saved,
        ),
        [((width // core, lanes), BF16)] * 2,
        [
            ((ASKED, width), F32),
            ((ASKED, width), BF16),
            ((ASKED, attn), BF16),
            ((nodes, attn), F32),
            ((nodes, attn), F32),
            ((nodes, attn), F32),
            ((nodes, 3 * attn), BF16),
        ],
        "backward",
    )

    total = kept.astype(F32) + lax.ppermute(sent, "core", [(0, 1), (1, 0)]).astype(F32)
    total = swap(total.astype(BF16).reshape(x * y, -1, lanes), ("x", "y"))
    total = jnp.sum(total.astype(F32), axis=0)
    total = swap(total.astype(BF16).reshape(zl * zh, rows, lanes), ("zl", "zh"))
    total = jnp.sum(total.astype(F32), axis=0)
    grad_qkv, grad_out, grad_enc, grad_map, grad_noise = (
        total[:, start:stop]
        for start, stop in (
            (0, 3 * attn),
            (3 * attn, 4 * attn),
            (4 * attn, 4 * attn + channels),
            (4 * attn + channels, 4 * attn + 2 * channels),
            (4 * attn + 2 * channels, 4 * attn + 2 * channels + noise),
        )
    )
    return (grad_noise.T, grad_enc.T, grad_qkv, grad_out.T, grad_map)


def solution(mesh):
    member, grid = mesh.shape["member"], mesh.shape["grid"]
    inner = 4 if member == 16 else 2
    fine = Mesh(
        mesh.devices.reshape(member // inner, inner, 2, grid // 4, 2), MEMBER + GRID
    )
    in_specs = (
        P(MEMBER, GRID, None),
        P(),
        P(MEMBER, GRID, None),
        P(),
        P(),
        P(GRID, None),
        P(GRID, None),
        P(),
        P(GRID),
        P(),
        P(),
        P(GRID, None),
        P(GRID, None),
    )
    both = MEMBER + GRID
    out_specs = (P(None, both), P(None, both), P(both, None), P(None, both), P(both, None))
    return jax.shard_map(
        per_device, mesh=fine, in_specs=in_specs, out_specs=out_specs, check_vma=False
    )
```

time: 242 us -> 203 us (0.84)
  matrix products: 55.8 us -> 2.5 us
  Pallas kernels: 0 us -> 35.1 us
  other arithmetic: 29.3 us -> 11.5 us
  local copies, waits for them, and re-layouts: 30.2 us -> 19.9 us
  waiting for transfers between devices: 38.2 us -> 47.6 us
    dot_general x26 -> x1, matrix products: 40.9 us -> 2.5 us  [dot(): lax.dot_general(left, right, (dims, ((), ())), preferred_element_type=F32...]
    pallas_call x0 -> x2, Pallas kernels: none -> 35.1 us  [call(): pl.pallas_call(kernel, out_shape=[jax.ShapeDtypeStruct(*out) for out in o...]
    dot_general x5 -> x0, matrix products: 10.4 us -> none  [the longest x1 2.46 us: per_device(): jnp.einsum('qhd,khd->hqk', query_norm, key_norm, preferred_element_type=F32)]
    slice x9 -> x3, local copies, waits for them, and re-layouts: 8.83 us -> 1.2 us  [the longest x2 1.19 us: per_device(): total[:, start:stop]]
    unnamed x125 -> x65, local copies, waits for them, and re-layouts: 7.82 us -> 13.8 us
    all_to_all x5, waiting for transfers between devices: 28.6 us -> 33.6 us  [swap(): return lax.all_to_all(values, axes, split_axis=0, concat_axis=0, tiled=True)]
    sub x1 -> x0, matrix products: 4.59 us -> none  [per_device(): grad_probs - jnp.sum(prob_wide * grad_probs, axis=-1, keepdims=True)]
    ppermute x2, waiting for transfers between devices: 4.6 us -> 9.04 us  [shifted(): lax.ppermute(values, GRID, [(i, (i + step) % count) for i in range(count)])]
  transfers between devices with their start and end apart: 8 -> 8, of which waited for: 7 -> 8; matrix products, arithmetic and copies ran while one was open for 9% -> 6% of each run, Pallas kernels for 0% -> 0%
where the time goes in v1:
time: 203 us; the launch traced here: 201 us
  blocking collectives  49.3 us (24%)
  waiting for transfers between devices  47.6 us (23%)
  Pallas kernels  35.1 us (17%)
  starting transfers between devices  33.8 us (17%)
  local copies, waits for them, and re-layouts  19.9 us (10%)
  other arithmetic  11.5 us (6%)
  matrix products  2.5 us (1%)
    all_to_all x2, blocking collectives, swap(): return lax.all_to_all(values, axes, split_axis=0, concat_axis=0, tiled=True)  49.3 us
    pallas_call x2, Pallas kernels, call(): pl.pallas_call(kernel, out_shape=[jax.ShapeDtypeStruct(*out) for out in o...  35.1 us
    all_to_all x5, waiting for transfers between devices, swap(): return lax.all_to_all(values, axes, split_axis=0, concat_axis=0, tiled=True)  33.6 us
    all_to_all x5, starting transfers between devices, swap(): return lax.all_to_all(values, axes, split_axis=0, concat_axis=0, tiled=True)  33.3 us
    unnamed x65, local copies, waits for them, and re-layouts  13.8 us
    ppermute x2, waiting for transfers between devices, shifted(): lax.ppermute(values, GRID, [(i, (i + step) % count) for i in range(count)])  9.04 us
    ppermute x1, waiting for transfers between devices, per_device(): lax.ppermute(sent, 'core', [(0, 1), (1, 0)]).astype(F32)  4.93 us
  transfers between devices with their start and end apart: 8, of which 8 were waited for; matrix products, arithmetic and copies ran while one was open for 6% of the time, Pallas kernels for 0%

profile of v1, /device:TPU:32, one launch (start us, length us, event | category | flops | bytes accessed | tf_op | source)
XLA Modules:
  0.0 201.4 jit_solution(15281291120484621474)
XLA Ops:
  0.6 8.5 %all-to-all-start = ((bf16[16,16,256]{2,1,0:T(8,128)(2,1)}), bf16[16,16,256]{2,1,0:T(8,128)(2,1)S(1)}, u32[]{:S(2)}, u32[]{:S(2)}) async-start(bf16[16,16,256]{2,1,0:T(8,128)(2,1)} %bitcast.81), calls=%async_computation | async-start | bytes 262144 | tf_op jit(solution)/shard_map/all_to_all | solution.py:68
  9.8 0.7 convert_element_type.79
  10.5 0.7 convert_element_type.85
  11.2 0.7 fusion.7
  11.9 0.8 copy.113
  13.1 0.8 copy.115
  14.1 0.7 convert_bitcast_fusion.1
  15.3 0.8 all-to-all-done
  16.1 0.7 broadcast_in_dim.4
  16.8 8.5 %all-to-all-start.1 = ((bf16[16,40,128]{2,1,0:T(8,128)(2,1)}), bf16[16,40,128]{2,1,0:T(8,128)(2,1)S(1)}, u32[]{:S(2)}, u32[]{:S(2)}) async-start(bf16[16,40,128]{2,1,0:T(8,128)(2,1)} %broadcast_in_dim.4), calls=%async_computation.1 | async-start | bytes 327680 | tf_op jit(solution)/shard_map/all_to_all | solution.py:68
  25.4 12.6 %all-to-all-done.1 = bf16[16,40,128]{2,1,0:T(8,128)(2,1)S(1)} async-done(((bf16[16,40,128]{2,1,0:T(8,128)(2,1)}), bf16[16,40,128]{2,1,0:T(8,128)(2,1)S(1)}, u32[]{:S(2)}, u32[]{:S(2)}) %all-to-all-start.1) | async-done | bytes 163872 | tf_op jit(solution)/shard_map/all_to_all | solution.py:68
  38.1 0.8 broadcast_in_dim.5
  38.8 5.8 %all-to-all-start.2 = ((bf16[16,88,128]{2,1,0:T(8,128)(2,1)}), bf16[16,88,128]{2,1,0:T(8,128)(2,1)S(1)}, u32[]{:S(2)}, u32[]{:S(2)}) async-start(bf16[16,88,128]{2,1,0:T(8,128)(2,1)} %broadcast_in_dim.5), calls=%async_computation.2 | async-start | bytes 720896 | tf_op jit(solution)/shard_map/all_to_all | solution.py:68
  45.2 10.8 %all-to-all-done.2 = bf16[16,88,128]{2,1,0:T(8,128)(2,1)S(1)} async-done(((bf16[16,88,128]{2,1,0:T(8,128)(2,1)}), bf16[16,88,128]{2,1,0:T(8,128)(2,1)S(1)}, u32[]{:S(2)}, u32[]{:S(2)}) %all-to-all-start.2) | async-done | bytes 360480 | tf_op jit(solution)/shard_map/all_to_all | solution.py:68
  57.8 0.5 copy-done.20
  58.4 13.6 %forward.1 = (f32[256,128]{1,0:T(8,128)}, f32[128,1024]{1,0:T(8,128)S(1)}, f32[128,1024]{1,0:T(8,128)S(1)}, bf16[128,1024]{1,0:T(8,128)(2,1)S(1)}, f32[128,1024]...) custom-call(bf16[1024,128]{1,0:T(8,128)(2,1)S(1)} %constant_dynamic-, ...), custom_call_target="tpu_custom_call" | custom-call | tf_op jit(solution)/shard_map/forward/pallas_call | solution.py:312
  72.0 0.8 copy-done.2
  72.8 0.8 copy-done.4
  73.6 0.7 copy-done.6
  74.3 0.8 copy-done.8
  75.1 0.7 copy-done.10
  75.8 5.1 %all-to-all-start.3 = ((f32[16,16,128]{2,1,0:T(8,128)}), f32[16,16,128]{2,1,0:T(8,128)}, u32[]{:S(2)}, u32[]{:S(2)}) async-start(f32[16,16,128]{2,1,0:T(8,128)} %bitcast.22), calls=%async_computation.3 | async-start | bytes 262144 | tf_op jit(solution)/shard_map/all_to_all | solution.py:68
  80.9 1.7 fusion.refs_11_
  82.7 5.3 %all-to-all-done.3 = f32[16,16,128]{2,1,0:T(8,128)} async-done(((f32[16,16,128]{2,1,0:T(8,128)}), f32[16,16,128]{2,1,0:T(8,128)}, u32[]{:S(2)}, u32[]{:S(2)}) %all-to-all-start.3) | async-done | bytes 131104 | tf_op jit(solution)/shard_map/all_to_all | solution.py:68
  88.0 1.4 fusion.4
  89.4 1.6 multiply_convert_fusion
  91.0 5.4 %all-to-all-start.4 = ((bf16[16,16,128]{2,1,0:T(8,128)(2,1)}), bf16[16,16,128]{2,1,0:T(8,128)(2,1)S(1)}, u32[]{:S(2)}, u32[]{:S(2)}) async-start(bf16[16,16,128]{2,1,0:T(8,128)(2,1)} %multiply_convert_fusion), calls=%async_computation.4 | async-start | bytes 131072 | tf_op jit(solution)/shard_map/all_to_all | solution.py:68
  96.4 2.5 %fusion.6.refs_7_ = bf16[1024,128]{1,0:T(8,128)(2,1)} fusion(bf16[128,1024]{1,0:T(8,128)(2,1)} %refs_4_.1, s32[1024]{0:T(1024)S(1)} %reshape.141), kind=kOutput, calls=%fused_computation.10 | convolution fusion | flops 269615104 | bytes 528384 | tf_op jit(solution)/shard_map/dot_general | solution.py:48
  98.9 4.2 %all-to-all-done.4 = bf16[16,16,128]{2,1,0:T(8,128)(2,1)S(1)} async-done(((bf16[16,16,128]{2,1,0:T(8,128)(2,1)}), bf16[16,16,128]{2,1,0:T(8,128)(2,1)S(1)}, u32[]{:S(2)}, u32[]{:S(2)}) %all-to-all-start.4) | async-done | bytes 65568 | tf_op jit(solution)/shard_map/all_to_all | solution.py:68
  103.6 0.9 pad_maximum_fusion.refs_5_
  104.4 1.2 collective-permute-done.1.refs_2_
  105.6 7.9 %collective-permute-done.refs_0_ = bf16[256,128]{1,0:T(8,128)(2,1)S(1)} collective-permute-done((bf16[256,128]{1,0:T(8,128)(2,1)S(1)}, bf16[256,128]{1,0:T(8,128)(2,1)S(1)}, u32[]{:S(2)}, u32[]{:S(2)}) %collective-permute-start) | collective-permute-done | bytes 65568 | tf_op jit(solution)/shard_map/ppermute | solution.py:73
  113.5 1.0 copy-done.3
  114.5 1.0 copy-done.5
  115.5 1.0 copy-done.7
  116.5 1.0 copy-done.9
  117.5 0.9 copy-done.11
  118.5 0.9 copy-done.13
  119.4 0.9 copy-done.14
  120.4 21.5 %backward.1 = (bf16[512,2432]{1,0:T(8,128)(2,1)}, bf16[512,2432]{1,0:T(8,128)(2,1)}) custom-call(bf16[256,128]{1,0:T(8,128)(2,1)S(1)} %collective-permute-done.refs_0_, bf16[256,128]{1,0:T(8,128)(2,1)S(1)} %bitcast.70, bf16[256,128]{1,0:T(8,128)(2,1)S(1)} %collective-permute-done.1.refs_2_, f32[384,128]{1,0:T(8,128)S(1)} %copy.129.refs_1_.refs_3_, ...), custom_call_target="tpu_custom_call" | custom-call | tf_op jit(solution)/shard_map/backward/pallas_call | solution.py:312
  141.8 4.9 %collective-permute-done.2 = bf16[512,2432]{1,0:T(8,128)(2,1)S(1)} collective-permute-done((bf16[512,2432]{1,0:T(8,128)(2,1)}, bf16[512,2432]{1,0:T(8,128)(2,1)S(1)}, u32[]{:S(2)}, u32[]{:S(2)}) %collective-permute-start.2) | collective-permute-done | bytes 2490400 | tf_op jit(solution)/shard_map/ppermute | solution.py:501
  146.7 2.4 %add_convert_fusion = bf16[512,2432]{1,0:T(8,128)(2,1)S(1)} fusion(bf16[512,2432]{1,0:T(8,128)(2,1)S(1)} %collective-permute-done.2, bf16[512,2432]{1,0:T(8,128)(2,1)} %get-tuple-element.31), kind=kLoop, calls=%fused_computation | loop fusion | flops 4980736 | bytes 7471104 | tf_op jit(solution)/shard_map/convert_element_type | solution.py:502
  149.1 35.5 %all_to_all.35 = bf16[16,32,2432]{2,1,0:T(8,128)(2,1)S(1)} all-to-all(bf16[16,32,2432]{2,1,0:T(8,128)(2,1)S(1)} %bitcast.74), channel_id=1, replica_groups=mesh['zl'=4,'x'=4,'zh'=2,'y'=4,'core'=2] {'x','y'}, dimensions={0} | all-to-all | bytes 4980736 | tf_op jit(solution)/shard_map/all_to_all | solution.py:68
  185.0 13.9 %all_to_all.36 = bf16[8,4,2432]{2,1,0:T(4,128)(2,1)S(1)} all-to-all(bf16[8,4,2432]{2,1,0:T(4,128)(2,1)S(1)} %reshape.132), channel_id=1, replica_groups=mesh['zl'=4,'x'=4,'zh'=2,'y'=4,'core'=2] {'zl','zh'}, dimensions={0} | all-to-all | bytes 311296 | tf_op jit(solution)/shard_map/all_to_all | solution.py:68
  199.0 0.6 slice_bitcast_fusion.3
  199.6 0.6 fusion.18
  200.2 0.6 slice_bitcast_fusion.1
  200.8 0.6 slice.198
  (93 shorter events, 4.5 us)
Async XLA Ops:
  0.6 44.4 %copy-start.22 = (bf16[16,1024]{1,0:T(8,128)(2,1)S(1)}, bf16[16,1024]{1,0:T(8,128)(2,1)}, u32[]{:S(2)}) copy-start(bf16[16,1024]{1,0:T(8,128)(2,1)} %param.16) | copy-start | bytes 98308
  0.6 15.4 %all-to-all-start = ((bf16[16,16,256]{2,1,0:T(8,128)(2,1)}), bf16[16,16,256]{2,1,0:T(8,128)(2,1)S(1)}, u32[]{:S(2)}, u32[]{:S(2)}) async-start(bf16[16,16,256]{2,1,0:T(8,128)(2,1)} %bitcast.81), calls=%async_computation | async-start | bytes 262144 | tf_op jit(solution)/shard_map/all_to_all | solution.py:68
  16.8 21.2 %all-to-all-start.1 = ((bf16[16,40,128]{2,1,0:T(8,128)(2,1)}), bf16[16,40,128]{2,1,0:T(8,128)(2,1)S(1)}, u32[]{:S(2)}, u32[]{:S(2)}) async-start(bf16[16,40,128]{2,1,0:T(8,128)(2,1)} %broadcast_in_dim.4), calls=%async_computation.1 | async-start | bytes 327680 | tf_op jit(solution)/shard_map/all_to_all | solution.py:68
  38.8 17.2 %all-to-all-start.2 = ((bf16[16,88,128]{2,1,0:T(8,128)(2,1)}), bf16[16,88,128]{2,1,0:T(8,128)(2,1)S(1)}, u32[]{:S(2)}, u32[]{:S(2)}) async-start(bf16[16,88,128]{2,1,0:T(8,128)(2,1)} %broadcast_in_dim.5), calls=%async_computation.2 | async-start | bytes 720896 | tf_op jit(solution)/shard_map/all_to_all | solution.py:68
  45.2 10.8 %copy-start.16 = (bf16[384,16]{1,0:T(8,128)(2,1)}, bf16[384,16]{1,0:T(8,128)(2,1)S(1)}, u32[]{:S(2)}) copy-start(bf16[384,16]{1,0:T(8,128)(2,1)S(1)} %reshape.128) | copy-start | bytes 36868
  56.4 2.0 copy-start.1
  56.4 2.0 copy-start.15
  57.7 0.6 copy-start.20
  57.7 0.6 copy-start.21
  57.7 14.3 %copy-start.18 = (bf16[16,16,128]{2,1,0:T(8,128)(2,1)}, bf16[16,16,128]{2,1,0:T(8,128)(2,1)S(1)}, u32[]{:S(2)}) copy-start(bf16[16,16,128]{2,1,0:T(8,128)(2,1)S(1)} %get-tuple-element.35) | copy-start | bytes 196612
  72.0 0.8 copy-start.2
  72.8 0.8 copy-start.4
  73.6 0.7 copy-start.6
  74.3 0.8 copy-start.8
  75.1 0.7 copy-start.10
  75.8 5.1 %copy-start.12 = (bf16[256,512]{1,0:T(8,128)(2,1)}, bf16[256,512]{1,0:T(8,128)(2,1)S(1)}, u32[]{:S(2)}) copy-start(bf16[256,512]{1,0:T(8,128)(2,1)S(1)} %get-tuple-element.28.refs_20_) | copy-start | bytes 786436
  75.8 12.2 %all-to-all-start.3 = ((f32[16,16,128]{2,1,0:T(8,128)}), f32[16,16,128]{2,1,0:T(8,128)}, u32[]{:S(2)}, u32[]{:S(2)}) async-start(f32[16,16,128]{2,1,0:T(8,128)} %bitcast.22), calls=%async_computation.3 | async-start | bytes 262144 | tf_op jit(solution)/shard_map/all_to_all | solution.py:68
  80.9 18.0 %copy-start.17 = (bf16[384,16]{1,0:T(8,128)(2,1)S(1)}, bf16[384,16]{1,0:T(8,128)(2,1)}, u32[]{:S(2)}) copy-start(bf16[384,16]{1,0:T(8,128)(2,1)} %copy-done.16) | copy-start | bytes 36868
  80.9 22.7 %copy-start.19 = (bf16[16,16,128]{2,1,0:T(8,128)(2,1)S(1)}, bf16[16,16,128]{2,1,0:T(8,128)(2,1)}, u32[]{:S(2)}) copy-start(bf16[16,16,128]{2,1,0:T(8,128)(2,1)} %copy-done.18) | copy-start | bytes 196612
  82.7 30.8 %copy-start = (bf16[512,1024]{1,0:T(8,128)(2,1)S(1)}, bf16[512,1024]{1,0:T(8,128)(2,1)}, u32[]{:S(2)}) copy-start(bf16[512,1024]{1,0:T(8,128)(2,1)} %refs_9_.1) | copy-start | bytes 3145732
  91.0 12.1 %all-to-all-start.4 = ((bf16[16,16,128]{2,1,0:T(8,128)(2,1)}), bf16[16,16,128]{2,1,0:T(8,128)(2,1)S(1)}, u32[]{:S(2)}, u32[]{:S(2)}) async-start(bf16[16,16,128]{2,1,0:T(8,128)(2,1)} %multiply_convert_fusion), calls=%async_computation.4 | async-start | bytes 131072 | tf_op jit(solution)/shard_map/all_to_all | solution.py:68
  103.1 2.5 %collective-permute-start.1 = (bf16[256,128]{1,0:T(8,128)(2,1)S(1)}, bf16[256,128]{1,0:T(8,128)(2,1)S(1)}, u32[]{:S(2)}, u32[]{:S(2)}) collective-permute-start(bf16[256,128]{1,0:T(8,128)(2,1)S(1)} %bitcast.68), channel_id=1, source_target_pairs={{0,15},{1,0},{2,1},{3,2},{4,3},{5,4},{6,5},{7,6},{8,7},{9,8},{10,9... | collective-permute-start | bytes 196616 | tf_op jit(solution)/shard_map/ppermute | solution.py:73
  103.1 10.4 %collective-permute-start = (bf16[256,128]{1,0:T(8,128)(2,1)S(1)}, bf16[256,128]{1,0:T(8,128)(2,1)S(1)}, u32[]{:S(2)}, u32[]{:S(2)}) collective-permute-start(bf16[256,128]{1,0:T(8,128)(2,1)S(1)} %bitcast.69), channel_id=1, source_target_pairs={{0,1},{1,2},{2,3},{3,4},{4,5},{5,6},{6,7},{7,8},{8,9},{9,10},{10,1... | collective-permute-start | bytes 196616 | tf_op jit(solution)/shard_map/ppermute | solution.py:73
  113.5 1.0 copy-start.3
  114.5 1.0 copy-start.5
  115.5 1.0 copy-start.7
  116.5 1.0 copy-start.9
  117.5 0.9 copy-start.11
  118.5 0.9 copy-start.13
  119.4 0.9 copy-start.14
  141.8 4.9 %collective-permute-start.2 = (bf16[512,2432]{1,0:T(8,128)(2,1)}, bf16[512,2432]{1,0:T(8,128)(2,1)S(1)}, u32[]{:S(2)}, u32[]{:S(2)}) collective-permute-start(bf16[512,2432]{1,0:T(8,128)(2,1)} %get-tuple-element.32), channel_id=1, source_target_pairs={{0,1},{1,0},{2,3},{3,2},{4,5},{5,4},{6,7},{7,6},{8,9},{9,8},{10,11... | collective-permute-start | bytes 7471112 | tf_op jit(solution)/shard_map/ppermute | solution.py:501

commit v2 on v1

--- a/solution.py
+++ b/solution.py
@@ -114,7 +114,7 @@
     return jnp.where(point == 2 * node + parity, 1.0, 0.0).astype(BF16)
 
 
-def forward_kernel(k_enc, k_dec, *refs):
+def forward_kernel(k_enc, k_dec, need, push, *refs):
     x_ref, facts_ref, jitter_ref, wn_ref, we_ref, wq_ref, wo_ref, u_ref = refs[:8]
     (forecast_ref, pooled_ref, state0_ref, normed_ref, raw_ref, qn_ref, kn_ref, v_ref) = refs[8:16]
     prob_ref, att_ref, state1_ref, dnorm_ref, msg_ref, all0_ref, proj_ref = refs[16:]
@@ -138,6 +138,8 @@
         state0 = pooled * rms_factor(pooled) + dot(jitter_ref[rows, :], wn_ref[...], NN)
         all0_ref[rows, :] = state0
         normed = (state0 * rms_factor(state0)).astype(BF16)
+        if s == 0:
+            need(5)
         mixed = dot(normed, wq_ref[...], NN)
         queries, keys = mixed[:, :attn], mixed[:, attn : 2 * attn]
         qn_ref[rows, :] = (
@@ -150,6 +152,9 @@
             state0_ref[...] = state0
             normed_ref[...] = normed
             raw_ref[...] = mixed[:, : 2 * attn]
+            push(1, 2, 3, 4)
+    push(5, 6, 7)
+    need(6, 7)
 
     masks = head_masks()
     span = 2 * NODES
@@ -180,6 +185,7 @@
         dnorm = (state1 * rms_factor(state1)).astype(BF16)
         dnorm_ref[rows, :] = dnorm
         proj_ref[rows, :] = dot(dnorm, u_ref[...], NN)
+    push(8, 9, 10, 11)
 
     proj_high, proj_low = split2(proj_ref[...])
     facts = facts_ref[NODES : 2 * NODES, :]
@@ -201,7 +207,7 @@
     forecast_ref[...] = forecast
 
 
-def backward_kernel(k_enc, k_dec, *refs):
+def backward_kernel(k_enc, k_dec, need, push, *refs):
     (low_ref, mid_ref, high_ref, facts_ref, turned_ref, x_ref, jitter_ref, wet_ref) = refs[:8]
     (wq_ref, wo_ref, u_ref, order_ref, pooled_ref, state0_ref, normed_ref, raw_ref) = refs[8:16]
     (qn_ref, kn_ref, v_ref, prob_ref, att_ref, state1_ref, dnorm_ref) = refs[16:23]
@@ -238,6 +244,7 @@
             high, low = split2(arcs)
             grad_proj = grad_proj + dot(high, grad, NN) + dot(low, grad, NN)
     proj_high, proj_low = split2(grad_proj)
+    need(21, 10, 9)
     for b in range(2):
         rows = slice(b * NODES, (b + 1) * NODES)
         state1 = state1_ref[rows, :]
@@ -246,6 +253,7 @@
         grad1_ref[rows, :] = grad
         g1b_ref[rows, :] = grad.astype(BF16)
         ga_ref[rows, :] = dot(g1b_ref[rows, :], wo_ref[...], NT).astype(BF16)
+    need(22, 11, 20)
     for r in range(4):
         dnorm = turned(r, dnorm_ref[own_asked, :])
         store(
@@ -255,6 +263,7 @@
         )
         store(r, 3 * attn, dot(turned(r, g1b_ref[own_asked, :]), att_ref[own_asked, :], NN))
 
+    need(16, 17, 18, 19)
     masks = head_masks()
     for pair in range(attn // 128):
         lanes = slice(pair * 128, (pair + 1) * 128)
@@ -282,6 +291,7 @@
         gk_ref[:, lanes] = grad_key * inv_root
         gv_ref[:, lanes] = grad_value
     heads = same_head(attn)
+    need(15)
     for i, ref in enumerate((gq_ref, gk_ref)):
         values = raw_ref[:, i * attn : (i + 1) * attn]
         grad = ref[...]
@@ -291,6 +301,7 @@
         mixed_ref[:, i * attn : (i + 1) * attn] = grad.astype(BF16)
     mixed_ref[:, 2 * attn :] = gv_ref[...].astype(BF16)
 
+    need(8, 13, 12, 14, 7)
     grad_normed = dot(mixed_ref[...], wq_ref[...], NT)
     state0 = state0_ref[...]
     grad0 = grad1_ref[own_asked, :] + rms_back(state0, rms_factor(state0), grad_normed)
@@ -308,11 +319,56 @@
         store(r, 4 * attn, dot(grad_high, x_ref[...], NN) + dot(grad_low, x_ref[...], NN))
 
 
-def call(kernel, args, outs, scratch, name):
+def call(kernel, args, late, outs, pushed, scratch, name):
+    n_in, n_out = len(args), len(outs)
+    sems = len(late) + len(pushed)
+
+    def body(*refs):
+        ins, out_refs = list(refs[:n_in]), list(refs[n_in : n_in + n_out])
+        rest = refs[n_in + n_out :]
+        sem, rest = rest[0], rest[1:]
+        incoming, outgoing = {}, {}
+        for j, i in enumerate(late):
+            incoming[i] = pltpu.make_async_copy(ins[i], rest[j], sem.at[j])
+            incoming[i].start()
+            ins[i] = rest[j]
+        for j, o in enumerate(pushed):
+            buffer = rest[len(late) + j]
+            outgoing[o] = pltpu.make_async_copy(buffer, out_refs[o], sem.at[len(late) + j])
+            out_refs[o] = buffer
+
+        def need(*which):
+            for i in which:
+                incoming[i].wait()
+
+        def push(*which):
+            for o in which:
+                outgoing[o].start()
+
+        kernel(need, push, *ins, *out_refs, *rest[sems:])
+        for o in pushed:
+            outgoing[o].wait()
+
+    vmem = pl.BlockSpec(memory_space=pltpu.VMEM)
+    hbm = pl.BlockSpec(memory_space=pltpu.HBM)
+    buffers = [pltpu.VMEM(args[i].shape, args[i].dtype) for i in late]
+    buffers += [pltpu.VMEM(*outs[o]) for o in pushed]
+    if not INTERPRET:
+        args = [
+            pltpu.with_memory_space_constraint(arg, pltpu.HBM) if i in late else arg
+            for i, arg in enumerate(args)
+        ]
     return pl.pallas_call(
-        kernel,
-        out_shape=[jax.ShapeDtypeStruct(*out) for out in outs],
-        scratch_shapes=[pltpu.VMEM(*one) for one in scratch],
+        body,
+        out_shape=[
+            (pltpu.HBM if o in pushed and not INTERPRET else jax.ShapeDtypeStruct)(*out)
+            for o, out in enumerate(outs)
+        ],
+        in_specs=[hbm if i in late else vmem for i in range(n_in)],
+        out_specs=[hbm if o in pushed else vmem for o in range(n_out)],
+        scratch_shapes=[pltpu.SemaphoreType.DMA((sems,))]
+        + buffers
+        + [pltpu.VMEM(*one) for one in scratch],
         compiler_params=pltpu.CompilerParams(vmem_limit_bytes=48 << 20),
         interpret=INTERPRET,
         name=name,
@@ -363,7 +419,6 @@
     packed = jnp.pad(packed, ((0, 0), (0, channels - packed.shape[1])))
     share = nodes // members
     member = lax.axis_index(MEMBER)
-    shard = lax.axis_index(GRID)
     jitter_rows = nodes * noise // channels
     chunk = jnp.concatenate(
         [
@@ -373,13 +428,14 @@
         ],
         axis=0,
     )
-    got = swap(jnp.broadcast_to(chunk[None], (shards,) + chunk.shape), GRID)
-    far2, low, mid, high, far1 = (
-        lax.dynamic_index_in_dim(got, (shard + o) % shards, 0, keepdims=False)
-        for o in (-2, -1, 0, 1, 2)
-    )
+    low, mid, high = shifted(chunk, 1), chunk, shifted(chunk, -1)
     at = sub + jitter_rows
-    far = jnp.where(member >= members // 2, far2[:sub], far1[:sub])
+    pairs = []
+    for m in range(members):
+        step = 2 if m >= members // 2 else -2
+        for i in range(shards):
+            pairs.append((m * shards + i, m * shards + (i + step) % shards))
+    far = lax.ppermute(piece[:, :channels], MEMBER + GRID, pairs)
     payload = jnp.concatenate(
         [low[:sub], mid[:sub], high[:sub], far, low[at:], mid[at:], high[at:]], axis=0
     )
@@ -437,7 +493,9 @@
     forecast, *saved = call(
         functools.partial(forward_kernel, k_enc, k_dec),
         (x_all, facts, jitter_all, w_noise, w_enc, w_qkv, w_out, unpacker_linear_map),
+        (5, 6, 7),
         [((points, channels), F32)] + residuals,
+        tuple(range(1, 1 + len(residuals))),
         [
             ((4 * points, width), BF16),
             ((3 * nodes, width), F32),
@@ -485,7 +543,9 @@
             reorder,
             *saved,
         ),
+        (21, 10, 9, 22, 11, 20, 16, 17, 18, 19, 15, 8, 13, 12, 14, 7),
         [((width // core, lanes), BF16)] * 2,
+        (),
         [
             ((ASKED, width), F32),
             ((ASKED, width), BF16),

time: 203 us -> 176 us (0.87)
  local copies, waits for them, and re-layouts: 19.9 us -> 7.89 us
  waiting for transfers between devices: 47.6 us -> 38.3 us
  starting transfers between devices: 33.8 us -> 38.8 us
  other arithmetic: 11.5 us -> 7.01 us
  Pallas kernels: 35.1 us -> 31.9 us
    all_to_all x5 -> x4, waiting for transfers between devices: 33.6 us -> 21.8 us  [swap(): return lax.all_to_all(values, axes, split_axis=0, concat_axis=0, tiled=True)]
    unnamed x65 -> x21, local copies, waits for them, and re-layouts: 13.8 us -> 2.55 us
    ppermute x0 -> x1, starting transfers between devices: none -> 7.02 us  [per_device(): far = lax.ppermute(piece[:, :channels], MEMBER + GRID, pairs)]
    all_to_all x5 -> x4, starting transfers between devices: 33.3 us -> 26.4 us  [swap(): return lax.all_to_all(values, axes, split_axis=0, concat_axis=0, tiled=True)]
    ppermute x2 -> x4, starting transfers between devices: 0.51 us -> 5.3 us  [shifted(): lax.ppermute(values, GRID, [(i, (i + step) % count) for i in range(count)])]
    pallas_call x2, Pallas kernels: 35.1 us -> 31.9 us  [call(): pl.pallas_call(body, out_shape=[(pltpu.HBM if o in pushed and (not INTERP...]
    ppermute x2 -> x4, waiting for transfers between devices: 9.04 us -> 11.8 us  [shifted(): lax.ppermute(values, GRID, [(i, (i + step) % count) for i in range(count)])]
  transfers between devices with their start and end apart: 8 -> 10, of which waited for: 8 -> 9; matrix products, arithmetic and copies ran while one was open for 6% -> 5% of each run, Pallas kernels for 0% -> 0%
where the time goes in v2:
time: 176 us; the launch traced here: 175 us
  blocking collectives  48 us (27%)
  starting transfers between devices  38.8 us (22%)
  waiting for transfers between devices  38.3 us (22%)
  Pallas kernels  31.9 us (18%)
  local copies, waits for them, and re-layouts  7.89 us (4%)
  other arithmetic  7.01 us (4%)
    all_to_all x2, blocking collectives, swap(): return lax.all_to_all(values, axes, split_axis=0, concat_axis=0, tiled=True)  48 us
    pallas_call x2, Pallas kernels, call(): pl.pallas_call(body, out_shape=[(pltpu.HBM if o in pushed and (not INTERP...  31.9 us
    all_to_all x4, starting transfers between devices, swap(): return lax.all_to_all(values, axes, split_axis=0, concat_axis=0, tiled=True)  26.4 us
    all_to_all x4, waiting for transfers between devices, swap(): return lax.all_to_all(values, axes, split_axis=0, concat_axis=0, tiled=True)  21.8 us
    ppermute x4, waiting for transfers between devices, shifted(): lax.ppermute(values, GRID, [(i, (i + step) % count) for i in range(count)])  11.8 us
    ppermute x1, starting transfers between devices, per_device(): far = lax.ppermute(piece[:, :channels], MEMBER + GRID, pairs)  7.02 us
    ppermute x4, starting transfers between devices, shifted(): lax.ppermute(values, GRID, [(i, (i + step) % count) for i in range(count)])  5.3 us
    ppermute x1, waiting for transfers between devices, per_device(): lax.ppermute(sent, 'core', [(0, 1), (1, 0)]).astype(F32)  4.71 us
  transfers between devices with their start and end apart: 10, of which 9 were waited for; matrix products, arithmetic and copies ran while one was open for 5% of the time, Pallas kernels for 0%

profile of v2, /device:TPU:32, one launch (start us, length us, event | category | flops | bytes accessed | tf_op | source)
XLA Modules:
  0.0 175.0 jit_solution(888852108731344597)
XLA Ops:
  0.6 8.5 %all-to-all-start = ((bf16[16,16,256]{2,1,0:T(8,128)(2,1)}), bf16[16,16,256]{2,1,0:T(8,128)(2,1)S(1)}, u32[]{:S(2)}, u32[]{:S(2)}) async-start(bf16[16,16,256]{2,1,0:T(8,128)(2,1)} %bitcast.47), calls=%async_computation | async-start | bytes 262144 | tf_op jit(solution)/shard_map/all_to_all | solution.py:68
  9.8 0.7 convert_element_type.79
  10.5 0.7 convert_element_type.85
  11.2 0.7 fusion.7
  11.9 0.8 copy.115
  12.8 0.1 copy.116
  13.1 0.8 copy.117
  14.1 0.7 convert_bitcast_fusion.1
  14.8 0.3 concatenate.22
  15.3 0.8 all-to-all-done
  16.1 7.0 %collective-permute-start.2 = (bf16[16,128]{1,0:T(8,128)(2,1)S(1)}, bf16[16,128]{1,0:T(8,128)(2,1)S(1)}, u32[]{:S(2)}, u32[]{:S(2)}) collective-permute-start(bf16[16,128]{1,0:T(8,128)(2,1)S(1)} %slice.123), channel_id=1, source_target_pairs={{0,14},{1,15},{2,0},{3,1},{4,2},{5,3},{6,4},{7,5},{8,6},{9,7},{10,... | collective-permute-start | bytes 12296 | tf_op jit(solution)/shard_map/ppermute | solution.py:438
  23.2 1.4 collective-permute-start.1
  24.5 0.7 collective-permute-done
  25.3 0.7 collective-permute-done.1
  26.0 0.8 broadcast_in_dim.2
  26.8 7.4 %all-to-all-start.1 = ((bf16[16,88,128]{2,1,0:T(8,128)(2,1)}), bf16[16,88,128]{2,1,0:T(8,128)(2,1)S(1)}, u32[]{:S(2)}, u32[]{:S(2)}) async-start(bf16[16,88,128]{2,1,0:T(8,128)(2,1)} %broadcast_in_dim.2), calls=%async_computation.1 | async-start | bytes 720896 | tf_op jit(solution)/shard_map/all_to_all | solution.py:68
  34.2 0.2 multiply_add_fusion
  34.4 0.2 reshape.127
  34.6 0.1 reshape.114
  34.8 10.7 %all-to-all-done.1 = bf16[16,88,128]{2,1,0:T(8,128)(2,1)S(1)} async-done(((bf16[16,88,128]{2,1,0:T(8,128)(2,1)}), bf16[16,88,128]{2,1,0:T(8,128)(2,1)S(1)}, u32[]{:S(2)}, u32[]{:S(2)}) %all-to-all-start.1) | async-done | bytes 360480 | tf_op jit(solution)/shard_map/all_to_all | solution.py:68
  45.7 0.2 fusion.13
  45.9 0.2 fusion.12
  46.3 0.1 copy.140
  46.4 0.1 copy.142
  47.0 0.1 copy.132.refs_1_.refs_3_
  47.3 12.6 %forward.1 = (f32[256,128]{1,0:T(8,128)}, f32[128,1024]{1,0:T(8,128)}, f32[128,1024]{1,0:T(8,128)}, bf16[128,1024]{1,0:T(8,128)(2,1)}, f32[128,1024]{1,0:T(8,128...) custom-call(bf16[1024,128]{1,0:T(8,128)(2,1)S(1)} %constant_dynamic-, ...), custom_call_target="tpu_custom_call" | custom-call | tf_op jit(solution)/shard_map/forward/pallas_call | solution.py:361
  59.9 5.1 %all-to-all-start.2 = ((f32[16,16,128]{2,1,0:T(8,128)}), f32[16,16,128]{2,1,0:T(8,128)S(1)}, u32[]{:S(2)}, u32[]{:S(2)}) async-start(f32[16,16,128]{2,1,0:T(8,128)} %bitcast.12), calls=%async_computation.2 | async-start | bytes 262144 | tf_op jit(solution)/shard_map/all_to_all | solution.py:68
  65.0 1.7 fusion.refs_11_
  66.7 5.2 %all-to-all-done.2 = f32[16,16,128]{2,1,0:T(8,128)S(1)} async-done(((f32[16,16,128]{2,1,0:T(8,128)}), f32[16,16,128]{2,1,0:T(8,128)S(1)}, u32[]{:S(2)}, u32[]{:S(2)}) %all-to-all-start.2) | async-done | bytes 131104 | tf_op jit(solution)/shard_map/all_to_all | solution.py:68
  71.9 0.4 fusion.4
  72.3 0.7 multiply_convert_fusion
  73.0 5.4 %all-to-all-start.3 = ((bf16[16,16,128]{2,1,0:T(8,128)(2,1)}), bf16[16,16,128]{2,1,0:T(8,128)(2,1)S(1)}, u32[]{:S(2)}, u32[]{:S(2)}) async-start(bf16[16,16,128]{2,1,0:T(8,128)(2,1)} %multiply_convert_fusion), calls=%async_computation.3 | async-start | bytes 131072 | tf_op jit(solution)/shard_map/all_to_all | solution.py:68
  78.4 1.6 fusion.6.refs_7_
  80.0 5.1 %all-to-all-done.3 = bf16[16,16,128]{2,1,0:T(8,128)(2,1)S(1)} async-done(((bf16[16,16,128]{2,1,0:T(8,128)(2,1)}), bf16[16,16,128]{2,1,0:T(8,128)(2,1)S(1)}, u32[]{:S(2)}, u32[]{:S(2)}) %all-to-all-start.3) | async-done | bytes 65568 | tf_op jit(solution)/shard_map/all_to_all | solution.py:68
  85.1 3.9 %collective-permute-start.4 = (bf16[256,128]{1,0:T(8,128)(2,1)S(1)}, bf16[256,128]{1,0:T(8,128)(2,1)S(1)}, u32[]{:S(2)}, u32[]{:S(2)}) collective-permute-start(bf16[256,128]{1,0:T(8,128)(2,1)S(1)} %bitcast.34), channel_id=1, source_target_pairs={{0,15},{1,0},{2,1},{3,2},{4,3},{5,4},{6,5},{7,6},{8,7},{9,8},{10,9... | collective-permute-start | bytes 196616 | tf_op jit(solution)/shard_map/ppermute | solution.py:73
  88.9 2.5 %collective-permute-done.4.refs_2_ = bf16[256,128]{1,0:T(8,128)(2,1)S(1)} collective-permute-done((bf16[256,128]{1,0:T(8,128)(2,1)S(1)}, bf16[256,128]{1,0:T(8,128)(2,1)S(1)}, u32[]{:S(2)}, u32[]{:S(2)}) %collective-permute-start.4) | collective-permute-done | bytes 65568 | tf_op jit(solution)/shard_map/ppermute | solution.py:73
  91.5 7.9 %collective-permute-done.3.refs_0_ = bf16[256,128]{1,0:T(8,128)(2,1)S(1)} collective-permute-done((bf16[256,128]{1,0:T(8,128)(2,1)S(1)}, bf16[256,128]{1,0:T(8,128)(2,1)S(1)}, u32[]{:S(2)}, u32[]{:S(2)}) %collective-permute-start.3) | collective-permute-done | bytes 65568 | tf_op jit(solution)/shard_map/ppermute | solution.py:73
  99.3 19.3 %backward.1 = (bf16[512,2432]{1,0:T(8,128)(2,1)S(1)}, bf16[512,2432]{1,0:T(8,128)(2,1)S(1)}) custom-call(bf16[256,128]{1,0:T(8,128)(2,1)S(1)} %collective-permute-done.3.refs_0_, bf16[256,128]{1,0:T(8,128)(2,1)S(1)} %bitcast.36, bf16[256,128]{1,0:T(8,128)(2,1)S(1)} %collective-permute-done.4.refs_2_, f32[384,128]{1,0:T(8,128)S(1)} %copy.132.refs_1_.refs_3_, ...), custom_call_target="tpu_custom_call" | custom-call | tf_op jit(solution)/shard_map/backward/pallas_call | solution.py:361
  118.7 4.7 %collective-permute-done.5 = bf16[512,2432]{1,0:T(8,128)(2,1)S(1)} collective-permute-done((bf16[512,2432]{1,0:T(8,128)(2,1)S(1)}, bf16[512,2432]{1,0:T(8,128)(2,1)S(1)}, u32[]{:S(2)}, u32[]{:S(2)}) %collective-permute-start.5) | collective-permute-done | bytes 2490400 | tf_op jit(solution)/shard_map/ppermute | solution.py:561
  123.4 0.7 add_convert_fusion
  124.1 35.5 %all_to_all.30 = bf16[16,32,2432]{2,1,0:T(8,128)(2,1)S(1)} all-to-all(bf16[16,32,2432]{2,1,0:T(8,128)(2,1)S(1)} %bitcast.40), channel_id=1, replica_groups=mesh['zl'=4,'x'=4,'zh'=2,'y'=4,'core'=2] {'x','y'}, dimensions={0} | all-to-all | bytes 4980736 | tf_op jit(solution)/shard_map/all_to_all | solution.py:68
  159.6 0.4 reduce_sum.31
  160.0 12.5 %all_to_all.31 = bf16[8,4,2432]{2,1,0:T(4,128)(2,1)S(1)} all-to-all(bf16[8,4,2432]{2,1,0:T(4,128)(2,1)S(1)} %reshape.118), channel_id=1, replica_groups=mesh['zl'=4,'x'=4,'zh'=2,'y'=4,'core'=2] {'zl','zh'}, dimensions={0} | all-to-all | bytes 311296 | tf_op jit(solution)/shard_map/all_to_all | solution.py:68
  172.5 0.1 convert_reduce_fusion
  172.6 0.6 slice_bitcast_fusion.3
  173.2 0.6 fusion.14
  173.8 0.6 slice_bitcast_fusion.1
  174.4 0.6 slice.147
  (53 shorter events, 1.8 us)
Async XLA Ops:
  0.6 33.9 %copy-start.1 = (bf16[16,1024]{1,0:T(8,128)(2,1)S(1)}, bf16[16,1024]{1,0:T(8,128)(2,1)}, u32[]{:S(2)}) copy-start(bf16[16,1024]{1,0:T(8,128)(2,1)} %param.16) | copy-start | bytes 98308
  0.6 15.4 %all-to-all-start = ((bf16[16,16,256]{2,1,0:T(8,128)(2,1)}), bf16[16,16,256]{2,1,0:T(8,128)(2,1)S(1)}, u32[]{:S(2)}, u32[]{:S(2)}) async-start(bf16[16,16,256]{2,1,0:T(8,128)(2,1)} %bitcast.47), calls=%async_computation | async-start | bytes 262144 | tf_op jit(solution)/shard_map/all_to_all | solution.py:68
  16.1 9.2 %collective-permute-start = (bf16[40,128]{1,0:T(8,128)(2,1)S(1)}, bf16[40,128]{1,0:T(8,128)(2,1)S(1)}, u32[]{:S(2)}, u32[]{:S(2)}) collective-permute-start(bf16[40,128]{1,0:T(8,128)(2,1)S(1)} %pad_maximum_fusion.3), channel_id=1, source_target_pairs={{0,1},{1,2},{2,3},{3,4},{4,5},{5,6},{6,7},{7,8},{8,9},{9,10},{10,1... | collective-permute-start | bytes 30728 | tf_op jit(solution)/shard_map/ppermute | solution.py:73
  16.1 9.8 %collective-permute-start.2 = (bf16[16,128]{1,0:T(8,128)(2,1)S(1)}, bf16[16,128]{1,0:T(8,128)(2,1)S(1)}, u32[]{:S(2)}, u32[]{:S(2)}) collective-permute-start(bf16[16,128]{1,0:T(8,128)(2,1)S(1)} %slice.123), channel_id=1, source_target_pairs={{0,14},{1,15},{2,0},{3,1},{4,2},{5,3},{6,4},{7,5},{8,6},{9,7},{10,... | collective-permute-start | bytes 12296 | tf_op jit(solution)/shard_map/ppermute | solution.py:438
  23.2 2.8 %collective-permute-start.1 = (bf16[40,128]{1,0:T(8,128)(2,1)S(1)}, bf16[40,128]{1,0:T(8,128)(2,1)S(1)}, u32[]{:S(2)}, u32[]{:S(2)}) collective-permute-start(bf16[40,128]{1,0:T(8,128)(2,1)S(1)} %pad_maximum_fusion.3), channel_id=1, source_target_pairs={{0,15},{1,0},{2,1},{3,2},{4,3},{5,4},{6,5},{7,6},{8,7},{9,8},{10,9... | collective-permute-start | bytes 30728 | tf_op jit(solution)/shard_map/ppermute | solution.py:73
  26.8 18.7 %all-to-all-start.1 = ((bf16[16,88,128]{2,1,0:T(8,128)(2,1)}), bf16[16,88,128]{2,1,0:T(8,128)(2,1)S(1)}, u32[]{:S(2)}, u32[]{:S(2)}) async-start(bf16[16,88,128]{2,1,0:T(8,128)(2,1)} %broadcast_in_dim.2), calls=%async_computation.1 | async-start | bytes 720896 | tf_op jit(solution)/shard_map/all_to_all | solution.py:68
  45.9 1.4 copy-start
  59.9 12.0 %all-to-all-start.2 = ((f32[16,16,128]{2,1,0:T(8,128)}), f32[16,16,128]{2,1,0:T(8,128)S(1)}, u32[]{:S(2)}, u32[]{:S(2)}) async-start(f32[16,16,128]{2,1,0:T(8,128)} %bitcast.12), calls=%async_computation.2 | async-start | bytes 262144 | tf_op jit(solution)/shard_map/all_to_all | solution.py:68
  73.0 12.1 %all-to-all-start.3 = ((bf16[16,16,128]{2,1,0:T(8,128)(2,1)}), bf16[16,16,128]{2,1,0:T(8,128)(2,1)S(1)}, u32[]{:S(2)}, u32[]{:S(2)}) async-start(bf16[16,16,128]{2,1,0:T(8,128)(2,1)} %multiply_convert_fusion), calls=%async_computation.3 | async-start | bytes 131072 | tf_op jit(solution)/shard_map/all_to_all | solution.py:68
  85.1 6.4 %collective-permute-start.4 = (bf16[256,128]{1,0:T(8,128)(2,1)S(1)}, bf16[256,128]{1,0:T(8,128)(2,1)S(1)}, u32[]{:S(2)}, u32[]{:S(2)}) collective-permute-start(bf16[256,128]{1,0:T(8,128)(2,1)S(1)} %bitcast.34), channel_id=1, source_target_pairs={{0,15},{1,0},{2,1},{3,2},{4,3},{5,4},{6,5},{7,6},{8,7},{9,8},{10,9... | collective-permute-start | bytes 196616 | tf_op jit(solution)/shard_map/ppermute | solution.py:73
  88.9 10.4 %collective-permute-start.3 = (bf16[256,128]{1,0:T(8,128)(2,1)S(1)}, bf16[256,128]{1,0:T(8,128)(2,1)S(1)}, u32[]{:S(2)}, u32[]{:S(2)}) collective-permute-start(bf16[256,128]{1,0:T(8,128)(2,1)S(1)} %bitcast.35), channel_id=1, source_target_pairs={{0,1},{1,2},{2,3},{3,4},{4,5},{5,6},{6,7},{7,8},{8,9},{9,10},{10,1... | collective-permute-start | bytes 196616 | tf_op jit(solution)/shard_map/ppermute | solution.py:73
  118.6 4.8 %collective-permute-start.5 = (bf16[512,2432]{1,0:T(8,128)(2,1)S(1)}, bf16[512,2432]{1,0:T(8,128)(2,1)S(1)}, u32[]{:S(2)}, u32[]{:S(2)}) collective-permute-start(bf16[512,2432]{1,0:T(8,128)(2,1)S(1)} %get-tuple-element.32), channel_id=1, source_target_pairs={{0,1},{1,0},{2,3},{3,2},{4,5},{5,4},{6,7},{7,6},{8,9},{9,8},{10,11... | collective-permute-start | bytes 7471112 | tf_op jit(solution)/shard_map/ppermute | solution.py:561

commit v3 on v2

--- a/solution.py
+++ b/solution.py
@@ -35,8 +35,12 @@
     return factor * gradient - values * (factor * factor * factor) * inner
 
 
+def sigmoid(values):
+    return 0.5 + 0.5 * jnp.tanh(0.5 * values)
+
+
 def silu_slope(pre):
-    sigma = jax.nn.sigmoid(pre)
+    sigma = sigmoid(pre)
     return sigma * (1.0 + pre * (1.0 - sigma))
 
 
@@ -115,17 +119,44 @@
 
 
 def forward_kernel(k_enc, k_dec, need, push, *refs):
-    x_ref, facts_ref, jitter_ref, wn_ref, we_ref, wq_ref, wo_ref, u_ref = refs[:8]
-    (forecast_ref, pooled_ref, state0_ref, normed_ref, raw_ref, qn_ref, kn_ref, v_ref) = refs[8:16]
-    prob_ref, att_ref, state1_ref, dnorm_ref, msg_ref, all0_ref, proj_ref = refs[16:]
+    got_ref, jitter_ref, wn_ref, we_ref, wq_ref, wo_ref, u_ref = refs[:7]
+    (forecast_ref, pooled_ref, state0_ref, normed_ref, raw_ref, qn_ref, kn_ref, v_ref) = refs[7:15]
+    prob_ref, att_ref, state1_ref, dnorm_ref, facts_ref, near_ref = refs[15:21]
+    x_ref, msg_ref, all0_ref, proj_ref = refs[21:]
     attn = wo_ref.shape[0]
     reach = POINTS + 2 * RIM_G
     inv_root = HEAD_DIM ** (-0.5)
+    members = got_ref.shape[0]
+    sub, share = POINTS // members, NODES // members
+
+    for m in range(members):
+        for i in range(3):
+            start = RIM_G + i * POINTS + m * sub
+            x_ref[start : start + sub, :] = got_ref[m, i * sub : (i + 1) * sub, :]
+        start = m * sub - RIM_G if m >= members // 2 else RIM_G + 3 * POINTS + m * sub
+        x_ref[start : start + sub, :] = got_ref[m, 3 * sub : 4 * sub, :]
+    near_ref[...] = x_ref[POINTS : POINTS + reach, :]
+    each = 2 * k_dec
+    at = 4 * k_enc + 1
+    for m in range(members):
+        for i in range(3):
+            start = 4 * sub + i * share
+            facts_ref[i * NODES + m * share : i * NODES + (m + 1) * share, :] = got_ref[
+                m, start : start + share, :
+            ].astype(F32)
+    facts = facts_ref[...]
+    weight = sum(facts[:, k_enc * i : k_enc * (i + 1)] for i in (3, 2, 1))
+    scale = sum(facts[:, at + each * i : at + each * (i + 1)] for i in (3, 2, 1))
+    facts_ref[:, k_enc : 2 * k_enc] = weight
+    facts_ref[:, 2 * k_enc : 2 * k_enc + 1] = facts[:, at - 1 : at]
+    facts_ref[:, 2 * k_enc + 1 : 2 * k_enc + 1 + each] = facts[:, at : at + each]
+    facts_ref[:, 2 * k_enc + 1 + each : 2 * k_enc + 1 + 2 * each] = scale
+    push(12, 13)
 
     def message_rows(i, carry):
         rows = pl.ds(pl.multiple_of(i * 128, 128), 128)
         pre = dot(x_ref[rows, :], we_ref[...], NN)
-        msg_ref[rows, :] = (pre * jax.nn.sigmoid(pre)).astype(BF16)
+        msg_ref[rows, :] = (pre * sigmoid(pre)).astype(BF16)
         return carry
 
     lax.fori_loop(0, x_ref.shape[0] // 128, message_rows, 0)
@@ -139,7 +170,7 @@
         all0_ref[rows, :] = state0
         normed = (state0 * rms_factor(state0)).astype(BF16)
         if s == 0:
-            need(5)
+            need(4)
         mixed = dot(normed, wq_ref[...], NN)
         queries, keys = mixed[:, :attn], mixed[:, attn : 2 * attn]
         qn_ref[rows, :] = (
@@ -154,7 +185,7 @@
             raw_ref[...] = mixed[:, : 2 * attn]
             push(1, 2, 3, 4)
     push(5, 6, 7)
-    need(6, 7)
+    need(5, 6)
 
     masks = head_masks()
     span = 2 * NODES
@@ -176,7 +207,7 @@
             for h in range(2):
                 scores = dot(masked(masks[h], query), key, NT) * inv_root
                 weights = jnp.where(allowed, jnp.exp(scores), 0.0)
-                prob = (weights / jnp.sum(weights, axis=-1, keepdims=True)).astype(BF16)
+                prob = (weights * (1.0 / jnp.sum(weights, axis=-1, keepdims=True))).astype(BF16)
                 prob_ref[(b * attn // 128 + pair) * 2 + h] = prob
                 out = out + dot(prob, masked(masks[h], value), NN)
             att_ref[rows, lanes] = out.astype(BF16)
@@ -207,30 +238,25 @@
     forecast_ref[...] = forecast
 
 
-def backward_kernel(k_enc, k_dec, need, push, *refs):
-    (low_ref, mid_ref, high_ref, facts_ref, turned_ref, x_ref, jitter_ref, wet_ref) = refs[:8]
-    (wq_ref, wo_ref, u_ref, order_ref, pooled_ref, state0_ref, normed_ref, raw_ref) = refs[8:16]
-    (qn_ref, kn_ref, v_ref, prob_ref, att_ref, state1_ref, dnorm_ref) = refs[16:23]
-    kept_ref, sent_ref, grad1_ref, g1b_ref, ga_ref, gq_ref, gk_ref, gv_ref, mixed_ref = refs[23:]
-    attn, width = wo_ref.shape
-    reach = POINTS + 2 * RIM_G
-    inv_root = HEAD_DIM ** (-0.5)
-    own = slice(NODES, 2 * NODES)
-    own_asked = slice(WIN, WIN + NODES)
-    quarter = width // 4
-
-    def store(r, start, values):
-        ref = kept_ref if r < 2 else sent_ref
-        at = (r % 2) * quarter
-        ref[at : at + quarter, start : start + values.shape[1]] = values.astype(BF16)
-
-    def turned(r, values):
-        return dot(order_ref[r * quarter : (r + 1) * quarter, :], values, NT).astype(BF16)
-
-    grad_proj = jnp.zeros((ASKED, low_ref.shape[1]), F32)
+def prepare_kernel(k_enc, k_dec, need, push, *refs):
+    facts_ref, turned_ref, x_ref, wet_ref, order_ref, normed_ref, dnorm_ref = refs[:7]
+    slope_ref, nt_ref, dt_ref, sh_ref, sl_ref, ah_ref, al_ref = refs[7:]
+    quarter = order_ref.shape[0] // 4
+    for r in range(4):
+        rows = slice(r * quarter, (r + 1) * quarter)
+        slope_ref[rows, :] = silu_slope(dot(wet_ref[rows, :], x_ref[...], NT))
+    push(0)
+    for r in range(4):
+        rows = slice(r * quarter, (r + 1) * quarter)
+        nt_ref[rows, :] = dot(order_ref[rows, :], normed_ref[...], NT).astype(BF16)
+        dt_ref[rows, :] = dot(order_ref[rows, :], dnorm_ref[WIN : WIN + NODES, :], NT).astype(BF16)
+    push(1, 2)
+    facts = facts_ref[NODES : 2 * NODES, :]
+    sh_ref[...], sl_ref[...] = spread_matrix(facts, k_enc, POINTS + 2 * RIM_G)
+    push(3, 4)
     span = lax.broadcasted_iota(jnp.int32, (ASKED, NODES), 0)
     node = lax.broadcasted_iota(jnp.int32, (1, NODES), 1)
-    for s, ref in enumerate((low_ref, mid_ref, high_ref)):
+    for s in range(3):
         lanes = slice(s * NODES, (s + 1) * NODES)
         for parity in range(2):
             arcs = jnp.zeros((ASKED, NODES), F32)
@@ -240,11 +266,37 @@
                 source = source + (s * NODES - NODES + RIM_H)
                 scale = turned_ref[at + 2 * k_dec : at + 2 * k_dec + 1, lanes]
                 arcs = arcs + jnp.where(source == span, scale, 0.0)
+            ah_ref[2 * s + parity], al_ref[2 * s + parity] = split2(arcs)
+    push(5, 6)
+
+
+def backward_kernel(need, push, *refs):
+    (low_ref, mid_ref, high_ref, x_ref, jitter_ref, wq_ref, wo_ref, u_ref, order_ref) = refs[:9]
+    (pooled_ref, state0_ref, raw_ref, qn_ref, kn_ref, v_ref, prob_ref, att_ref) = refs[9:17]
+    (state1_ref, slope_ref, nt_ref, dt_ref, sh_ref, sl_ref, ah_ref, al_ref) = refs[17:25]
+    kept_ref, sent_ref, grad1_ref, g1b_ref, ga_ref, gq_ref, gk_ref, gv_ref, mixed_ref = refs[25:]
+    attn, width = wo_ref.shape
+    inv_root = HEAD_DIM ** (-0.5)
+    own_asked = slice(WIN, WIN + NODES)
+    quarter = width // 4
+
+    def store(r, start, values):
+        ref = kept_ref if r < 2 else sent_ref
+        at = (r % 2) * quarter
+        ref[at : at + quarter, start : start + values.shape[1]] = values.astype(BF16)
+
+    def turned(r, values):
+        return dot(order_ref[r * quarter : (r + 1) * quarter, :], values, NT).astype(BF16)
+
+    need(23, 24)
+    grad_proj = jnp.zeros((ASKED, low_ref.shape[1]), F32)
+    for s, ref in enumerate((low_ref, mid_ref, high_ref)):
+        for parity in range(2):
             grad = dot(interleave(parity, (NODES, POINTS), 1), ref[...], NN).astype(BF16)
-            high, low = split2(arcs)
-            grad_proj = grad_proj + dot(high, grad, NN) + dot(low, grad, NN)
+            grad_proj = grad_proj + dot(ah_ref[2 * s + parity], grad, NN)
+            grad_proj = grad_proj + dot(al_ref[2 * s + parity], grad, NN)
     proj_high, proj_low = split2(grad_proj)
-    need(21, 10, 9)
+    need(17, 7, 6)
     for b in range(2):
         rows = slice(b * NODES, (b + 1) * NODES)
         state1 = state1_ref[rows, :]
@@ -253,9 +305,9 @@
         grad1_ref[rows, :] = grad
         g1b_ref[rows, :] = grad.astype(BF16)
         ga_ref[rows, :] = dot(g1b_ref[rows, :], wo_ref[...], NT).astype(BF16)
-    need(22, 11, 20)
+    need(20, 8, 16)
     for r in range(4):
-        dnorm = turned(r, dnorm_ref[own_asked, :])
+        dnorm = dt_ref[r * quarter : (r + 1) * quarter, :]
         store(
             r,
             4 * attn + 128,
@@ -263,7 +315,7 @@
         )
         store(r, 3 * attn, dot(turned(r, g1b_ref[own_asked, :]), att_ref[own_asked, :], NN))
 
-    need(16, 17, 18, 19)
+    need(12, 13, 14, 15)
     masks = head_masks()
     for pair in range(attn // 128):
         lanes = slice(pair * 128, (pair + 1) * 128)
@@ -291,7 +343,7 @@
         gk_ref[:, lanes] = grad_key * inv_root
         gv_ref[:, lanes] = grad_value
     heads = same_head(attn)
-    need(15)
+    need(11)
     for i, ref in enumerate((gq_ref, gk_ref)):
         values = raw_ref[:, i * attn : (i + 1) * attn]
         grad = ref[...]
@@ -301,21 +353,21 @@
         mixed_ref[:, i * attn : (i + 1) * attn] = grad.astype(BF16)
     mixed_ref[:, 2 * attn :] = gv_ref[...].astype(BF16)
 
-    need(8, 13, 12, 14, 7)
+    need(5, 10, 9, 19, 18, 21, 22)
     grad_normed = dot(mixed_ref[...], wq_ref[...], NT)
     state0 = state0_ref[...]
     grad0 = grad1_ref[own_asked, :] + rms_back(state0, rms_factor(state0), grad_normed)
     grad0_b = grad0.astype(BF16)
     pooled = pooled_ref[...]
     pool_high, pool_low = split2(rms_back(pooled, rms_factor(pooled), grad0))
-    high, low = spread_matrix(facts_ref[own, :], k_enc, reach)
+    high, low = sh_ref[...], sl_ref[...]
     for r in range(4):
-        store(r, 0, dot(turned(r, normed_ref[...]), mixed_ref[...], NN))
+        rows = slice(r * quarter, (r + 1) * quarter)
+        store(r, 0, dot(nt_ref[rows, :], mixed_ref[...], NN))
         store(r, 4 * attn + 256, dot(turned(r, grad0_b), jitter_ref[...], NN))
         first = turned(r, pool_high)
         grad = dot(first, high, NN) + dot(first, low, NN) + dot(turned(r, pool_low), high, NN)
-        pre = dot(wet_ref[r * quarter : (r + 1) * quarter, :], x_ref[...], NT)
-        grad_high, grad_low = split2(grad * silu_slope(pre))
+        grad_high, grad_low = split2(grad * slope_ref[rows, :])
         store(r, 4 * attn, dot(grad_high, x_ref[...], NN) + dot(grad_low, x_ref[...], NN))
 
 
@@ -440,42 +492,8 @@
         [low[:sub], mid[:sub], high[:sub], far, low[at:], mid[at:], high[at:]], axis=0
     )
     got = swap(jnp.broadcast_to(payload[None], (members,) + payload.shape), MEMBER)
-    x_parts = [
-        got[:, i * sub : (i + 1) * sub].reshape(points, channels) for i in range(3)
-    ]
-    x_own = x_parts[1]
-    far = got[:, 3 * sub : 4 * sub]
-    x_all = jnp.concatenate(
-        [far[members // 2 :].reshape(-1, channels)]
-        + x_parts
-        + [far[: members // 2].reshape(-1, channels)],
-        axis=0,
-    )
-    packed = got[:, 4 * sub :].reshape(members, 3, share, channels)
-    packed = packed.transpose(1, 0, 2, 3).reshape(3 * nodes, channels)
     jitter_all = jnp.concatenate([low[sub:at], mid[sub:at], high[sub:at]], axis=0)
     jitter_all = jnp.pad(jitter_all.reshape(3 * nodes, noise), ((0, 0), (0, channels - noise)))
-    packed = packed.astype(F32)
-
-    def column(start, count):
-        return packed[:, start : start + count]
-
-    def summed(start, count):
-        return sum(column(start + i * count, count) for i in range(1, 3)) + column(start, count)
-
-    each = per_node * k_dec
-    at = 4 * k_enc
-    facts = jnp.concatenate(
-        [
-            column(0, k_enc),
-            summed(k_enc, k_enc),
-            column(at, 1),
-            column(at + 1, each),
-            summed(at + 1 + each, each),
-        ],
-        axis=1,
-    )
-    facts = jnp.pad(facts, ((0, 0), (0, channels - facts.shape[1])))
     w_noise = jnp.pad(w_noise, ((0, channels - noise), (0, 0)))
     residuals = [
         ((nodes, width), F32),
@@ -489,14 +507,17 @@
         ((ASKED, attn), BF16),
         ((ASKED, width), F32),
         ((ASKED, width), BF16),
+        ((3 * nodes, channels), F32),
+        ((points + 2 * RIM_G, channels), BF16),
     ]
     forecast, *saved = call(
         functools.partial(forward_kernel, k_enc, k_dec),
-        (x_all, facts, jitter_all, w_noise, w_enc, w_qkv, w_out, unpacker_linear_map),
-        (5, 6, 7),
+        (got, jitter_all, w_noise, w_enc, w_qkv, w_out, unpacker_linear_map),
+        (4, 5, 6),
         [((points, channels), F32)] + residuals,
         tuple(range(1, 1 + len(residuals))),
         [
+            ((4 * points, channels), BF16),
             ((4 * points, width), BF16),
             ((3 * nodes, width), F32),
             ((ASKED, channels), F32),
@@ -526,24 +547,48 @@
     reorder = (lax.broadcasted_iota(jnp.int32, (width, width), 1) == target).astype(BF16)
     w_enc_turned = dot(reorder, w_enc, NT).astype(BF16)
     lanes = 4 * attn + 3 * channels
+    pooled, state0, normed, raw, query, key, value, prob, attended, state1, dnorm, facts, near = saved
+    prepared = call(
+        functools.partial(prepare_kernel, k_enc, k_dec),
+        (facts, facts.T, near, w_enc_turned, reorder, normed, dnorm),
+        (),
+        [
+            ((width, points + 2 * RIM_G), F32),
+            ((width, nodes), BF16),
+            ((width, nodes), BF16),
+            ((nodes, points + 2 * RIM_G), BF16),
+            ((nodes, points + 2 * RIM_G), BF16),
+            ((3 * per_node, ASKED, nodes), BF16),
+            ((3 * per_node, ASKED, nodes), BF16),
+        ],
+        tuple(range(7)),
+        [],
+        "prepare",
+    )
     kept, sent = call(
-        functools.partial(backward_kernel, k_enc, k_dec),
+        backward_kernel,
         (
             grad_low,
             grad_forecast,
             grad_high,
-            facts,
-            facts.T,
-            x_all[points : 3 * points],
+            near,
             jitter_all[nodes : 2 * nodes],
-            w_enc_turned,
             w_qkv,
             w_out,
             unpacker_linear_map,
             reorder,
-            *saved,
+            pooled,
+            state0,
+            raw,
+            query,
+            key,
+            value,
+            prob,
+            attended,
+            state1,
+            *prepared,
         ),
-        (21, 10, 9, 22, 11, 20, 16, 17, 18, 19, 15, 8, 13, 12, 14, 7),
+        (23, 24, 17, 7, 6, 20, 8, 16, 12, 13, 14, 15, 11, 5, 10, 9, 19, 18, 21, 22),
         [((width // core, lanes), BF16)] * 2,
         (),
         [

time: 176 us -> 176 us (level)
  waiting for transfers between devices: 38.3 us -> 34.6 us
    ppermute x4, waiting for transfers between devices: 11.8 us -> 6.58 us  [shifted(): lax.ppermute(values, GRID, [(i, (i + step) % count) for i in range(count)])]
    pallas_call x2 -> x3, Pallas kernels: 31.9 us -> 33.5 us  [call(): pl.pallas_call(body, out_shape=[(pltpu.HBM if o in pushed and (not INTERP...]
  transfers between devices with their start and end apart: 10 -> 10, of which waited for: 9 -> 8; matrix products, arithmetic and copies ran while one was open for 5% -> 5% of each run, Pallas kernels for 0% -> 2%
where the time goes in v3:
time: 176 us; the launch traced here: 175 us
  blocking collectives  48.4 us (28%)
  starting transfers between devices  39.7 us (23%)
  waiting for transfers between devices  34.6 us (20%)
  Pallas kernels  33.5 us (19%)
  local copies, waits for them, and re-layouts  8.15 us (5%)
  other arithmetic  7.48 us (4%)
    all_to_all x2, blocking collectives, swap(): return lax.all_to_all(values, axes, split_axis=0, concat_axis=0, tiled=True)  48.4 us
    pallas_call x3, Pallas kernels, call(): pl.pallas_call(body, out_shape=[(pltpu.HBM if o in pushed and (not INTERP...  33.5 us
    all_to_all x4, starting transfers between devices, swap(): return lax.all_to_all(values, axes, split_axis=0, concat_axis=0, tiled=True)  26.6 us
    all_to_all x4, waiting for transfers between devices, swap(): return lax.all_to_all(values, axes, split_axis=0, concat_axis=0, tiled=True)  23.3 us
    ppermute x1, starting transfers between devices, per_device(): far = lax.ppermute(piece[:, :channels], MEMBER + GRID, pairs)  7.02 us
    ppermute x4, waiting for transfers between devices, shifted(): lax.ppermute(values, GRID, [(i, (i + step) % count) for i in range(count)])  6.58 us
    ppermute x4, starting transfers between devices, shifted(): lax.ppermute(values, GRID, [(i, (i + step) % count) for i in range(count)])  6.03 us
    ppermute x1, waiting for transfers between devices, per_device(): lax.ppermute(sent, 'core', [(0, 1), (1, 0)]).astype(F32)  4.71 us
  transfers between devices with their start and end apart: 10, of which 8 were waited for; matrix products, arithmetic and copies ran while one was open for 5% of the time, Pallas kernels for 2%

profile of v3, /device:TPU:32, one launch (start us, length us, event | category | flops | bytes accessed | tf_op | source)
XLA Modules:
  0.0 175.0 jit_solution(5785652765046468026)
XLA Ops:
  0.7 8.6 %all-to-all-start = ((bf16[16,16,256]{2,1,0:T(8,128)(2,1)}), bf16[16,16,256]{2,1,0:T(8,128)(2,1)S(1)}, u32[]{:S(2)}, u32[]{:S(2)}) async-start(bf16[16,16,256]{2,1,0:T(8,128)(2,1)} %bitcast.25), calls=%async_computation | async-start | bytes 262144 | tf_op jit(solution)/shard_map/all_to_all | solution.py:72
  9.9 0.7 convert_element_type.65
  10.6 0.7 convert_element_type.71
  11.3 0.7 fusion.7
  12.0 0.8 copy.56
  12.8 0.1 reshape_squeeze.7
  12.9 0.1 copy.57
  13.1 0.1 convert_element_type.72
  13.2 0.8 copy.58
  14.2 0.7 convert_bitcast_fusion
  14.9 0.3 concatenate.12
  15.4 0.8 all-to-all-done
  16.3 7.0 %collective-permute-start.2 = (bf16[16,128]{1,0:T(8,128)(2,1)S(1)}, bf16[16,128]{1,0:T(8,128)(2,1)S(1)}, u32[]{:S(2)}, u32[]{:S(2)}) collective-permute-start(bf16[16,128]{1,0:T(8,128)(2,1)S(1)} %slice.57), channel_id=1, source_target_pairs={{0,14},{1,15},{2,0},{3,1},{4,2},{5,3},{6,4},{7,5},{8,6},{9,7},{10,... | collective-permute-start | bytes 12296 | tf_op jit(solution)/shard_map/ppermute | solution.py:490
  23.3 1.4 collective-permute-start.1
  24.7 0.7 collective-permute-done
  25.4 0.7 collective-permute-done.1
  26.1 0.8 broadcast_in_dim.2
  26.9 7.4 %all-to-all-start.1 = ((bf16[16,88,128]{2,1,0:T(8,128)(2,1)}), bf16[16,88,128]{2,1,0:T(8,128)(2,1)S(1)}, u32[]{:S(2)}, u32[]{:S(2)}) async-start(bf16[16,88,128]{2,1,0:T(8,128)(2,1)} %broadcast_in_dim.2), calls=%async_computation.1 | async-start | bytes 720896 | tf_op jit(solution)/shard_map/all_to_all | solution.py:72
  34.4 0.2 multiply_add_fusion
  34.5 0.2 reshape.99
  34.8 0.1 reshape.88
  34.9 10.7 %all-to-all-done.1.refs_0_ = bf16[16,88,128]{2,1,0:T(8,128)(2,1)S(1)} async-done(((bf16[16,88,128]{2,1,0:T(8,128)(2,1)}), bf16[16,88,128]{2,1,0:T(8,128)(2,1)S(1)}, u32[]{:S(2)}, u32[]{:S(2)}) %all-to-all-start.1) | async-done | bytes 360480 | tf_op jit(solution)/shard_map/all_to_all | solution.py:72
  45.6 12.5 %forward.1 = (f32[256,128]{1,0:T(8,128)}, f32[128,1024]{1,0:T(8,128)}, f32[128,1024]{1,0:T(8,128)}, bf16[128,1024]{1,0:T(8,128)(2,1)}, f32[128,1024]{1,0:T(8,128...) custom-call(bf16[16,88,128]{2,1,0:T(8,128)(2,1)S(1)} %all-to-all-don, ...), custom_call_target="tpu_custom_call" | custom-call | tf_op jit(solution)/shard_map/forward/pallas_call | solution.py:413
  58.1 5.1 %all-to-all-start.2 = ((f32[16,16,128]{2,1,0:T(8,128)}), f32[16,16,128]{2,1,0:T(8,128)}, u32[]{:S(2)}, u32[]{:S(2)}) async-start(f32[16,16,128]{2,1,0:T(8,128)} %bitcast.4), calls=%async_computation.2 | async-start | bytes 262144 | tf_op jit(solution)/shard_map/all_to_all | solution.py:72
  63.3 0.4 fusion.1.refs_4_.refs_8_
  63.7 6.6 %all-to-all-done.2 = f32[16,16,128]{2,1,0:T(8,128)} async-done(((f32[16,16,128]{2,1,0:T(8,128)}), f32[16,16,128]{2,1,0:T(8,128)}, u32[]{:S(2)}, u32[]{:S(2)}) %all-to-all-start.2) | async-done | bytes 131104 | tf_op jit(solution)/shard_map/all_to_all | solution.py:72
  70.3 1.4 fusion.4
  71.8 1.6 multiply_convert_fusion
  73.3 5.4 %all-to-all-start.3 = ((bf16[16,16,128]{2,1,0:T(8,128)(2,1)}), bf16[16,16,128]{2,1,0:T(8,128)(2,1)S(1)}, u32[]{:S(2)}, u32[]{:S(2)}) async-start(bf16[16,16,128]{2,1,0:T(8,128)(2,1)} %multiply_convert_fusion), calls=%async_computation.3 | async-start | bytes 131072 | tf_op jit(solution)/shard_map/all_to_all | solution.py:72
  78.7 1.5 fusion.6.refs_3_
  80.3 5.1 %all-to-all-done.3 = bf16[16,16,128]{2,1,0:T(8,128)(2,1)S(1)} async-done(((bf16[16,16,128]{2,1,0:T(8,128)(2,1)}), bf16[16,16,128]{2,1,0:T(8,128)(2,1)S(1)}, u32[]{:S(2)}, u32[]{:S(2)}) %all-to-all-start.3) | async-done | bytes 65568 | tf_op jit(solution)/shard_map/all_to_all | solution.py:72
  85.4 4.6 %collective-permute-start.4 = (bf16[256,128]{1,0:T(8,128)(2,1)S(1)}, bf16[256,128]{1,0:T(8,128)(2,1)}, u32[]{:S(2)}, u32[]{:S(2)}) collective-permute-start(bf16[256,128]{1,0:T(8,128)(2,1)S(1)} %bitcast.21), channel_id=1, source_target_pairs={{0,15},{1,0},{2,1},{3,2},{4,3},{5,4},{6,5},{7,6},{8,7},{9,8},{10,9... | collective-permute-start | bytes 196616 | tf_op jit(solution)/shard_map/ppermute | solution.py:77
  90.0 0.8 pad_slice_fusion.refs_4_
  90.8 0.1 copy.64
  90.9 0.9 copy-done.5
  91.9 3.4 %prepare.1 = (f32[1024,512]{1,0:T(8,128)}, bf16[1024,128]{1,0:T(8,128)(2,1)}, bf16[1024,128]{1,0:T(8,128)(2,1)}, bf16[128,512]{1,0:T(8,128)(2,1)}, bf16[128,512]...) custom-call(f32[384,128]{1,0:T(8,128)S(1)} %copy-done.1, f32[128,384]{1,0:T(8,128)S(1)} %bitcast.20, ...), custom_call_target="tpu_custom_call" | custom-call | tf_op jit(solution)/shard_map/prepare/pallas_call | solution.py:413
  95.3 5.2 %collective-permute-done.3.refs_0_ = bf16[256,128]{1,0:T(8,128)(2,1)} collective-permute-done((bf16[256,128]{1,0:T(8,128)(2,1)S(1)}, bf16[256,128]{1,0:T(8,128)(2,1)}, u32[]{:S(2)}, u32[]{:S(2)}) %collective-permute-start.3) | collective-permute-done | bytes 65568 | tf_op jit(solution)/shard_map/ppermute | solution.py:77
  100.5 17.7 %backward.1 = (bf16[512,2432]{1,0:T(8,128)(2,1)S(1)}, bf16[512,2432]{1,0:T(8,128)(2,1)S(1)}) custom-call(bf16[256,128]{1,0:T(8,128)(2,1)} %collective-permute-done.3.refs_0_, bf16[256,128]{1,0:T(8,128)(2,1)S(1)} %bitcast.23, bf16[256,128]{1,0:T(8,128)(2,1)} %collective-permute-done.4.refs_2_, bf16[512,128]{1,0:T(8,128)(2,1)S(1)} %copy-done.2, ...), custom_call_target="tpu_custom_call" | custom-call | tf_op jit(solution)/shard_map/backward/pallas_call | solution.py:413
  118.3 4.7 %collective-permute-done.5 = bf16[512,2432]{1,0:T(8,128)(2,1)S(1)} collective-permute-done((bf16[512,2432]{1,0:T(8,128)(2,1)S(1)}, bf16[512,2432]{1,0:T(8,128)(2,1)S(1)}, u32[]{:S(2)}, u32[]{:S(2)}) %collective-permute-start.5) | collective-permute-done | bytes 2490400 | tf_op jit(solution)/shard_map/ppermute | solution.py:606
  123.0 0.7 add_convert_fusion
  123.7 35.5 %all_to_all.30 = bf16[16,32,2432]{2,1,0:T(8,128)(2,1)S(1)} all-to-all(bf16[16,32,2432]{2,1,0:T(8,128)(2,1)S(1)} %bitcast.24), channel_id=1, replica_groups=mesh['zl'=4,'x'=4,'zh'=2,'y'=4,'core'=2] {'x','y'}, dimensions={0} | all-to-all | bytes 4980736 | tf_op jit(solution)/shard_map/all_to_all | solution.py:72
  159.2 0.4 reduce_sum.31
  159.6 12.9 %all_to_all.31 = bf16[8,4,2432]{2,1,0:T(4,128)(2,1)S(1)} all-to-all(bf16[8,4,2432]{2,1,0:T(4,128)(2,1)S(1)} %reshape.92), channel_id=1, replica_groups=mesh['zl'=4,'x'=4,'zh'=2,'y'=4,'core'=2] {'zl','zh'}, dimensions={0} | all-to-all | bytes 311296 | tf_op jit(solution)/shard_map/all_to_all | solution.py:72
  172.5 0.1 convert_reduce_fusion
  172.6 0.6 slice_bitcast_fusion.2
  173.2 0.6 fusion.9
  173.8 0.6 slice_bitcast_fusion
  174.4 0.6 slice.67
  (44 shorter events, 0.7 us)
Async XLA Ops:
  0.6 34.1 %copy-start.8 = (bf16[16,1024]{1,0:T(8,128)(2,1)S(1)}, bf16[16,1024]{1,0:T(8,128)(2,1)}, u32[]{:S(2)}) copy-start(bf16[16,1024]{1,0:T(8,128)(2,1)} %param.16) | copy-start | bytes 98308
  0.6 45.0 %copy-start.6 = (bf16[128,1024]{1,0:T(8,128)(2,1)S(1)}, bf16[128,1024]{1,0:T(8,128)(2,1)}, u32[]{:S(2)}) copy-start(bf16[128,1024]{1,0:T(8,128)(2,1)} %refs_3_.1) | copy-start | bytes 786436
  0.7 15.5 %all-to-all-start = ((bf16[16,16,256]{2,1,0:T(8,128)(2,1)}), bf16[16,16,256]{2,1,0:T(8,128)(2,1)S(1)}, u32[]{:S(2)}, u32[]{:S(2)}) async-start(bf16[16,16,256]{2,1,0:T(8,128)(2,1)} %bitcast.25), calls=%async_computation | async-start | bytes 262144 | tf_op jit(solution)/shard_map/all_to_all | solution.py:72
  16.2 9.2 %collective-permute-start = (bf16[40,128]{1,0:T(8,128)(2,1)S(1)}, bf16[40,128]{1,0:T(8,128)(2,1)S(1)}, u32[]{:S(2)}, u32[]{:S(2)}) collective-permute-start(bf16[40,128]{1,0:T(8,128)(2,1)S(1)} %pad_maximum_fusion.1), channel_id=1, source_target_pairs={{0,1},{1,2},{2,3},{3,4},{4,5},{5,6},{6,7},{7,8},{8,9},{9,10},{10,1... | collective-permute-start | bytes 30728 | tf_op jit(solution)/shard_map/ppermute | solution.py:77
  16.3 9.8 %collective-permute-start.2 = (bf16[16,128]{1,0:T(8,128)(2,1)S(1)}, bf16[16,128]{1,0:T(8,128)(2,1)S(1)}, u32[]{:S(2)}, u32[]{:S(2)}) collective-permute-start(bf16[16,128]{1,0:T(8,128)(2,1)S(1)} %slice.57), channel_id=1, source_target_pairs={{0,14},{1,15},{2,0},{3,1},{4,2},{5,3},{6,4},{7,5},{8,6},{9,7},{10,... | collective-permute-start | bytes 12296 | tf_op jit(solution)/shard_map/ppermute | solution.py:490
  23.3 2.8 %collective-permute-start.1 = (bf16[40,128]{1,0:T(8,128)(2,1)S(1)}, bf16[40,128]{1,0:T(8,128)(2,1)S(1)}, u32[]{:S(2)}, u32[]{:S(2)}) collective-permute-start(bf16[40,128]{1,0:T(8,128)(2,1)S(1)} %pad_maximum_fusion.1), channel_id=1, source_target_pairs={{0,15},{1,0},{2,1},{3,2},{4,3},{5,4},{6,5},{7,6},{8,7},{9,8},{10,9... | collective-permute-start | bytes 30728 | tf_op jit(solution)/shard_map/ppermute | solution.py:77
  26.9 18.7 %all-to-all-start.1 = ((bf16[16,88,128]{2,1,0:T(8,128)(2,1)}), bf16[16,88,128]{2,1,0:T(8,128)(2,1)S(1)}, u32[]{:S(2)}, u32[]{:S(2)}) async-start(bf16[16,88,128]{2,1,0:T(8,128)(2,1)} %broadcast_in_dim.2), calls=%async_computation.1 | async-start | bytes 720896 | tf_op jit(solution)/shard_map/all_to_all | solution.py:72
  34.9 23.2 %copy-start.7 = (bf16[384,16]{1,0:T(8,128)(2,1)}, bf16[384,16]{1,0:T(8,128)(2,1)S(1)}, u32[]{:S(2)}) copy-start(bf16[384,16]{1,0:T(8,128)(2,1)S(1)} %reshape.88) | copy-start | bytes 36868
  58.1 12.2 %all-to-all-start.2 = ((f32[16,16,128]{2,1,0:T(8,128)}), f32[16,16,128]{2,1,0:T(8,128)}, u32[]{:S(2)}, u32[]{:S(2)}) async-start(f32[16,16,128]{2,1,0:T(8,128)} %bitcast.4), calls=%async_computation.2 | async-start | bytes 262144 | tf_op jit(solution)/shard_map/all_to_all | solution.py:72
  63.3 27.5 %copy-start.1 = (f32[384,128]{1,0:T(8,128)S(1)}, f32[384,128]{1,0:T(8,128)}, u32[]{:S(2)}) copy-start(f32[384,128]{1,0:T(8,128)} %get-tuple-element.39.refs_0_) | copy-start | bytes 589828
  63.7 31.6 %copy-start = (bf16[1024,1024]{1,0:T(8,128)(2,1)}, bf16[1024,1024]{1,0:T(8,128)(2,1)S(1)}, u32[]{:S(2)}) copy-start(bf16[1024,1024]{1,0:T(8,128)(2,1)S(1)} %fusion.1.refs_4_.refs_8_) | copy-start | bytes 6291460
  63.7 27.2 %copy-start.2 = (bf16[512,128]{1,0:T(8,128)(2,1)S(1)}, bf16[512,128]{1,0:T(8,128)(2,1)}, u32[]{:S(2)}) copy-start(bf16[512,128]{1,0:T(8,128)(2,1)} %get-tuple-element.29.refs_2_.refs_3_) | copy-start | bytes 393220
  63.7 27.2 %copy-start.3 = (bf16[256,1024]{1,0:T(8,128)(2,1)S(1)}, bf16[256,1024]{1,0:T(8,128)(2,1)}, u32[]{:S(2)}) copy-start(bf16[256,1024]{1,0:T(8,128)(2,1)} %get-tuple-element.41.refs_6_) | copy-start | bytes 1572868
  63.7 27.2 %copy-start.4 = (bf16[128,1024]{1,0:T(8,128)(2,1)S(1)}, bf16[128,1024]{1,0:T(8,128)(2,1)}, u32[]{:S(2)}) copy-start(bf16[128,1024]{1,0:T(8,128)(2,1)} %get-tuple-element.40.refs_5_) | copy-start | bytes 786436
  73.3 12.1 %all-to-all-start.3 = ((bf16[16,16,128]{2,1,0:T(8,128)(2,1)}), bf16[16,16,128]{2,1,0:T(8,128)(2,1)S(1)}, u32[]{:S(2)}, u32[]{:S(2)}) async-start(bf16[16,16,128]{2,1,0:T(8,128)(2,1)} %multiply_convert_fusion), calls=%async_computation.3 | async-start | bytes 131072 | tf_op jit(solution)/shard_map/all_to_all | solution.py:72
  85.4 9.9 %collective-permute-start.4 = (bf16[256,128]{1,0:T(8,128)(2,1)S(1)}, bf16[256,128]{1,0:T(8,128)(2,1)}, u32[]{:S(2)}, u32[]{:S(2)}) collective-permute-start(bf16[256,128]{1,0:T(8,128)(2,1)S(1)} %bitcast.21), channel_id=1, source_target_pairs={{0,15},{1,0},{2,1},{3,2},{4,3},{5,4},{6,5},{7,6},{8,7},{9,8},{10,9... | collective-permute-start | bytes 196616 | tf_op jit(solution)/shard_map/ppermute | solution.py:77
  90.0 10.5 %collective-permute-start.3 = (bf16[256,128]{1,0:T(8,128)(2,1)S(1)}, bf16[256,128]{1,0:T(8,128)(2,1)}, u32[]{:S(2)}, u32[]{:S(2)}) collective-permute-start(bf16[256,128]{1,0:T(8,128)(2,1)S(1)} %bitcast.22), channel_id=1, source_target_pairs={{0,1},{1,2},{2,3},{3,4},{4,5},{5,6},{6,7},{7,8},{8,9},{9,10},{10,1... | collective-permute-start | bytes 196616 | tf_op jit(solution)/shard_map/ppermute | solution.py:77
  90.9 1.0 copy-start.5
  118.2 4.8 %collective-permute-start.5 = (bf16[512,2432]{1,0:T(8,128)(2,1)S(1)}, bf16[512,2432]{1,0:T(8,128)(2,1)S(1)}, u32[]{:S(2)}, u32[]{:S(2)}) collective-permute-start(bf16[512,2432]{1,0:T(8,128)(2,1)S(1)} %get-tuple-element.50), channel_id=1, source_target_pairs={{0,1},{1,0},{2,3},{3,2},{4,5},{5,4},{6,7},{7,6},{8,9},{9,8},{10,11... | collective-permute-start | bytes 7471112 | tf_op jit(solution)/shard_map/ppermute | solution.py:606

commit v4 on v3

--- a/solution.py
+++ b/solution.py
@@ -72,9 +72,13 @@
     return lax.all_to_all(values, axes, split_axis=0, concat_axis=0, tiled=True)
 
 
-def shifted(values, step):
+def exchanged(values):
     count = lax.axis_size(GRID)
-    return lax.ppermute(values, GRID, [(i, (i + step) % count) for i in range(count)])
+    near = lax.ppermute(values, GRID, [(i, i ^ 1) for i in range(count)])
+    beyond = lax.ppermute(
+        values, GRID, [(i, (i + 1 if i % 2 else i - 1) % count) for i in range(count)]
+    )
+    return near, beyond
 
 
 def split2(values):
@@ -89,8 +93,7 @@
 
 
 def head_mean(values, heads):
-    high, low = split2(values)
-    return (dot(high, heads, NN) + dot(low, heads, NN)) * (1.0 / HEAD_DIM)
+    return dot(values.astype(BF16), heads, NN) * (1.0 / HEAD_DIM)
 
 
 def head_masks():
@@ -240,7 +243,7 @@
 
 def prepare_kernel(k_enc, k_dec, need, push, *refs):
     facts_ref, turned_ref, x_ref, wet_ref, order_ref, normed_ref, dnorm_ref = refs[:7]
-    slope_ref, nt_ref, dt_ref, sh_ref, sl_ref, ah_ref, al_ref = refs[7:]
+    slope_ref, nt_ref, dt_ref, sh_ref, ah_ref, al_ref = refs[7:]
     quarter = order_ref.shape[0] // 4
     for r in range(4):
         rows = slice(r * quarter, (r + 1) * quarter)
@@ -252,8 +255,8 @@
         dt_ref[rows, :] = dot(order_ref[rows, :], dnorm_ref[WIN : WIN + NODES, :], NT).astype(BF16)
     push(1, 2)
     facts = facts_ref[NODES : 2 * NODES, :]
-    sh_ref[...], sl_ref[...] = spread_matrix(facts, k_enc, POINTS + 2 * RIM_G)
-    push(3, 4)
+    sh_ref[...] = spread_matrix(facts, k_enc, POINTS + 2 * RIM_G)[0]
+    push(3)
     span = lax.broadcasted_iota(jnp.int32, (ASKED, NODES), 0)
     node = lax.broadcasted_iota(jnp.int32, (1, NODES), 1)
     for s in range(3):
@@ -267,13 +270,14 @@
                 scale = turned_ref[at + 2 * k_dec : at + 2 * k_dec + 1, lanes]
                 arcs = arcs + jnp.where(source == span, scale, 0.0)
             ah_ref[2 * s + parity], al_ref[2 * s + parity] = split2(arcs)
-    push(5, 6)
+    push(4, 5)
 
 
 def backward_kernel(need, push, *refs):
-    (low_ref, mid_ref, high_ref, x_ref, jitter_ref, wq_ref, wo_ref, u_ref, order_ref) = refs[:9]
+    (near_ref, mid_ref, beyond_ref, x_ref, jitter_ref, wq_ref, wo_ref, u_ref, order_ref) = refs[:9]
     (pooled_ref, state0_ref, raw_ref, qn_ref, kn_ref, v_ref, prob_ref, att_ref) = refs[9:17]
-    (state1_ref, slope_ref, nt_ref, dt_ref, sh_ref, sl_ref, ah_ref, al_ref) = refs[17:25]
+    (state1_ref, slope_ref, nt_ref, dt_ref, sh_ref, ah_ref, al_ref) = refs[17:24]
+    core_ref = refs[24]
     kept_ref, sent_ref, grad1_ref, g1b_ref, ga_ref, gq_ref, gk_ref, gv_ref, mixed_ref = refs[25:]
     attn, width = wo_ref.shape
     inv_root = HEAD_DIM ** (-0.5)
@@ -288,11 +292,15 @@
     def turned(r, values):
         return dot(order_ref[r * quarter : (r + 1) * quarter, :], values, NT).astype(BF16)
 
-    need(23, 24)
-    grad_proj = jnp.zeros((ASKED, low_ref.shape[1]), F32)
-    for s, ref in enumerate((low_ref, mid_ref, high_ref)):
+    need(22, 23)
+    odd = core_ref[0] == 1
+    near, beyond = near_ref[...].astype(F32), beyond_ref[...].astype(F32)
+    low = jnp.where(odd, near, beyond).astype(BF16)
+    high = jnp.where(odd, beyond, near).astype(BF16)
+    grad_proj = jnp.zeros((ASKED, mid_ref.shape[1]), F32)
+    for s, part in enumerate((low, mid_ref[...], high)):
         for parity in range(2):
-            grad = dot(interleave(parity, (NODES, POINTS), 1), ref[...], NN).astype(BF16)
+            grad = dot(interleave(parity, (NODES, POINTS), 1), part, NN).astype(BF16)
             grad_proj = grad_proj + dot(ah_ref[2 * s + parity], grad, NN)
             grad_proj = grad_proj + dot(al_ref[2 * s + parity], grad, NN)
     proj_high, proj_low = split2(grad_proj)
@@ -353,27 +361,40 @@
         mixed_ref[:, i * attn : (i + 1) * attn] = grad.astype(BF16)
     mixed_ref[:, 2 * attn :] = gv_ref[...].astype(BF16)
 
-    need(5, 10, 9, 19, 18, 21, 22)
+    need(5, 10, 9, 19, 18, 21)
     grad_normed = dot(mixed_ref[...], wq_ref[...], NT)
     state0 = state0_ref[...]
     grad0 = grad1_ref[own_asked, :] + rms_back(state0, rms_factor(state0), grad_normed)
     grad0_b = grad0.astype(BF16)
     pooled = pooled_ref[...]
-    pool_high, pool_low = split2(rms_back(pooled, rms_factor(pooled), grad0))
-    high, low = sh_ref[...], sl_ref[...]
+    grad_pooled = rms_back(pooled, rms_factor(pooled), grad0).astype(BF16)
+    spread = sh_ref[...]
     for r in range(4):
         rows = slice(r * quarter, (r + 1) * quarter)
         store(r, 0, dot(nt_ref[rows, :], mixed_ref[...], NN))
         store(r, 4 * attn + 256, dot(turned(r, grad0_b), jitter_ref[...], NN))
-        first = turned(r, pool_high)
-        grad = dot(first, high, NN) + dot(first, low, NN) + dot(turned(r, pool_low), high, NN)
-        grad_high, grad_low = split2(grad * slope_ref[rows, :])
-        store(r, 4 * attn, dot(grad_high, x_ref[...], NN) + dot(grad_low, x_ref[...], NN))
+        grad = dot(turned(r, grad_pooled), spread, NN) * slope_ref[rows, :]
+        store(r, 4 * attn, dot(grad.astype(BF16), x_ref[...], NN))
+
+
+def loss_kernel(scale, need, push, cells_ref, truth_ref, out_ref):
+    members = cells_ref.shape[0]
+    cells = [cells_ref[m] for m in range(members)]
+    fair = [jnp.zeros_like(cells[0]) for _ in range(members)]
+    for m in range(members):
+        for n in range(m + 1, members):
+            slope = eased_sensitivity(cells[m] - cells[n])
+            fair[m] = fair[m] + slope
+            fair[n] = fair[n] - slope
+    for m in range(members):
+        first = eased_sensitivity(cells[m] - truth_ref[...]) * (scale / members)
+        out_ref[m] = (first - fair[m] * (scale / (members * (members - 1)))).astype(BF16)
 
 
 def call(kernel, args, late, outs, pushed, scratch, name):
     n_in, n_out = len(args), len(outs)
     sems = len(late) + len(pushed)
+    smem = pl.BlockSpec(memory_space=pltpu.SMEM)
 
     def body(*refs):
         ins, out_refs = list(refs[:n_in]), list(refs[n_in : n_in + n_out])
@@ -416,9 +437,12 @@
             (pltpu.HBM if o in pushed and not INTERPRET else jax.ShapeDtypeStruct)(*out)
             for o, out in enumerate(outs)
         ],
-        in_specs=[hbm if i in late else vmem for i in range(n_in)],
+        in_specs=[
+            hbm if i in late else (smem if arg.shape == (1,) else vmem)
+            for i, arg in enumerate(args)
+        ],
         out_specs=[hbm if o in pushed else vmem for o in range(n_out)],
-        scratch_shapes=[pltpu.SemaphoreType.DMA((sems,))]
+        scratch_shapes=[pltpu.SemaphoreType.DMA((max(sems, 1),))]
         + buffers
         + [pltpu.VMEM(*one) for one in scratch],
         compiler_params=pltpu.CompilerParams(vmem_limit_bytes=48 << 20),
@@ -480,7 +504,9 @@
         ],
         axis=0,
     )
-    low, mid, high = shifted(chunk, 1), chunk, shifted(chunk, -1)
+    near, beyond = exchanged(chunk)
+    odd = lax.axis_index("core") == 1
+    low, mid, high = jnp.where(odd, near, beyond), chunk, jnp.where(odd, beyond, near)
     at = sub + jitter_rows
     pairs = []
     for m in range(members):
@@ -527,12 +553,17 @@
 
     cells = swap(forecast.reshape(members, sub, channels), MEMBER)
     loss_scale = float(members * points * shards * channels) ** (-0.5)
-    fair = jnp.sum(eased_sensitivity(cells[:, None] - cells[None, :]), axis=1)
-    sensitivity = (
-        eased_sensitivity(cells - truth[None]) / members - fair / (members * (members - 1))
-    ) * loss_scale
-    grad_forecast = swap(sensitivity.astype(BF16), MEMBER).reshape(points, channels)
-    grad_low, grad_high = shifted(grad_forecast, 1), shifted(grad_forecast, -1)
+    (sensitivity,) = call(
+        functools.partial(loss_kernel, loss_scale),
+        (cells, truth),
+        (),
+        [((members, sub, channels), BF16)],
+        (),
+        [],
+        "loss",
+    )
+    grad_forecast = swap(sensitivity, MEMBER).reshape(points, channels)
+    grad_near, grad_beyond = exchanged(grad_forecast)
 
     zl, x = (lax.axis_size(a) for a in MEMBER)
     zh, y, core = (lax.axis_size(a) for a in GRID)
@@ -557,20 +588,19 @@
             ((width, nodes), BF16),
             ((width, nodes), BF16),
             ((nodes, points + 2 * RIM_G), BF16),
-            ((nodes, points + 2 * RIM_G), BF16),
             ((3 * per_node, ASKED, nodes), BF16),
             ((3 * per_node, ASKED, nodes), BF16),
         ],
-        tuple(range(7)),
+        tuple(range(6)),
         [],
         "prepare",
     )
     kept, sent = call(
         backward_kernel,
         (
-            grad_low,
+            grad_near,
             grad_forecast,
-            grad_high,
+            grad_beyond,
             near,
             jitter_all[nodes : 2 * nodes],
             w_qkv,
@@ -587,8 +617,9 @@
             attended,
             state1,
             *prepared,
+            lax.axis_index("core").astype(jnp.int32).reshape(1),
         ),
-        (23, 24, 17, 7, 6, 20, 8, 16, 12, 13, 14, 15, 11, 5, 10, 9, 19, 18, 21, 22),
+        (22, 23, 17, 7, 6, 20, 8, 16, 12, 13, 14, 15, 11, 5, 10, 9, 19, 18, 21),
         [((width // core, lanes), BF16)] * 2,
         (),
         [

time: 176 us -> 172 us (0.977)
  other arithmetic: 7.48 us -> 4.52 us
  waiting for transfers between devices: 34.6 us -> 32.5 us
    all_to_all x4, starting transfers between devices: 26.6 us -> 32.8 us  [swap(): return lax.all_to_all(values, axes, split_axis=0, concat_axis=0, tiled=True)]
    ppermute x1, starting transfers between devices: 7.02 us -> 2.33 us  [per_device(): far = lax.ppermute(piece[:, :channels], MEMBER + GRID, pairs)]
    all_to_all x4, waiting for transfers between devices: 23.3 us -> 21 us  [swap(): return lax.all_to_all(values, axes, split_axis=0, concat_axis=0, tiled=True)]
    pallas_call x3 -> x4, Pallas kernels: 33.5 us -> 32.6 us  [call(): pl.pallas_call(body, out_shape=[(pltpu.HBM if o in pushed and (not INTERP...]
  transfers between devices with their start and end apart: 10 -> 10, of which waited for: 8 -> 7; matrix products, arithmetic and copies ran while one was open for 5% -> 6% of each run, Pallas kernels for 2% -> 2%
where the time goes in v4:
time: 172 us; the launch traced here: 171 us
  blocking collectives  48.1 us (28%)
  starting transfers between devices  41.1 us (24%)
  Pallas kernels  32.6 us (19%)
  waiting for transfers between devices  32.5 us (19%)
  local copies, waits for them, and re-layouts  8.54 us (5%)
  other arithmetic  4.52 us (3%)
  matrix products  2.48 us (1%)
    all_to_all x2, blocking collectives, swap(): return lax.all_to_all(values, axes, split_axis=0, concat_axis=0, tiled=True)  48.1 us
    all_to_all x4, starting transfers between devices, swap(): return lax.all_to_all(values, axes, split_axis=0, concat_axis=0, tiled=True)  32.8 us
    pallas_call x4, Pallas kernels, call(): pl.pallas_call(body, out_shape=[(pltpu.HBM if o in pushed and (not INTERP...  32.6 us
    all_to_all x4, waiting for transfers between devices, swap(): return lax.all_to_all(values, axes, split_axis=0, concat_axis=0, tiled=True)  21 us
    ppermute x2, waiting for transfers between devices, exchanged(): lax.ppermute(values, GRID, [(i, (i + 1 if i % 2 else i - 1) % count) for...  6.42 us
    ppermute x2, starting transfers between devices, exchanged(): lax.ppermute(values, GRID, [(i, (i + 1 if i % 2 else i - 1) % count) for...  5.91 us
    ppermute x1, waiting for transfers between devices, per_device(): lax.ppermute(sent, 'core', [(0, 1), (1, 0)]).astype(F32)  4.71 us
  transfers between devices with their start and end apart: 10, of which 7 were waited for; matrix products, arithmetic and copies ran while one was open for 6% of the time, Pallas kernels for 2%

profile of v4, /device:TPU:32, one launch (start us, length us, event | category | flops | bytes accessed | tf_op | source)
XLA Modules:
  0.0 171.4 jit_solution(3012783093306284333)
XLA Ops:
  0.7 8.6 %all-to-all-start = ((bf16[16,16,256]{2,1,0:T(8,128)(2,1)}), bf16[16,16,256]{2,1,0:T(8,128)(2,1)S(1)}, u32[]{:S(2)}, u32[]{:S(2)}) async-start(bf16[16,16,256]{2,1,0:T(8,128)(2,1)} %bitcast.26), calls=%async_computation | async-start | bytes 262144 | tf_op jit(solution)/shard_map/all_to_all | solution.py:72
  9.3 0.7 fusion.10
  10.0 0.8 copy.65
  11.4 0.7 convert_bitcast_fusion
  12.1 0.7 convert_element_type.62
  12.8 0.7 convert_element_type.68
  13.5 0.1 copy.71
  13.6 0.1 copy.73
  13.7 0.1 copy.72
  13.8 0.8 copy.64
  14.8 0.1 copy.67
  15.1 0.8 copy.68
  16.1 0.1 copy.74
  16.2 0.1 copy.70
  16.4 0.2 concatenate.12
  16.6 5.9 %collective-permute-start.1 = (bf16[40,128]{1,0:T(8,128)(2,1)S(1)}, bf16[40,128]{1,0:T(8,128)(2,1)S(1)}, u32[]{:S(2)}, u32[]{:S(2)}) collective-permute-start(bf16[40,128]{1,0:T(8,128)(2,1)S(1)} %pad_maximum_fusion.1), channel_id=1, source_target_pairs={{0,15},{1,2},{2,1},{3,4},{4,3},{5,6},{6,5},{7,8},{8,7},{9,10},{10,... | collective-permute-start | bytes 30728 | tf_op jit(solution)/shard_map/ppermute | solution.py:78
  22.6 2.3 %collective-permute-start.2 = (bf16[16,128]{1,0:T(8,128)(2,1)S(1)}, bf16[16,128]{1,0:T(8,128)(2,1)S(1)}, u32[]{:S(2)}, u32[]{:S(2)}) collective-permute-start(bf16[16,128]{1,0:T(8,128)(2,1)S(1)} %slice.57), channel_id=1, source_target_pairs={{0,14},{1,15},{2,0},{3,1},{4,2},{5,3},{6,4},{7,5},{8,6},{9,7},{10,... | collective-permute-start | bytes 12296 | tf_op jit(solution)/shard_map/ppermute | solution.py:516
  24.9 1.0 collective-permute-done.1
  25.9 0.3 collective-permute-done.2
  26.3 0.8 broadcast_in_dim.2
  27.1 13.5 %all-to-all-start.1 = ((bf16[16,88,128]{2,1,0:T(8,128)(2,1)}), bf16[16,88,128]{2,1,0:T(8,128)(2,1)S(1)}, u32[]{:S(2)}, u32[]{:S(2)}) async-start(bf16[16,88,128]{2,1,0:T(8,128)(2,1)} %broadcast_in_dim.2), calls=%async_computation.1 | async-start | bytes 720896 | tf_op jit(solution)/shard_map/all_to_all | solution.py:72
  40.6 0.2 multiply_add_fusion
  40.7 0.2 reshape.100
  40.9 0.1 reshape.88
  41.1 10.3 %all-to-all-done.1.refs_0_ = bf16[16,88,128]{2,1,0:T(8,128)(2,1)S(1)} async-done(((bf16[16,88,128]{2,1,0:T(8,128)(2,1)}), bf16[16,88,128]{2,1,0:T(8,128)(2,1)S(1)}, u32[]{:S(2)}, u32[]{:S(2)}) %all-to-all-start.1) | async-done | bytes 360480 | tf_op jit(solution)/shard_map/all_to_all | solution.py:72
  51.4 12.0 %forward.1 = (f32[256,128]{1,0:T(8,128)}, f32[128,1024]{1,0:T(8,128)}, f32[128,1024]{1,0:T(8,128)}, bf16[128,1024]{1,0:T(8,128)(2,1)}, f32[128,1024]{1,0:T(8,128...) custom-call(bf16[16,88,128]{2,1,0:T(8,128)(2,1)S(1)} %all-to-all-don, ...), custom_call_target="tpu_custom_call" | custom-call | tf_op jit(solution)/shard_map/forward/pallas_call | solution.py:434
  63.4 5.2 %all-to-all-start.2 = ((f32[16,16,128]{2,1,0:T(8,128)}), f32[16,16,128]{2,1,0:T(8,128)S(1)}, u32[]{:S(2)}, u32[]{:S(2)}) async-start(f32[16,16,128]{2,1,0:T(8,128)} %bitcast.4), calls=%async_computation.2 | async-start | bytes 262144 | tf_op jit(solution)/shard_map/all_to_all | solution.py:72
  68.7 0.4 fusion.1.refs_4_.refs_8_
  69.1 6.5 %all-to-all-done.2.refs_0_ = f32[16,16,128]{2,1,0:T(8,128)S(1)} async-done(((f32[16,16,128]{2,1,0:T(8,128)}), f32[16,16,128]{2,1,0:T(8,128)S(1)}, u32[]{:S(2)}, u32[]{:S(2)}) %all-to-all-start.2) | async-done | bytes 131104 | tf_op jit(solution)/shard_map/all_to_all | solution.py:72
  75.6 0.9 loss.1
  76.5 5.4 %all-to-all-start.3 = ((bf16[16,16,128]{2,1,0:T(8,128)(2,1)}), bf16[16,16,128]{2,1,0:T(8,128)(2,1)S(1)}, u32[]{:S(2)}, u32[]{:S(2)}) async-start(bf16[16,16,128]{2,1,0:T(8,128)(2,1)} %loss.1), calls=%async_computation.3 | async-start | bytes 131072 | tf_op jit(solution)/shard_map/all_to_all | solution.py:72
  81.9 2.5 %fusion.3.refs_3_ = bf16[1024,128]{1,0:T(8,128)(2,1)} fusion(bf16[128,1024]{1,0:T(8,128)(2,1)} %refs_3_.1, s32[1024]{0:T(1024)S(1)} %reshape.100), kind=kOutput, calls=%fused_computation.5 | convolution fusion | flops 269615104 | bytes 528384 | tf_op jit(solution)/shard_map/dot_general | solution.py:52
  84.4 4.2 %all-to-all-done.3 = bf16[16,16,128]{2,1,0:T(8,128)(2,1)S(1)} async-done(((bf16[16,16,128]{2,1,0:T(8,128)(2,1)}), bf16[16,16,128]{2,1,0:T(8,128)(2,1)S(1)}, u32[]{:S(2)}, u32[]{:S(2)}) %all-to-all-start.3) | async-done | bytes 65568 | tf_op jit(solution)/shard_map/all_to_all | solution.py:72
  88.6 0.1 copy.75
  88.8 0.9 copy-done.5
  89.8 3.9 %prepare.1 = (f32[1024,512]{1,0:T(8,128)}, bf16[1024,128]{1,0:T(8,128)(2,1)}, bf16[1024,128]{1,0:T(8,128)(2,1)}, bf16[128,512]{1,0:T(8,128)(2,1)}, bf16[6,256,12...) custom-call(f32[384,128]{1,0:T(8,128)S(1)} %copy-done.1, f32[128,384]{1,0:T(8,128)S(1)} %bitcast.21, ...), custom_call_target="tpu_custom_call" | custom-call | tf_op jit(solution)/shard_map/prepare/pallas_call | solution.py:434
  93.7 5.5 %collective-permute-done.4.refs_2_ = bf16[256,128]{1,0:T(8,128)(2,1)} collective-permute-done((bf16[256,128]{1,0:T(8,128)(2,1)S(1)}, bf16[256,128]{1,0:T(8,128)(2,1)}, u32[]{:S(2)}, u32[]{:S(2)}) %collective-permute-start.4) | collective-permute-done | bytes 65568 | tf_op jit(solution)/shard_map/ppermute | solution.py:78
  99.1 15.8 %backward.1 = (bf16[512,2432]{1,0:T(8,128)(2,1)S(1)}, bf16[512,2432]{1,0:T(8,128)(2,1)S(1)}) custom-call(bf16[256,128]{1,0:T(8,128)(2,1)} %collective-permute-done.3.refs_0_, bf16[256,128]{1,0:T(8,128)(2,1)S(1)} %bitcast.24, bf16[256,128]{1,0:T(8,128)(2,1)} %collective-permute-done.4.refs_2_, bf16[512,128]{1,0:T(8,128)(2,1)S(1)} %copy-done.2, ...), custom_call_target="tpu_custom_call" | custom-call | tf_op jit(solution)/shard_map/backward/pallas_call | solution.py:434
  115.0 4.7 %collective-permute-done.5 = bf16[512,2432]{1,0:T(8,128)(2,1)S(1)} collective-permute-done((bf16[512,2432]{1,0:T(8,128)(2,1)S(1)}, bf16[512,2432]{1,0:T(8,128)(2,1)S(1)}, u32[]{:S(2)}, u32[]{:S(2)}) %collective-permute-start.5) | collective-permute-done | bytes 2490400 | tf_op jit(solution)/shard_map/ppermute | solution.py:637
  119.7 0.7 add_convert_fusion
  120.4 35.5 %all_to_all.30 = bf16[16,32,2432]{2,1,0:T(8,128)(2,1)S(1)} all-to-all(bf16[16,32,2432]{2,1,0:T(8,128)(2,1)S(1)} %bitcast.25), channel_id=1, replica_groups=mesh['zl'=4,'x'=4,'zh'=2,'y'=4,'core'=2] {'x','y'}, dimensions={0} | all-to-all | bytes 4980736 | tf_op jit(solution)/shard_map/all_to_all | solution.py:72
  155.9 0.4 reduce_sum.21
  156.3 12.6 %all_to_all.31 = bf16[8,4,2432]{2,1,0:T(4,128)(2,1)S(1)} all-to-all(bf16[8,4,2432]{2,1,0:T(4,128)(2,1)S(1)} %reshape.93), channel_id=1, replica_groups=mesh['zl'=4,'x'=4,'zh'=2,'y'=4,'core'=2] {'zl','zh'}, dimensions={0} | all-to-all | bytes 311296 | tf_op jit(solution)/shard_map/all_to_all | solution.py:72
  169.0 0.1 convert_reduce_fusion
  169.1 0.6 slice_bitcast_fusion.2
  169.6 0.6 fusion.6
  170.2 0.6 slice_bitcast_fusion
  170.8 0.6 slice.67
  (49 shorter events, 0.8 us)
Async XLA Ops:
  0.6 40.3 %copy-start.7 = (bf16[16,1024]{1,0:T(8,128)(2,1)S(1)}, bf16[16,1024]{1,0:T(8,128)(2,1)}, u32[]{:S(2)}) copy-start(bf16[16,1024]{1,0:T(8,128)(2,1)} %param.16) | copy-start | bytes 98308
  0.6 50.8 %copy-start.6 = (bf16[128,1024]{1,0:T(8,128)(2,1)S(1)}, bf16[128,1024]{1,0:T(8,128)(2,1)}, u32[]{:S(2)}) copy-start(bf16[128,1024]{1,0:T(8,128)(2,1)} %refs_3_.1) | copy-start | bytes 786436
  0.7 15.9 %all-to-all-start = ((bf16[16,16,256]{2,1,0:T(8,128)(2,1)}), bf16[16,16,256]{2,1,0:T(8,128)(2,1)S(1)}, u32[]{:S(2)}, u32[]{:S(2)}) async-start(bf16[16,16,256]{2,1,0:T(8,128)(2,1)} %bitcast.26), calls=%async_computation | async-start | bytes 262144 | tf_op jit(solution)/shard_map/all_to_all | solution.py:72
  16.6 9.2 %collective-permute-start.1 = (bf16[40,128]{1,0:T(8,128)(2,1)S(1)}, bf16[40,128]{1,0:T(8,128)(2,1)S(1)}, u32[]{:S(2)}, u32[]{:S(2)}) collective-permute-start(bf16[40,128]{1,0:T(8,128)(2,1)S(1)} %pad_maximum_fusion.1), channel_id=1, source_target_pairs={{0,15},{1,2},{2,1},{3,4},{4,3},{5,6},{6,5},{7,8},{8,7},{9,10},{10,... | collective-permute-start | bytes 30728 | tf_op jit(solution)/shard_map/ppermute | solution.py:78
  22.6 3.3 %collective-permute-start = (bf16[40,128]{1,0:T(8,128)(2,1)S(1)}, bf16[40,128]{1,0:T(8,128)(2,1)S(1)}, u32[]{:S(2)}, u32[]{:S(2)}) collective-permute-start(bf16[40,128]{1,0:T(8,128)(2,1)S(1)} %pad_maximum_fusion.1), channel_id=1, source_target_pairs={{0,1},{1,0},{2,3},{3,2},{4,5},{5,4},{6,7},{7,6},{8,9},{9,8},{10,11... | collective-permute-start | bytes 30728 | tf_op jit(solution)/shard_map/ppermute | solution.py:77
  22.6 3.7 %collective-permute-start.2 = (bf16[16,128]{1,0:T(8,128)(2,1)S(1)}, bf16[16,128]{1,0:T(8,128)(2,1)S(1)}, u32[]{:S(2)}, u32[]{:S(2)}) collective-permute-start(bf16[16,128]{1,0:T(8,128)(2,1)S(1)} %slice.57), channel_id=1, source_target_pairs={{0,14},{1,15},{2,0},{3,1},{4,2},{5,3},{6,4},{7,5},{8,6},{9,7},{10,... | collective-permute-start | bytes 12296 | tf_op jit(solution)/shard_map/ppermute | solution.py:516
  27.1 24.4 %all-to-all-start.1 = ((bf16[16,88,128]{2,1,0:T(8,128)(2,1)}), bf16[16,88,128]{2,1,0:T(8,128)(2,1)S(1)}, u32[]{:S(2)}, u32[]{:S(2)}) async-start(bf16[16,88,128]{2,1,0:T(8,128)(2,1)} %broadcast_in_dim.2), calls=%async_computation.1 | async-start | bytes 720896 | tf_op jit(solution)/shard_map/all_to_all | solution.py:72
  63.4 25.2 %copy-start.1 = (f32[384,128]{1,0:T(8,128)S(1)}, f32[384,128]{1,0:T(8,128)}, u32[]{:S(2)}) copy-start(f32[384,128]{1,0:T(8,128)} %get-tuple-element.38.refs_0_) | copy-start | bytes 589828
  63.4 12.2 %all-to-all-start.2 = ((f32[16,16,128]{2,1,0:T(8,128)}), f32[16,16,128]{2,1,0:T(8,128)S(1)}, u32[]{:S(2)}, u32[]{:S(2)}) async-start(f32[16,16,128]{2,1,0:T(8,128)} %bitcast.4), calls=%async_computation.2 | async-start | bytes 262144 | tf_op jit(solution)/shard_map/all_to_all | solution.py:72
  68.7 20.1 %copy-start.2 = (bf16[512,128]{1,0:T(8,128)(2,1)S(1)}, bf16[512,128]{1,0:T(8,128)(2,1)}, u32[]{:S(2)}) copy-start(bf16[512,128]{1,0:T(8,128)(2,1)} %get-tuple-element.28.refs_2_.refs_3_) | copy-start | bytes 393220
  68.7 20.1 %copy-start.3 = (bf16[256,1024]{1,0:T(8,128)(2,1)S(1)}, bf16[256,1024]{1,0:T(8,128)(2,1)}, u32[]{:S(2)}) copy-start(bf16[256,1024]{1,0:T(8,128)(2,1)} %get-tuple-element.40.refs_6_) | copy-start | bytes 1572868
  68.7 20.1 %copy-start.4 = (bf16[128,1024]{1,0:T(8,128)(2,1)S(1)}, bf16[128,1024]{1,0:T(8,128)(2,1)}, u32[]{:S(2)}) copy-start(bf16[128,1024]{1,0:T(8,128)(2,1)} %get-tuple-element.39.refs_5_) | copy-start | bytes 786436
  69.1 24.5 %copy-start = (bf16[1024,1024]{1,0:T(8,128)(2,1)}, bf16[1024,1024]{1,0:T(8,128)(2,1)S(1)}, u32[]{:S(2)}) copy-start(bf16[1024,1024]{1,0:T(8,128)(2,1)S(1)} %fusion.1.refs_4_.refs_8_) | copy-start | bytes 6291460
  76.5 12.1 %all-to-all-start.3 = ((bf16[16,16,128]{2,1,0:T(8,128)(2,1)}), bf16[16,16,128]{2,1,0:T(8,128)(2,1)S(1)}, u32[]{:S(2)}, u32[]{:S(2)}) async-start(bf16[16,16,128]{2,1,0:T(8,128)(2,1)} %loss.1), calls=%async_computation.3 | async-start | bytes 131072 | tf_op jit(solution)/shard_map/all_to_all | solution.py:72
  88.6 10.5 %collective-permute-start.4 = (bf16[256,128]{1,0:T(8,128)(2,1)S(1)}, bf16[256,128]{1,0:T(8,128)(2,1)}, u32[]{:S(2)}, u32[]{:S(2)}) collective-permute-start(bf16[256,128]{1,0:T(8,128)(2,1)S(1)} %bitcast.22), channel_id=1, source_target_pairs={{0,15},{1,2},{2,1},{3,4},{4,3},{5,6},{6,5},{7,8},{8,7},{9,10},{10,... | collective-permute-start | bytes 196616 | tf_op jit(solution)/shard_map/ppermute | solution.py:78
  88.6 10.5 %collective-permute-start.3 = (bf16[256,128]{1,0:T(8,128)(2,1)S(1)}, bf16[256,128]{1,0:T(8,128)(2,1)}, u32[]{:S(2)}, u32[]{:S(2)}) collective-permute-start(bf16[256,128]{1,0:T(8,128)(2,1)S(1)} %bitcast.23), channel_id=1, source_target_pairs={{0,1},{1,0},{2,3},{3,2},{4,5},{5,4},{6,7},{7,6},{8,9},{9,8},{10,11... | collective-permute-start | bytes 196616 | tf_op jit(solution)/shard_map/ppermute | solution.py:77
  88.8 1.0 copy-start.5
  114.9 4.8 %collective-permute-start.5 = (bf16[512,2432]{1,0:T(8,128)(2,1)S(1)}, bf16[512,2432]{1,0:T(8,128)(2,1)S(1)}, u32[]{:S(2)}, u32[]{:S(2)}) collective-permute-start(bf16[512,2432]{1,0:T(8,128)(2,1)S(1)} %get-tuple-element.48), channel_id=1, source_target_pairs={{0,1},{1,0},{2,3},{3,2},{4,5},{5,4},{6,7},{7,6},{8,9},{9,8},{10,11... | collective-permute-start | bytes 7471112 | tf_op jit(solution)/shard_map/ppermute | solution.py:637

commit v5 on v4

--- a/solution.py
+++ b/solution.py
@@ -57,17 +57,6 @@
 NT = ((1,), (1,))
 
 
-def two_terms(values):
-    high = lax.reduce_precision(values, 8, 7)
-    return high.astype(BF16), (values - high).astype(BF16)
-
-
-def three_terms(values):
-    high = lax.reduce_precision(values, 8, 7)
-    middle = lax.reduce_precision(values - high, 8, 7)
-    return [high.astype(BF16), middle.astype(BF16), (values - high - middle).astype(BF16)]
-
-
 def swap(values, axes):
     return lax.all_to_all(values, axes, split_axis=0, concat_axis=0, tiled=True)
 
@@ -119,6 +108,49 @@
     point = lax.broadcasted_iota(jnp.int32, shape, point_dim)
     node = lax.broadcasted_iota(jnp.int32, shape, 1 - point_dim)
     return jnp.where(point == 2 * node + parity, 1.0, 0.0).astype(BF16)
+
+
+def split3(values):
+    high = values.astype(BF16)
+    rest = values - high.astype(F32)
+    middle = rest.astype(BF16)
+    return high, middle, (rest - middle.astype(F32)).astype(BF16)
+
+
+def pack_kernel(need, push, member_ref, off_ref, w_ref, win_ref, jit_ref, doff_ref, dw_ref, *refs):
+    out_ref, all_ref = refs
+    k_enc, k_dec = w_ref.shape[0], dw_ref.shape[0]
+    noise = jit_ref.shape[0]
+    all_ref[...] = jnp.zeros_like(all_ref)
+    all_ref[:k_enc, :] = off_ref[...].astype(F32)
+    for i, term in enumerate(split3(w_ref[...])):
+        all_ref[k_enc * (i + 1) : k_enc * (i + 2), :] = term.astype(F32)
+    at = 4 * k_enc
+    all_ref[at : at + 1, :] = win_ref[...].astype(F32)
+    at += 1
+    tables = (doff_ref[...].astype(F32).astype(BF16),) + split3(dw_ref[...])
+    for i, table in enumerate(tables):
+        for parity in range(POINTS // NODES):
+            start = at + (i * (POINTS // NODES) + parity) * k_dec
+            place = interleave(parity, (POINTS, NODES), 0)
+            all_ref[start : start + k_dec, :] = dot(table, place, NN)
+    width = all_ref.shape[0]
+    each = width // noise
+    rows = NODES // each
+    jitter = jnp.zeros((rows, width), F32)
+    target = lax.broadcasted_iota(jnp.int32, (rows, NODES), 0)
+    node = lax.broadcasted_iota(jnp.int32, (rows, NODES), 1)
+    source = lax.broadcasted_iota(jnp.int32, (noise, width), 0)
+    lane = lax.broadcasted_iota(jnp.int32, (noise, width), 1)
+    for b in range(each):
+        pick = jnp.where(node == target * each + b, 1.0, 0.0).astype(BF16)
+        shift = jnp.where(lane == source + b * noise, 1.0, 0.0).astype(BF16)
+        jitter = jitter + dot(dot(pick, jit_ref[...], NT).astype(BF16), shift, NN)
+    out_ref[:rows, :] = jitter.astype(BF16)
+    share = out_ref.shape[0] - rows
+    row = lax.broadcasted_iota(jnp.int32, (share, NODES), 0) + member_ref[0] * share
+    pick = jnp.where(row == lax.broadcasted_iota(jnp.int32, (share, NODES), 1), 1.0, 0.0)
+    out_ref[rows:, :] = dot(pick.astype(BF16), all_ref[...].astype(BF16), NT).astype(BF16)
 
 
 def forward_kernel(k_enc, k_dec, need, push, *refs):
@@ -245,10 +277,12 @@
     facts_ref, turned_ref, x_ref, wet_ref, order_ref, normed_ref, dnorm_ref = refs[:7]
     slope_ref, nt_ref, dt_ref, sh_ref, ah_ref, al_ref = refs[7:]
     quarter = order_ref.shape[0] // 4
+    need(2)
     for r in range(4):
         rows = slice(r * quarter, (r + 1) * quarter)
         slope_ref[rows, :] = silu_slope(dot(wet_ref[rows, :], x_ref[...], NT))
     push(0)
+    need(4, 5, 6, 0)
     for r in range(4):
         rows = slice(r * quarter, (r + 1) * quarter)
         nt_ref[rows, :] = dot(order_ref[rows, :], normed_ref[...], NT).astype(BF16)
@@ -480,30 +514,44 @@
     k_dec = dec_offset.shape[1]
     inv_root = HEAD_DIM ** (-0.5)
 
+    zl, x = (lax.axis_size(a) for a in MEMBER)
+    zh, y, core = (lax.axis_size(a) for a in GRID)
+    rows = width // (members * shards)
+    order = jnp.arange(width, dtype=jnp.int32).reshape(core, x, y, zl, zh, rows)
+    c_i, x_i, y_i, zl_i, zh_i, r_i = (
+        lax.broadcasted_iota(jnp.int32, order.shape, d) for d in range(6)
+    )
+    c_i = c_i ^ lax.axis_index("core")
+    target = ((((zl_i * x + x_i) * zh + zh_i) * y + y_i) * core + c_i) * rows + r_i
+    target = target.reshape(width, 1)
+    reorder = (lax.broadcasted_iota(jnp.int32, (width, width), 1) == target).astype(BF16)
+    w_enc_turned = dot(reorder, w_enc, NT).astype(BF16)
+
     pieces = swap(slabs[0].reshape(members, sub, 2 * channels), MEMBER)
     piece = lax.dynamic_index_in_dim(pieces, loader[0], 0, keepdims=False)
     truth = piece[:, channels:].astype(F32)
 
-    packed = jnp.concatenate(
-        [enc_offset.astype(BF16)]
-        + three_terms(enc_weight)
-        + [window_offset[:, None].astype(BF16)]
-        + [dec_offset.reshape(nodes, per_node * k_dec).astype(BF16)]
-        + three_terms(unpacker_arc_scales.reshape(nodes, per_node * k_dec)),
-        axis=1,
-    )
-    packed = jnp.pad(packed, ((0, 0), (0, channels - packed.shape[1])))
     share = nodes // members
     member = lax.axis_index(MEMBER)
     jitter_rows = nodes * noise // channels
-    chunk = jnp.concatenate(
-        [
-            piece[:, :channels],
-            hidden_jitter[0].reshape(jitter_rows, channels),
-            lax.dynamic_slice_in_dim(packed, member * share, share, 0),
-        ],
-        axis=0,
-    )
+    (packed,) = call(
+        pack_kernel,
+        (
+            member.astype(jnp.int32).reshape(1),
+            enc_offset.T,
+            enc_weight.T,
+            window_offset.reshape(1, nodes),
+            hidden_jitter[0].T,
+            dec_offset.T,
+            unpacker_arc_scales.T,
+        ),
+        (),
+        [((jitter_rows + share, channels), BF16)],
+        (),
+        [((channels, nodes), F32)],
+        "pack",
+    )
+    chunk = jnp.concatenate([piece[:, :channels], packed], axis=0)
     near, beyond = exchanged(chunk)
     odd = lax.axis_index("core") == 1
     low, mid, high = jnp.where(odd, near, beyond), chunk, jnp.where(odd, beyond, near)
@@ -518,6 +566,7 @@
         [low[:sub], mid[:sub], high[:sub], far, low[at:], mid[at:], high[at:]], axis=0
     )
     got = swap(jnp.broadcast_to(payload[None], (members,) + payload.shape), MEMBER)
+    got, reorder, w_enc_turned = lax.optimization_barrier((got, reorder, w_enc_turned))
     jitter_all = jnp.concatenate([low[sub:at], mid[sub:at], high[sub:at]], axis=0)
     jitter_all = jnp.pad(jitter_all.reshape(3 * nodes, noise), ((0, 0), (0, channels - noise)))
     w_noise = jnp.pad(w_noise, ((0, channels - noise), (0, 0)))
@@ -552,37 +601,11 @@
     )
 
     cells = swap(forecast.reshape(members, sub, channels), MEMBER)
-    loss_scale = float(members * points * shards * channels) ** (-0.5)
-    (sensitivity,) = call(
-        functools.partial(loss_kernel, loss_scale),
-        (cells, truth),
-        (),
-        [((members, sub, channels), BF16)],
-        (),
-        [],
-        "loss",
-    )
-    grad_forecast = swap(sensitivity, MEMBER).reshape(points, channels)
-    grad_near, grad_beyond = exchanged(grad_forecast)
-
-    zl, x = (lax.axis_size(a) for a in MEMBER)
-    zh, y, core = (lax.axis_size(a) for a in GRID)
-    rows = width // (members * shards)
-    order = jnp.arange(width, dtype=jnp.int32).reshape(core, x, y, zl, zh, rows)
-    c_i, x_i, y_i, zl_i, zh_i, r_i = (
-        lax.broadcasted_iota(jnp.int32, order.shape, d) for d in range(6)
-    )
-    c_i = c_i ^ lax.axis_index("core")
-    target = ((((zl_i * x + x_i) * zh + zh_i) * y + y_i) * core + c_i) * rows + r_i
-    target = target.reshape(width, 1)
-    reorder = (lax.broadcasted_iota(jnp.int32, (width, width), 1) == target).astype(BF16)
-    w_enc_turned = dot(reorder, w_enc, NT).astype(BF16)
-    lanes = 4 * attn + 3 * channels
     pooled, state0, normed, raw, query, key, value, prob, attended, state1, dnorm, facts, near = saved
     prepared = call(
         functools.partial(prepare_kernel, k_enc, k_dec),
         (facts, facts.T, near, w_enc_turned, reorder, normed, dnorm),
-        (),
+        (2, 4, 5, 6, 0),
         [
             ((width, points + 2 * RIM_G), F32),
             ((width, nodes), BF16),
@@ -595,6 +618,21 @@
         [],
         "prepare",
     )
+    cells, *prepared = lax.optimization_barrier((cells, *prepared))
+    loss_scale = float(members * points * shards * channels) ** (-0.5)
+    (sensitivity,) = call(
+        functools.partial(loss_kernel, loss_scale),
+        (cells, truth),
+        (),
+        [((members, sub, channels), BF16)],
+        (),
+        [],
+        "loss",
+    )
+    grad_forecast = swap(sensitivity, MEMBER).reshape(points, channels)
+    grad_near, grad_beyond = exchanged(grad_forecast)
+
+    lanes = 4 * attn + 3 * channels
     kept, sent = call(
         backward_kernel,
         (

time: 172 us -> 168 us (0.977)
  blocking collectives: 48.1 us -> 59.6 us
  starting transfers between devices: 41.1 us -> 33.8 us
  waiting for transfers between devices: 32.5 us -> 25.4 us
    all_to_all x4 -> x3, waiting for transfers between devices: 21 us -> 9.03 us  [swap(): return lax.all_to_all(values, axes, split_axis=0, concat_axis=0, tiled=True)]
    all_to_all x2 -> x3, blocking collectives: 48.1 us -> 59.6 us  [swap(): return lax.all_to_all(values, axes, split_axis=0, concat_axis=0, tiled=True)]
    all_to_all x4 -> x3, starting transfers between devices: 32.8 us -> 25.6 us  [swap(): return lax.all_to_all(values, axes, split_axis=0, concat_axis=0, tiled=True)]
    ppermute x2, waiting for transfers between devices: 6.42 us -> 11.3 us  [exchanged(): lax.ppermute(values, GRID, [(i, (i + 1 if i % 2 else i - 1) % count) for...]
    convert_element_type x5 -> x0, other arithmetic: 2.08 us -> none  [the longest x1 0.69 us: per_device(): enc_offset.astype(BF16)]
    unnamed x22 -> x19, local copies, waits for them, and re-layouts: 3.41 us -> 4.11 us
    pallas_call x4 -> x5, Pallas kernels: 32.6 us -> 32.3 us  [call(): pl.pallas_call(body, out_shape=[(pltpu.HBM if o in pushed and (not INTERP...]
  transfers between devices with their start and end apart: 10 -> 9, of which waited for: 7 -> 7; matrix products, arithmetic and copies ran while one was open for 6% -> 4% of each run, Pallas kernels for 2% -> 3%
where the time goes in v5:
time: 168 us; the launch traced here: 167 us
  blocking collectives  59.6 us (35%)
  starting transfers between devices  33.8 us (20%)
  Pallas kernels  32.3 us (19%)
  waiting for transfers between devices  25.4 us (15%)
  local copies, waits for them, and re-layouts  9.52 us (6%)
  other arithmetic  3.07 us (2%)
  matrix products  1.78 us (1%)
    all_to_all x3, blocking collectives, swap(): return lax.all_to_all(values, axes, split_axis=0, concat_axis=0, tiled=True)  59.6 us
    pallas_call x5, Pallas kernels, call(): pl.pallas_call(body, out_shape=[(pltpu.HBM if o in pushed and (not INTERP...  32.3 us
    all_to_all x3, starting transfers between devices, swap(): return lax.all_to_all(values, axes, split_axis=0, concat_axis=0, tiled=True)  25.6 us
    ppermute x2, waiting for transfers between devices, exchanged(): lax.ppermute(values, GRID, [(i, (i + 1 if i % 2 else i - 1) % count) for...  11.3 us
    all_to_all x3, waiting for transfers between devices, swap(): return lax.all_to_all(values, axes, split_axis=0, concat_axis=0, tiled=True)  9.03 us
    ppermute x2, starting transfers between devices, exchanged(): lax.ppermute(values, GRID, [(i, (i + 1 if i % 2 else i - 1) % count) for...  4.97 us
    ppermute x1, waiting for transfers between devices, per_device(): lax.ppermute(sent, 'core', [(0, 1), (1, 0)]).astype(F32)  4.71 us
    unnamed x19, local copies, waits for them, and re-layouts  4.11 us
  transfers between devices with their start and end apart: 9, of which 7 were waited for; matrix products, arithmetic and copies ran while one was open for 4% of the time, Pallas kernels for 3%

profile of v5, /device:TPU:32, one launch (start us, length us, event | category | flops | bytes accessed | tf_op | source)
XLA Modules:
  0.0 167.1 jit_solution(3466123894807191367)
XLA Ops:
  0.6 8.5 %all-to-all-start = ((bf16[16,16,256]{2,1,0:T(8,128)(2,1)}), bf16[16,16,256]{2,1,0:T(8,128)(2,1)S(1)}, u32[]{:S(2)}, u32[]{:S(2)}) async-start(bf16[16,16,256]{2,1,0:T(8,128)(2,1)} %bitcast.39), calls=%async_computation | async-start | bytes 262144 | tf_op jit(solution)/shard_map/all_to_all | solution.py:61
  9.8 0.0 copy-start.2
  9.8 0.7 copy-done.2
  10.5 0.7 copy-done.3
  11.2 0.7 copy-done.4
  11.8 0.7 copy-done.5
  12.5 0.7 copy-done.6
  13.2 0.7 copy-done.7
  13.9 0.4 pack.1
  14.3 1.8 %all-to-all-done = bf16[16,16,256]{2,1,0:T(8,128)(2,1)S(1)} async-done(((bf16[16,16,256]{2,1,0:T(8,128)(2,1)}), bf16[16,16,256]{2,1,0:T(8,128)(2,1)S(1)}, u32[]{:S(2)}, u32[]{:S(2)}) %all-to-all-start) | async-done | bytes 131104 | tf_op jit(solution)/shard_map/all_to_all | solution.py:61
  16.1 5.0 %collective-permute-start.1 = (bf16[40,128]{1,0:T(8,128)(2,1)S(1)}, bf16[40,128]{1,0:T(8,128)(2,1)S(1)}, u32[]{:S(2)}, u32[]{:S(2)}) collective-permute-start(bf16[40,128]{1,0:T(8,128)(2,1)S(1)} %pad_maximum_fusion.1), channel_id=1, source_target_pairs={{0,15},{1,2},{2,1},{3,4},{4,3},{5,6},{6,5},{7,8},{8,7},{9,10},{10,... | collective-permute-start | bytes 30728 | tf_op jit(solution)/shard_map/ppermute | solution.py:67
  21.0 0.0 collective-permute-start
  21.0 3.2 %collective-permute-start.2 = (bf16[16,128]{1,0:T(8,128)(2,1)S(1)}, bf16[16,128]{1,0:T(8,128)(2,1)S(1)}, u32[]{:S(2)}, u32[]{:S(2)}) collective-permute-start(bf16[16,128]{1,0:T(8,128)(2,1)S(1)} %slice.65), channel_id=1, source_target_pairs={{0,14},{1,15},{2,0},{3,1},{4,2},{5,3},{6,4},{7,5},{8,6},{9,7},{10,... | collective-permute-start | bytes 12296 | tf_op jit(solution)/shard_map/ppermute | solution.py:564
  24.2 1.0 collective-permute-done.1
  25.2 0.0 collective-permute-done
  25.2 0.3 collective-permute-done.2
  25.6 0.8 broadcast_in_dim.2
  26.4 11.8 %all-to-all-start.1 = ((bf16[16,88,128]{2,1,0:T(8,128)(2,1)}), bf16[16,88,128]{2,1,0:T(8,128)(2,1)S(1)}, u32[]{:S(2)}, u32[]{:S(2)}) async-start(bf16[16,88,128]{2,1,0:T(8,128)(2,1)} %broadcast_in_dim.2), calls=%async_computation.1 | async-start | bytes 720896 | tf_op jit(solution)/shard_map/all_to_all | solution.py:61
  38.2 0.1 multiply_add_fusion
  38.3 0.0 copy-start.1
  38.4 0.2 reshape.101
  38.6 0.8 pad.9.refs_2_
  39.3 1.8 %fusion.3.refs_3_ = bf16[1024,128]{1,0:T(8,128)(2,1)S(1)} fusion(bf16[128,1024]{1,0:T(8,128)(2,1)} %refs_3_.1, s32[1024]{0:T(1024)S(1)} %reshape.101), kind=kOutput, calls=%fused_computation.5 | convolution fusion | flops 269615104 | bytes 528384 | tf_op jit(solution)/shard_map/dot_general | solution.py:52
  41.1 1.7 %fusion.1.refs_4_.refs_8_ = bf16[1024,1024]{1,0:T(8,128)(2,1)} fusion(s32[1024]{0:T(1024)S(1)} %reshape.101), kind=kLoop, calls=%fused_computation.3 | loop fusion | flops 2097152 | bytes 2101248 | tf_op jit(solution)/shard_map/convert_element_type | solution.py:527
  42.9 0.1 reshape.89
  43.0 6.1 %all-to-all-done.1.refs_0_ = bf16[16,88,128]{2,1,0:T(8,128)(2,1)S(1)} async-done(((bf16[16,88,128]{2,1,0:T(8,128)(2,1)}), bf16[16,88,128]{2,1,0:T(8,128)(2,1)S(1)}, u32[]{:S(2)}, u32[]{:S(2)}) %all-to-all-start.1) | async-done | bytes 360480 | tf_op jit(solution)/shard_map/all_to_all | solution.py:61
  49.1 12.1 %forward.1 = (f32[256,128]{1,0:T(8,128)}, f32[128,1024]{1,0:T(8,128)}, f32[128,1024]{1,0:T(8,128)}, bf16[128,1024]{1,0:T(8,128)(2,1)}, f32[128,1024]{1,0:T(8,128...) custom-call(bf16[16,88,128]{2,1,0:T(8,128)(2,1)S(1)} %all-to-all-don, ...), custom_call_target="tpu_custom_call" | custom-call | tf_op jit(solution)/shard_map/forward/pallas_call | solution.py:468
  61.2 5.3 %all-to-all-start.2 = ((f32[16,16,128]{2,1,0:T(8,128)}), f32[16,16,128]{2,1,0:T(8,128)S(1)}, u32[]{:S(2)}, u32[]{:S(2)}) async-start(f32[16,16,128]{2,1,0:T(8,128)} %bitcast.11), calls=%async_computation.2 | async-start | bytes 262144 | tf_op jit(solution)/shard_map/all_to_all | solution.py:61
  66.5 1.1 copy.25
  67.5 4.7 %prepare.1 = (f32[1024,512]{1,0:T(8,128)}, bf16[1024,128]{1,0:T(8,128)(2,1)}, bf16[1024,128]{1,0:T(8,128)(2,1)}, bf16[128,512]{1,0:T(8,128)(2,1)}, bf16[6,256,12...) custom-call(f32[384,128]{1,0:T(8,128)} %get-tuple-element.39.refs_0_, f32[128,384]{1,0:T(8,128)S(1)} %bitcast.28, ...), custom_call_target="tpu_custom_call" | custom-call | tf_op jit(solution)/shard_map/prepare/pallas_call | solution.py:468
  72.2 1.2 all-to-all-done.2.refs_0_
  73.4 0.3 loss.1
  73.7 12.8 %all_to_all.30 = bf16[16,16,128]{2,1,0:T(8,128)(2,1)S(1)} all-to-all(bf16[16,16,128]{2,1,0:T(8,128)(2,1)S(1)} %loss.1), channel_id=1, replica_groups=mesh['zl'=4,'x'=4,'zh'=2,'y'=4,'core'=2] {'zl','x'}, dimensions={0} | all-to-all | bytes 131072 | tf_op jit(solution)/shard_map/all_to_all | solution.py:61
  86.4 0.0 collective-permute-start.4
  86.5 10.4 %collective-permute-done.4.refs_2_ = bf16[256,128]{1,0:T(8,128)(2,1)S(1)} collective-permute-done((bf16[256,128]{1,0:T(8,128)(2,1)S(1)}, bf16[256,128]{1,0:T(8,128)(2,1)S(1)}, u32[]{:S(2)}, u32[]{:S(2)}) %collective-permute-start.4) | collective-permute-done | bytes 65568 | tf_op jit(solution)/shard_map/ppermute | solution.py:67
  96.9 0.0 collective-permute-done.3.refs_0_
  96.9 14.9 %backward.1 = (bf16[512,2432]{1,0:T(8,128)(2,1)S(1)}, bf16[512,2432]{1,0:T(8,128)(2,1)S(1)}) custom-call(bf16[256,128]{1,0:T(8,128)(2,1)S(1)} %collective-permute-done.3.refs_0_, bf16[256,128]{1,0:T(8,128)(2,1)S(1)} %bitcast.31, bf16[256,128]{1,0:T(8,128)(2,1)S(1)} %collective-permute-done.4.refs_2_, bf16[512,128]{1,0:T(8,128)(2,1)S(1)} %copy-done, ...), custom_call_target="tpu_custom_call" | custom-call | tf_op jit(solution)/shard_map/backward/pallas_call | solution.py:468
  111.8 0.1 collective-permute-start.5
  111.9 4.7 %collective-permute-done.5 = bf16[512,2432]{1,0:T(8,128)(2,1)S(1)} collective-permute-done((bf16[512,2432]{1,0:T(8,128)(2,1)S(1)}, bf16[512,2432]{1,0:T(8,128)(2,1)S(1)}, u32[]{:S(2)}, u32[]{:S(2)}) %collective-permute-start.5) | collective-permute-done | bytes 2490400 | tf_op jit(solution)/shard_map/ppermute | solution.py:675
  116.6 0.7 add_convert_fusion
  117.3 35.5 %all_to_all.31 = bf16[16,32,2432]{2,1,0:T(8,128)(2,1)S(1)} all-to-all(bf16[16,32,2432]{2,1,0:T(8,128)(2,1)S(1)} %bitcast.38), channel_id=1, replica_groups=mesh['zl'=4,'x'=4,'zh'=2,'y'=4,'core'=2] {'x','y'}, dimensions={0} | all-to-all | bytes 4980736 | tf_op jit(solution)/shard_map/all_to_all | solution.py:61
  152.8 0.4 reduce_sum.21
  153.2 11.4 %all_to_all.32 = bf16[8,4,2432]{2,1,0:T(4,128)(2,1)S(1)} all-to-all(bf16[8,4,2432]{2,1,0:T(4,128)(2,1)S(1)} %reshape.94), channel_id=1, replica_groups=mesh['zl'=4,'x'=4,'zh'=2,'y'=4,'core'=2] {'zl','zh'}, dimensions={0} | all-to-all | bytes 311296 | tf_op jit(solution)/shard_map/all_to_all | solution.py:61
  164.6 0.1 convert_reduce_fusion
  164.7 0.6 slice_bitcast_fusion.2
  165.3 0.6 fusion.4
  165.8 0.6 slice_bitcast_fusion
  166.4 0.6 slice.77
  (27 shorter events, 0.2 us)
Async XLA Ops:
  0.6 15.4 %all-to-all-start = ((bf16[16,16,256]{2,1,0:T(8,128)(2,1)}), bf16[16,16,256]{2,1,0:T(8,128)(2,1)S(1)}, u32[]{:S(2)}, u32[]{:S(2)}) async-start(bf16[16,16,256]{2,1,0:T(8,128)(2,1)} %bitcast.39), calls=%async_computation | async-start | bytes 262144 | tf_op jit(solution)/shard_map/all_to_all | solution.py:61
  9.8 0.7 copy-start.2
  10.5 0.7 copy-start.3
  11.2 0.7 copy-start.4
  11.8 0.7 copy-start.5
  12.5 0.7 copy-start.6
  13.2 0.7 copy-start.7
  16.1 9.1 %collective-permute-start.1 = (bf16[40,128]{1,0:T(8,128)(2,1)S(1)}, bf16[40,128]{1,0:T(8,128)(2,1)S(1)}, u32[]{:S(2)}, u32[]{:S(2)}) collective-permute-start(bf16[40,128]{1,0:T(8,128)(2,1)S(1)} %pad_maximum_fusion.1), channel_id=1, source_target_pairs={{0,15},{1,2},{2,1},{3,4},{4,3},{5,6},{6,5},{7,8},{8,7},{9,10},{10,... | collective-permute-start | bytes 30728 | tf_op jit(solution)/shard_map/ppermute | solution.py:67
  21.0 4.1 %collective-permute-start = (bf16[40,128]{1,0:T(8,128)(2,1)S(1)}, bf16[40,128]{1,0:T(8,128)(2,1)S(1)}, u32[]{:S(2)}, u32[]{:S(2)}) collective-permute-start(bf16[40,128]{1,0:T(8,128)(2,1)S(1)} %pad_maximum_fusion.1), channel_id=1, source_target_pairs={{0,1},{1,0},{2,3},{3,2},{4,5},{5,4},{6,7},{7,6},{8,9},{9,8},{10,11... | collective-permute-start | bytes 30728 | tf_op jit(solution)/shard_map/ppermute | solution.py:66
  21.0 4.5 %collective-permute-start.2 = (bf16[16,128]{1,0:T(8,128)(2,1)S(1)}, bf16[16,128]{1,0:T(8,128)(2,1)S(1)}, u32[]{:S(2)}, u32[]{:S(2)}) collective-permute-start(bf16[16,128]{1,0:T(8,128)(2,1)S(1)} %slice.65), channel_id=1, source_target_pairs={{0,14},{1,15},{2,0},{3,1},{4,2},{5,3},{6,4},{7,5},{8,6},{9,7},{10,... | collective-permute-start | bytes 12296 | tf_op jit(solution)/shard_map/ppermute | solution.py:564
  26.4 22.7 %all-to-all-start.1 = ((bf16[16,88,128]{2,1,0:T(8,128)(2,1)}), bf16[16,88,128]{2,1,0:T(8,128)(2,1)S(1)}, u32[]{:S(2)}, u32[]{:S(2)}) async-start(bf16[16,88,128]{2,1,0:T(8,128)(2,1)} %broadcast_in_dim.2), calls=%async_computation.1 | async-start | bytes 720896 | tf_op jit(solution)/shard_map/all_to_all | solution.py:61
  38.3 10.8 %copy-start.1 = (bf16[128,1024]{1,0:T(8,128)(2,1)S(1)}, bf16[128,1024]{1,0:T(8,128)(2,1)}, u32[]{:S(2)}) copy-start(bf16[128,1024]{1,0:T(8,128)(2,1)} %refs_3_.1) | copy-start | bytes 786436
  61.2 35.7 %copy-start = (bf16[512,128]{1,0:T(8,128)(2,1)S(1)}, bf16[512,128]{1,0:T(8,128)(2,1)}, u32[]{:S(2)}) copy-start(bf16[512,128]{1,0:T(8,128)(2,1)} %get-tuple-element.40.refs_2_.refs_3_) | copy-start | bytes 393220
  61.2 12.2 %all-to-all-start.2 = ((f32[16,16,128]{2,1,0:T(8,128)}), f32[16,16,128]{2,1,0:T(8,128)S(1)}, u32[]{:S(2)}, u32[]{:S(2)}) async-start(f32[16,16,128]{2,1,0:T(8,128)} %bitcast.11), calls=%async_computation.2 | async-start | bytes 262144 | tf_op jit(solution)/shard_map/all_to_all | solution.py:61
  86.4 10.4 %collective-permute-start.4 = (bf16[256,128]{1,0:T(8,128)(2,1)S(1)}, bf16[256,128]{1,0:T(8,128)(2,1)S(1)}, u32[]{:S(2)}, u32[]{:S(2)}) collective-permute-start(bf16[256,128]{1,0:T(8,128)(2,1)S(1)} %bitcast.29), channel_id=1, source_target_pairs={{0,15},{1,2},{2,1},{3,4},{4,3},{5,6},{6,5},{7,8},{8,7},{9,10},{10,... | collective-permute-start | bytes 196616 | tf_op jit(solution)/shard_map/ppermute | solution.py:67
  86.5 10.4 %collective-permute-start.3 = (bf16[256,128]{1,0:T(8,128)(2,1)S(1)}, bf16[256,128]{1,0:T(8,128)(2,1)S(1)}, u32[]{:S(2)}, u32[]{:S(2)}) collective-permute-start(bf16[256,128]{1,0:T(8,128)(2,1)S(1)} %bitcast.30), channel_id=1, source_target_pairs={{0,1},{1,0},{2,3},{3,2},{4,5},{5,4},{6,7},{7,6},{8,9},{9,8},{10,11... | collective-permute-start | bytes 196616 | tf_op jit(solution)/shard_map/ppermute | solution.py:66
  111.8 4.8 %collective-permute-start.5 = (bf16[512,2432]{1,0:T(8,128)(2,1)S(1)}, bf16[512,2432]{1,0:T(8,128)(2,1)S(1)}, u32[]{:S(2)}, u32[]{:S(2)}) collective-permute-start(bf16[512,2432]{1,0:T(8,128)(2,1)S(1)} %get-tuple-element.68), channel_id=1, source_target_pairs={{0,1},{1,0},{2,3},{3,2},{4,5},{5,4},{6,7},{7,6},{8,9},{9,8},{10,11... | collective-permute-start | bytes 7471112 | tf_op jit(solution)/shard_map/ppermute | solution.py:675

commit v6 on v5

--- a/solution.py
+++ b/solution.py
@@ -61,13 +61,10 @@
     return lax.all_to_all(values, axes, split_axis=0, concat_axis=0, tiled=True)
 
 
-def exchanged(values):
+def beyond_pair(values):
     count = lax.axis_size(GRID)
-    near = lax.ppermute(values, GRID, [(i, i ^ 1) for i in range(count)])
-    beyond = lax.ppermute(
-        values, GRID, [(i, (i + 1 if i % 2 else i - 1) % count) for i in range(count)]
-    )
-    return near, beyond
+    pairs = [(i, (i + 1 if i % 2 else i - 1) % count) for i in range(count)]
+    return lax.ppermute(values, GRID, pairs)
 
 
 def split2(values):
@@ -122,6 +119,7 @@
     k_enc, k_dec = w_ref.shape[0], dw_ref.shape[0]
     noise = jit_ref.shape[0]
     all_ref[...] = jnp.zeros_like(all_ref)
+    need(1, 2, 3, 4, 5, 6)
     all_ref[:k_enc, :] = off_ref[...].astype(F32)
     for i, term in enumerate(split3(w_ref[...])):
         all_ref[k_enc * (i + 1) : k_enc * (i + 2), :] = term.astype(F32)
@@ -308,11 +306,11 @@
 
 
 def backward_kernel(need, push, *refs):
-    (near_ref, mid_ref, beyond_ref, x_ref, jitter_ref, wq_ref, wo_ref, u_ref, order_ref) = refs[:9]
-    (pooled_ref, state0_ref, raw_ref, qn_ref, kn_ref, v_ref, prob_ref, att_ref) = refs[9:17]
-    (state1_ref, slope_ref, nt_ref, dt_ref, sh_ref, ah_ref, al_ref) = refs[17:24]
-    core_ref = refs[24]
-    kept_ref, sent_ref, grad1_ref, g1b_ref, ga_ref, gq_ref, gk_ref, gv_ref, mixed_ref = refs[25:]
+    (pair_ref, beyond_ref, x_ref, jitter_ref, wq_ref, wo_ref, u_ref, order_ref) = refs[:8]
+    (pooled_ref, state0_ref, raw_ref, qn_ref, kn_ref, v_ref, prob_ref, att_ref) = refs[8:16]
+    (state1_ref, slope_ref, nt_ref, dt_ref, sh_ref, ah_ref, al_ref) = refs[16:23]
+    core_ref = refs[23]
+    kept_ref, sent_ref, grad1_ref, g1b_ref, ga_ref, gq_ref, gk_ref, gv_ref, mixed_ref, both_ref = refs[24:]
     attn, width = wo_ref.shape
     inv_root = HEAD_DIM ** (-0.5)
     own_asked = slice(WIN, WIN + NODES)
@@ -326,19 +324,25 @@
     def turned(r, values):
         return dot(order_ref[r * quarter : (r + 1) * quarter, :], values, NT).astype(BF16)
 
-    need(22, 23)
+    need(21, 22)
     odd = core_ref[0] == 1
-    near, beyond = near_ref[...].astype(F32), beyond_ref[...].astype(F32)
-    low = jnp.where(odd, near, beyond).astype(BF16)
-    high = jnp.where(odd, beyond, near).astype(BF16)
-    grad_proj = jnp.zeros((ASKED, mid_ref.shape[1]), F32)
-    for s, part in enumerate((low, mid_ref[...], high)):
+    members, sub = pair_ref.shape[0], pair_ref.shape[2]
+    for m in range(members):
+        for c in range(2):
+            both_ref[c, m * sub : (m + 1) * sub, :] = pair_ref[m, c]
+    even, second = both_ref[0].astype(F32), both_ref[1].astype(F32)
+    beyond = beyond_ref[...].astype(F32)
+    low = jnp.where(odd, even, beyond).astype(BF16)
+    middle = jnp.where(odd, second, even).astype(BF16)
+    high = jnp.where(odd, beyond, second).astype(BF16)
+    grad_proj = jnp.zeros((ASKED, beyond_ref.shape[1]), F32)
+    for s, part in enumerate((low, middle, high)):
         for parity in range(2):
             grad = dot(interleave(parity, (NODES, POINTS), 1), part, NN).astype(BF16)
             grad_proj = grad_proj + dot(ah_ref[2 * s + parity], grad, NN)
             grad_proj = grad_proj + dot(al_ref[2 * s + parity], grad, NN)
     proj_high, proj_low = split2(grad_proj)
-    need(17, 7, 6)
+    need(16, 6, 5)
     for b in range(2):
         rows = slice(b * NODES, (b + 1) * NODES)
         state1 = state1_ref[rows, :]
@@ -347,7 +351,7 @@
         grad1_ref[rows, :] = grad
         g1b_ref[rows, :] = grad.astype(BF16)
         ga_ref[rows, :] = dot(g1b_ref[rows, :], wo_ref[...], NT).astype(BF16)
-    need(20, 8, 16)
+    need(19, 7, 15)
     for r in range(4):
         dnorm = dt_ref[r * quarter : (r + 1) * quarter, :]
         store(
@@ -357,7 +361,7 @@
         )
         store(r, 3 * attn, dot(turned(r, g1b_ref[own_asked, :]), att_ref[own_asked, :], NN))
 
-    need(12, 13, 14, 15)
+    need(11, 12, 13, 14)
     masks = head_masks()
     for pair in range(attn // 128):
         lanes = slice(pair * 128, (pair + 1) * 128)
@@ -385,7 +389,7 @@
         gk_ref[:, lanes] = grad_key * inv_root
         gv_ref[:, lanes] = grad_value
     heads = same_head(attn)
-    need(11)
+    need(10)
     for i, ref in enumerate((gq_ref, gk_ref)):
         values = raw_ref[:, i * attn : (i + 1) * attn]
         grad = ref[...]
@@ -395,7 +399,7 @@
         mixed_ref[:, i * attn : (i + 1) * attn] = grad.astype(BF16)
     mixed_ref[:, 2 * attn :] = gv_ref[...].astype(BF16)
 
-    need(5, 10, 9, 19, 18, 21)
+    need(4, 9, 8, 18, 17, 20)
     grad_normed = dot(mixed_ref[...], wq_ref[...], NT)
     state0 = state0_ref[...]
     grad0 = grad1_ref[own_asked, :] + rms_back(state0, rms_factor(state0), grad_normed)
@@ -422,7 +426,9 @@
             fair[n] = fair[n] - slope
     for m in range(members):
         first = eased_sensitivity(cells[m] - truth_ref[...]) * (scale / members)
-        out_ref[m] = (first - fair[m] * (scale / (members * (members - 1)))).astype(BF16)
+        out = (first - fair[m] * (scale / (members * (members - 1)))).astype(BF16)
+        for c in range(out_ref.shape[1]):
+            out_ref[m, c] = out
 
 
 def call(kernel, args, late, outs, pushed, scratch, name):
@@ -545,14 +551,15 @@
             dec_offset.T,
             unpacker_arc_scales.T,
         ),
-        (),
+        (1, 2, 3, 4, 5, 6),
         [((jitter_rows + share, channels), BF16)],
         (),
         [((channels, nodes), F32)],
         "pack",
     )
     chunk = jnp.concatenate([piece[:, :channels], packed], axis=0)
-    near, beyond = exchanged(chunk)
+    near = lax.ppermute(chunk, "core", [(0, 1), (1, 0)])
+    beyond = beyond_pair(chunk)
     odd = lax.axis_index("core") == 1
     low, mid, high = jnp.where(odd, near, beyond), chunk, jnp.where(odd, beyond, near)
     at = sub + jitter_rows
@@ -624,20 +631,21 @@
         functools.partial(loss_kernel, loss_scale),
         (cells, truth),
         (),
-        [((members, sub, channels), BF16)],
+        [((members, core, sub, channels), BF16)],
         (),
         [],
         "loss",
     )
-    grad_forecast = swap(sensitivity, MEMBER).reshape(points, channels)
-    grad_near, grad_beyond = exchanged(grad_forecast)
+    pair = swap(sensitivity.reshape(members * core, sub, channels), MEMBER + ("core",))
+    pair = pair.reshape(members, core, sub, channels)
+    grad_own = lax.dynamic_index_in_dim(pair, lax.axis_index("core"), 1, keepdims=False)
+    grad_beyond = beyond_pair(grad_own.reshape(points, channels))
 
     lanes = 4 * attn + 3 * channels
     kept, sent = call(
         backward_kernel,
         (
-            grad_near,
-            grad_forecast,
+            pair,
             grad_beyond,
             near,
             jitter_all[nodes : 2 * nodes],
@@ -657,7 +665,7 @@
             *prepared,
             lax.axis_index("core").astype(jnp.int32).reshape(1),
         ),
-        (22, 23, 17, 7, 6, 20, 8, 16, 12, 13, 14, 15, 11, 5, 10, 9, 19, 18, 21),
+        (21, 22, 16, 6, 5, 19, 7, 15, 11, 12, 13, 14, 10, 4, 9, 8, 18, 17, 20),
         [((width // core, lanes), BF16)] * 2,
         (),
         [
@@ -668,6 +676,7 @@
             ((nodes, attn), F32),
             ((nodes, attn), F32),
             ((nodes, 3 * attn), BF16),
+            ((core, points, channels), BF16),
         ],
         "backward",
     )

time: 168 us -> 169 us (level)
  blocking collectives: 59.6 us -> 49.1 us
  starting transfers between devices: 33.8 us -> 41.8 us
  waiting for transfers between devices: 25.4 us -> 32.3 us
  local copies, waits for them, and re-layouts: 9.52 us -> 5.47 us
    all_to_all x3 -> x4, waiting for transfers between devices: 9.03 us -> 19.7 us  [swap(): return lax.all_to_all(values, axes, split_axis=0, concat_axis=0, tiled=True)]
    all_to_all x3 -> x2, blocking collectives: 59.6 us -> 49.1 us  [swap(): return lax.all_to_all(values, axes, split_axis=0, concat_axis=0, tiled=True)]
    all_to_all x3 -> x4, starting transfers between devices: 25.6 us -> 30.4 us  [swap(): return lax.all_to_all(values, axes, split_axis=0, concat_axis=0, tiled=True)]
    unnamed x19 -> x7, local copies, waits for them, and re-layouts: 4.11 us -> 0.03 us
    ppermute x4 -> x3, waiting for transfers between devices: 11.3 us -> 7.52 us  [the longest x2 7.52 us: beyond_pair(): return lax.ppermute(values, GRID, pairs)]
    ppermute x4 -> x3, starting transfers between devices: 4.98 us -> 8.11 us  [the longest x2 8.11 us: beyond_pair(): return lax.ppermute(values, GRID, pairs)]
  transfers between devices with their start and end apart: 9 -> 9, of which waited for: 7 -> 8; matrix products, arithmetic and copies ran while one was open for 4% -> 4% of each run, Pallas kernels for 3% -> 3%
where the time goes in v6:
time: 169 us
  blocking collectives  49.1 us (29%)
  starting transfers between devices  41.8 us (25%)
  Pallas kernels  33.8 us (20%)
  waiting for transfers between devices  32.3 us (19%)
  local copies, waits for them, and re-layouts  5.47 us (3%)
  other arithmetic  3.09 us (2%)
  matrix products  1.78 us (1%)
    all_to_all x2, blocking collectives, swap(): return lax.all_to_all(values, axes, split_axis=0, concat_axis=0, tiled=True)  49.1 us
    pallas_call x5, Pallas kernels, call(): pl.pallas_call(body, out_shape=[(pltpu.HBM if o in pushed and (not INTERP...  33.8 us
    all_to_all x4, starting transfers between devices, swap(): return lax.all_to_all(values, axes, split_axis=0, concat_axis=0, tiled=True)  30.4 us
    all_to_all x4, waiting for transfers between devices, swap(): return lax.all_to_all(values, axes, split_axis=0, concat_axis=0, tiled=True)  19.7 us
    ppermute x2, starting transfers between devices, beyond_pair(): return lax.ppermute(values, GRID, pairs)  8.11 us
    ppermute x2, waiting for transfers between devices, beyond_pair(): return lax.ppermute(values, GRID, pairs)  7.52 us
    ppermute x1, waiting for transfers between devices, per_device(): lax.ppermute(sent, 'core', [(0, 1), (1, 0)]).astype(F32)  4.71 us
  transfers between devices with their start and end apart: 9, of which 8 were waited for; matrix products, arithmetic and copies ran while one was open for 4% of the time, Pallas kernels for 3%

profile of v6, /device:TPU:32, one launch (start us, length us, event | category | flops | bytes accessed | tf_op | source)
XLA Modules:
  0.0 168.7 jit_solution(9750578722244036149)
XLA Ops:
  0.6 8.5 %all-to-all-start = ((bf16[16,16,256]{2,1,0:T(8,128)(2,1)}), bf16[16,16,256]{2,1,0:T(8,128)(2,1)S(1)}, u32[]{:S(2)}, u32[]{:S(2)}) async-start(bf16[16,16,256]{2,1,0:T(8,128)(2,1)} %bitcast.34), calls=%async_computation | async-start | bytes 262144 | tf_op jit(solution)/shard_map/all_to_all | solution.py:61
  9.8 1.2 pack.1
  11.0 5.1 %all-to-all-done = bf16[16,16,256]{2,1,0:T(8,128)(2,1)S(1)} async-done(((bf16[16,16,256]{2,1,0:T(8,128)(2,1)}), bf16[16,16,256]{2,1,0:T(8,128)(2,1)S(1)}, u32[]{:S(2)}, u32[]{:S(2)}) %all-to-all-start) | async-done | bytes 131104 | tf_op jit(solution)/shard_map/all_to_all | solution.py:61
  16.1 5.0 %collective-permute-start.1 = (bf16[40,128]{1,0:T(8,128)(2,1)S(1)}, bf16[40,128]{1,0:T(8,128)(2,1)S(1)}, u32[]{:S(2)}, u32[]{:S(2)}) collective-permute-start(bf16[40,128]{1,0:T(8,128)(2,1)S(1)} %pad_maximum_fusion.1), channel_id=1, source_target_pairs={{0,15},{1,2},{2,1},{3,4},{4,3},{5,6},{6,5},{7,8},{8,7},{9,10},{10,... | collective-permute-start | bytes 30728 | tf_op jit(solution)/shard_map/ppermute | solution.py:67
  21.0 0.0 collective-permute-start
  21.0 3.2 %collective-permute-start.2 = (bf16[16,128]{1,0:T(8,128)(2,1)S(1)}, bf16[16,128]{1,0:T(8,128)(2,1)S(1)}, u32[]{:S(2)}, u32[]{:S(2)}) collective-permute-start(bf16[16,128]{1,0:T(8,128)(2,1)S(1)} %slice.65), channel_id=1, source_target_pairs={{0,14},{1,15},{2,0},{3,1},{4,2},{5,3},{6,4},{7,5},{8,6},{9,7},{10,... | collective-permute-start | bytes 12296 | tf_op jit(solution)/shard_map/ppermute | solution.py:571
  24.2 1.0 collective-permute-done.1
  25.2 0.0 collective-permute-done
  25.2 0.3 collective-permute-done.2
  25.6 0.8 broadcast_in_dim.2
  26.4 10.2 %all-to-all-start.1 = ((bf16[16,88,128]{2,1,0:T(8,128)(2,1)}), bf16[16,88,128]{2,1,0:T(8,128)(2,1)S(1)}, u32[]{:S(2)}, u32[]{:S(2)}) async-start(bf16[16,88,128]{2,1,0:T(8,128)(2,1)} %broadcast_in_dim.2), calls=%async_computation.1 | async-start | bytes 720896 | tf_op jit(solution)/shard_map/all_to_all | solution.py:61
  36.6 0.1 multiply_add_fusion
  36.8 0.0 copy-start.1
  36.8 0.2 reshape.110
  37.0 0.8 pad.9.refs_2_
  37.8 1.8 %fusion.3.refs_3_ = bf16[1024,128]{1,0:T(8,128)(2,1)S(1)} fusion(bf16[128,1024]{1,0:T(8,128)(2,1)} %refs_3_.1, s32[1024]{0:T(1024)S(1)} %reshape.110), kind=kOutput, calls=%fused_computation.5 | convolution fusion | flops 269615104 | bytes 528384 | tf_op jit(solution)/shard_map/dot_general | solution.py:52
  39.5 1.8 %fusion.1.refs_4_.refs_7_ = bf16[1024,1024]{1,0:T(8,128)(2,1)} fusion(s32[1024]{0:T(1024)S(1)} %reshape.110), kind=kLoop, calls=%fused_computation.3 | loop fusion | flops 2097152 | bytes 2101248 | tf_op jit(solution)/shard_map/convert_element_type | solution.py:533
  41.3 0.1 reshape.96
  41.5 6.1 %all-to-all-done.1.refs_0_ = bf16[16,88,128]{2,1,0:T(8,128)(2,1)S(1)} async-done(((bf16[16,88,128]{2,1,0:T(8,128)(2,1)}), bf16[16,88,128]{2,1,0:T(8,128)(2,1)S(1)}, u32[]{:S(2)}, u32[]{:S(2)}) %all-to-all-start.1) | async-done | bytes 360480 | tf_op jit(solution)/shard_map/all_to_all | solution.py:61
  47.5 0.0 copy-done.1
  47.5 12.1 %forward.1 = (f32[256,128]{1,0:T(8,128)}, f32[128,1024]{1,0:T(8,128)}, f32[128,1024]{1,0:T(8,128)}, bf16[128,1024]{1,0:T(8,128)(2,1)}, f32[128,1024]{1,0:T(8,128...) custom-call(bf16[16,88,128]{2,1,0:T(8,128)(2,1)S(1)} %all-to-all-don, ...), custom_call_target="tpu_custom_call" | custom-call | tf_op jit(solution)/shard_map/forward/pallas_call | solution.py:474
  59.6 5.1 %all-to-all-start.2 = ((f32[16,16,128]{2,1,0:T(8,128)}), f32[16,16,128]{2,1,0:T(8,128)S(1)}, u32[]{:S(2)}, u32[]{:S(2)}) async-start(f32[16,16,128]{2,1,0:T(8,128)} %bitcast.11), calls=%async_computation.2 | async-start | bytes 262144 | tf_op jit(solution)/shard_map/all_to_all | solution.py:61
  64.7 0.0 copy-start
  64.7 1.1 copy.25
  65.8 4.7 %prepare.1 = (f32[1024,512]{1,0:T(8,128)}, bf16[1024,128]{1,0:T(8,128)(2,1)}, bf16[1024,128]{1,0:T(8,128)(2,1)}, bf16[128,512]{1,0:T(8,128)(2,1)}, bf16[6,256,12...) custom-call(f32[384,128]{1,0:T(8,128)} %get-tuple-element.39.refs_0_, f32[128,384]{1,0:T(8,128)S(1)} %bitcast.32, ...), custom_call_target="tpu_custom_call" | custom-call | tf_op jit(solution)/shard_map/prepare/pallas_call | solution.py:474
  70.5 1.2 all-to-all-done.2.refs_0_
  71.7 0.9 loss.1
  72.6 6.5 %all-to-all-start.3 = ((bf16[32,16,128]{2,1,0:T(8,128)(2,1)}), bf16[32,16,128]{2,1,0:T(8,128)(2,1)S(1)}, u32[]{:S(2)}, u32[]{:S(2)}) async-start(bf16[32,16,128]{2,1,0:T(8,128)(2,1)} %bitcast.13), calls=%async_computation.3 | async-start | bytes 262144 | tf_op jit(solution)/shard_map/all_to_all | solution.py:61
  79.1 7.4 %all-to-all-done.3 = bf16[32,16,128]{2,1,0:T(8,128)(2,1)S(1)} async-done(((bf16[32,16,128]{2,1,0:T(8,128)(2,1)}), bf16[32,16,128]{2,1,0:T(8,128)(2,1)S(1)}, u32[]{:S(2)}, u32[]{:S(2)}) %all-to-all-start.3) | async-done | bytes 131104 | tf_op jit(solution)/shard_map/all_to_all | solution.py:61
  86.6 3.1 %collective-permute-start.3 = (bf16[256,128]{1,0:T(8,128)(2,1)S(1)}, bf16[256,128]{1,0:T(8,128)(2,1)S(1)}, u32[]{:S(2)}, u32[]{:S(2)}) collective-permute-start(bf16[256,128]{1,0:T(8,128)(2,1)S(1)} %bitcast.35), channel_id=1, source_target_pairs={{0,15},{1,2},{2,1},{3,4},{4,3},{5,6},{6,5},{7,8},{8,7},{9,10},{10,... | collective-permute-start | bytes 196616 | tf_op jit(solution)/shard_map/ppermute | solution.py:67
  89.7 6.6 %collective-permute-done.3.refs_1_ = bf16[256,128]{1,0:T(8,128)(2,1)S(1)} collective-permute-done((bf16[256,128]{1,0:T(8,128)(2,1)S(1)}, bf16[256,128]{1,0:T(8,128)(2,1)S(1)}, u32[]{:S(2)}, u32[]{:S(2)}) %collective-permute-start.3) | collective-permute-done | bytes 65568 | tf_op jit(solution)/shard_map/ppermute | solution.py:67
  96.3 0.0 copy-done
  96.3 14.9 %backward.1 = (bf16[512,2432]{1,0:T(8,128)(2,1)S(1)}, bf16[512,2432]{1,0:T(8,128)(2,1)S(1)}) custom-call(bf16[16,2,16,128]{3,2,1,0:T(8,128)(2,1)S(1)} %bitcast.31, bf16[256,128]{1,0:T(8,128)(2,1)S(1)} %collective-permute-done.3.refs_1_, bf16[512,128]{1,0:T(8,128)(2,1)S(1)} %copy-done, bf16[128,128]{1,0:T(8,128)(2,1)S(1)} %pad_slice_fusion.refs_3_, ...), custom_call_target="tpu_custom_call" | custom-call | tf_op jit(solution)/shard_map/backward/pallas_call | solution.py:474
  111.2 0.1 collective-permute-start.4
  111.3 4.7 %collective-permute-done.4 = bf16[512,2432]{1,0:T(8,128)(2,1)S(1)} collective-permute-done((bf16[512,2432]{1,0:T(8,128)(2,1)S(1)}, bf16[512,2432]{1,0:T(8,128)(2,1)S(1)}, u32[]{:S(2)}, u32[]{:S(2)}) %collective-permute-start.4) | collective-permute-done | bytes 2490400 | tf_op jit(solution)/shard_map/ppermute | solution.py:684
  116.0 0.7 add_convert_fusion
  116.7 37.0 %all_to_all.30 = bf16[16,32,2432]{2,1,0:T(8,128)(2,1)S(1)} all-to-all(bf16[16,32,2432]{2,1,0:T(8,128)(2,1)S(1)} %bitcast.33), channel_id=1, replica_groups=mesh['zl'=4,'x'=4,'zh'=2,'y'=4,'core'=2] {'x','y'}, dimensions={0} | all-to-all | bytes 4980736 | tf_op jit(solution)/shard_map/all_to_all | solution.py:61
  153.7 0.4 reduce_sum.21
  154.1 12.1 %all_to_all.31 = bf16[8,4,2432]{2,1,0:T(4,128)(2,1)S(1)} all-to-all(bf16[8,4,2432]{2,1,0:T(4,128)(2,1)S(1)} %reshape.103), channel_id=1, replica_groups=mesh['zl'=4,'x'=4,'zh'=2,'y'=4,'core'=2] {'zl','zh'}, dimensions={0} | all-to-all | bytes 311296 | tf_op jit(solution)/shard_map/all_to_all | solution.py:61
  166.3 0.1 convert_reduce_fusion
  166.4 0.6 slice_bitcast_fusion.2
  166.9 0.6 fusion.4
  167.5 0.6 slice_bitcast_fusion
  168.1 0.6 slice.77
  (19 shorter events, 0.2 us)
Async XLA Ops:
  0.6 15.4 %all-to-all-start = ((bf16[16,16,256]{2,1,0:T(8,128)(2,1)}), bf16[16,16,256]{2,1,0:T(8,128)(2,1)S(1)}, u32[]{:S(2)}, u32[]{:S(2)}) async-start(bf16[16,16,256]{2,1,0:T(8,128)(2,1)} %bitcast.34), calls=%async_computation | async-start | bytes 262144 | tf_op jit(solution)/shard_map/all_to_all | solution.py:61
  16.1 9.1 %collective-permute-start.1 = (bf16[40,128]{1,0:T(8,128)(2,1)S(1)}, bf16[40,128]{1,0:T(8,128)(2,1)S(1)}, u32[]{:S(2)}, u32[]{:S(2)}) collective-permute-start(bf16[40,128]{1,0:T(8,128)(2,1)S(1)} %pad_maximum_fusion.1), channel_id=1, source_target_pairs={{0,15},{1,2},{2,1},{3,4},{4,3},{5,6},{6,5},{7,8},{8,7},{9,10},{10,... | collective-permute-start | bytes 30728 | tf_op jit(solution)/shard_map/ppermute | solution.py:67
  21.0 4.1 %collective-permute-start = (bf16[40,128]{1,0:T(8,128)(2,1)S(1)}, bf16[40,128]{1,0:T(8,128)(2,1)S(1)}, u32[]{:S(2)}, u32[]{:S(2)}) collective-permute-start(bf16[40,128]{1,0:T(8,128)(2,1)S(1)} %pad_maximum_fusion.1), channel_id=1, source_target_pairs={{0,1},{1,0},{2,3},{3,2},{4,5},{5,4},{6,7},{7,6},{8,9},{9,8},{10,11... | collective-permute-start | bytes 30728 | tf_op jit(solution)/shard_map/ppermute | solution.py:561
  21.0 4.5 %collective-permute-start.2 = (bf16[16,128]{1,0:T(8,128)(2,1)S(1)}, bf16[16,128]{1,0:T(8,128)(2,1)S(1)}, u32[]{:S(2)}, u32[]{:S(2)}) collective-permute-start(bf16[16,128]{1,0:T(8,128)(2,1)S(1)} %slice.65), channel_id=1, source_target_pairs={{0,14},{1,15},{2,0},{3,1},{4,2},{5,3},{6,4},{7,5},{8,6},{9,7},{10,... | collective-permute-start | bytes 12296 | tf_op jit(solution)/shard_map/ppermute | solution.py:571
  26.4 21.1 %all-to-all-start.1 = ((bf16[16,88,128]{2,1,0:T(8,128)(2,1)}), bf16[16,88,128]{2,1,0:T(8,128)(2,1)S(1)}, u32[]{:S(2)}, u32[]{:S(2)}) async-start(bf16[16,88,128]{2,1,0:T(8,128)(2,1)} %broadcast_in_dim.2), calls=%async_computation.1 | async-start | bytes 720896 | tf_op jit(solution)/shard_map/all_to_all | solution.py:61
  36.8 10.8 %copy-start.1 = (bf16[128,1024]{1,0:T(8,128)(2,1)S(1)}, bf16[128,1024]{1,0:T(8,128)(2,1)}, u32[]{:S(2)}) copy-start(bf16[128,1024]{1,0:T(8,128)(2,1)} %refs_3_.1) | copy-start | bytes 786436
  59.6 12.0 %all-to-all-start.2 = ((f32[16,16,128]{2,1,0:T(8,128)}), f32[16,16,128]{2,1,0:T(8,128)S(1)}, u32[]{:S(2)}, u32[]{:S(2)}) async-start(f32[16,16,128]{2,1,0:T(8,128)} %bitcast.11), calls=%async_computation.2 | async-start | bytes 262144 | tf_op jit(solution)/shard_map/all_to_all | solution.py:61
  64.7 31.5 %copy-start = (bf16[512,128]{1,0:T(8,128)(2,1)S(1)}, bf16[512,128]{1,0:T(8,128)(2,1)}, u32[]{:S(2)}) copy-start(bf16[512,128]{1,0:T(8,128)(2,1)} %get-tuple-element.40.refs_2_) | copy-start | bytes 393220
  72.6 14.0 %all-to-all-start.3 = ((bf16[32,16,128]{2,1,0:T(8,128)(2,1)}), bf16[32,16,128]{2,1,0:T(8,128)(2,1)S(1)}, u32[]{:S(2)}, u32[]{:S(2)}) async-start(bf16[32,16,128]{2,1,0:T(8,128)(2,1)} %bitcast.13), calls=%async_computation.3 | async-start | bytes 262144 | tf_op jit(solution)/shard_map/all_to_all | solution.py:61
  86.6 9.7 %collective-permute-start.3 = (bf16[256,128]{1,0:T(8,128)(2,1)S(1)}, bf16[256,128]{1,0:T(8,128)(2,1)S(1)}, u32[]{:S(2)}, u32[]{:S(2)}) collective-permute-start(bf16[256,128]{1,0:T(8,128)(2,1)S(1)} %bitcast.35), channel_id=1, source_target_pairs={{0,15},{1,2},{2,1},{3,4},{4,3},{5,6},{6,5},{7,8},{8,7},{9,10},{10,... | collective-permute-start | bytes 196616 | tf_op jit(solution)/shard_map/ppermute | solution.py:67
  111.2 4.8 %collective-permute-start.4 = (bf16[512,2432]{1,0:T(8,128)(2,1)S(1)}, bf16[512,2432]{1,0:T(8,128)(2,1)S(1)}, u32[]{:S(2)}, u32[]{:S(2)}) collective-permute-start(bf16[512,2432]{1,0:T(8,128)(2,1)S(1)} %get-tuple-element.68), channel_id=1, source_target_pairs={{0,1},{1,0},{2,3},{3,2},{4,5},{5,4},{6,7},{7,6},{8,9},{9,8},{10,11... | collective-permute-start | bytes 7471112 | tf_op jit(solution)/shard_map/ppermute | solution.py:684

commit v7 on v5

--- a/solution.py
+++ b/solution.py
@@ -122,6 +122,7 @@
     k_enc, k_dec = w_ref.shape[0], dw_ref.shape[0]
     noise = jit_ref.shape[0]
     all_ref[...] = jnp.zeros_like(all_ref)
+    need(1, 2, 3, 4, 5, 6)
     all_ref[:k_enc, :] = off_ref[...].astype(F32)
     for i, term in enumerate(split3(w_ref[...])):
         all_ref[k_enc * (i + 1) : k_enc * (i + 2), :] = term.astype(F32)
@@ -411,6 +412,16 @@
         store(r, 4 * attn, dot(grad.astype(BF16), x_ref[...], NN))
 
 
+def last_kernel(need, push, total_ref, *out_refs):
+    start = 0
+    for ref in out_refs:
+        stop = start + ref.shape[1]
+        ref[...] = sum(
+            total_ref[i, :, start:stop].astype(F32) for i in range(total_ref.shape[0])
+        )
+        start = stop
+
+
 def loss_kernel(scale, need, push, cells_ref, truth_ref, out_ref):
     members = cells_ref.shape[0]
     cells = [cells_ref[m] for m in range(members)]
@@ -545,7 +556,7 @@
             dec_offset.T,
             unpacker_arc_scales.T,
         ),
-        (),
+        (1, 2, 3, 4, 5, 6),
         [((jitter_rows + share, channels), BF16)],
         (),
         [((channels, nodes), F32)],
@@ -676,16 +687,15 @@
     total = swap(total.astype(BF16).reshape(x * y, -1, lanes), ("x", "y"))
     total = jnp.sum(total.astype(F32), axis=0)
     total = swap(total.astype(BF16).reshape(zl * zh, rows, lanes), ("zl", "zh"))
-    total = jnp.sum(total.astype(F32), axis=0)
-    grad_qkv, grad_out, grad_enc, grad_map, grad_noise = (
-        total[:, start:stop]
-        for start, stop in (
-            (0, 3 * attn),
-            (3 * attn, 4 * attn),
-            (4 * attn, 4 * attn + channels),
-            (4 * attn + channels, 4 * attn + 2 * channels),
-            (4 * attn + 2 * channels, 4 * attn + 2 * channels + noise),
-        )
+    cuts = (3 * attn, attn, channels, channels, noise)
+    grad_qkv, grad_out, grad_enc, grad_map, grad_noise = call(
+        last_kernel,
+        (total,),
+        (),
+        [((rows, cut), F32) for cut in cuts],
+        (),
+        [],
+        "last",
     )
     return (grad_noise.T, grad_enc.T, grad_qkv, grad_out.T, grad_map)
 

time: 168 us -> 164 us (0.976)
  local copies, waits for them, and re-layouts: 9.52 us -> 3.05 us
  waiting for transfers between devices: 25.4 us -> 28.7 us
    unnamed x19 -> x7, local copies, waits for them, and re-layouts: 4.11 us -> 0.03 us
    all_to_all x3, waiting for transfers between devices: 9.03 us -> 12.3 us  [swap(): return lax.all_to_all(values, axes, split_axis=0, concat_axis=0, tiled=True)]
    pallas_call x5 -> x6, Pallas kernels: 32.3 us -> 33.8 us  [call(): pl.pallas_call(body, out_shape=[(pltpu.HBM if o in pushed and (not INTERP...]
  transfers between devices with their start and end apart: 9 -> 9, of which waited for: 7 -> 7; matrix products, arithmetic and copies ran while one was open for 4% -> 4% of each run, Pallas kernels for 3% -> 4%
where the time goes in v7:
time: 164 us
  blocking collectives  59.6 us (36%)
  Pallas kernels  33.8 us (21%)
  starting transfers between devices  32.2 us (20%)
  waiting for transfers between devices  28.7 us (18%)
  local copies, waits for them, and re-layouts  3.05 us (2%)
  other arithmetic  2.98 us (2%)
  matrix products  1.78 us (1%)
    all_to_all x3, blocking collectives, swap(): return lax.all_to_all(values, axes, split_axis=0, concat_axis=0, tiled=True)  59.6 us
    pallas_call x6, Pallas kernels, call(): pl.pallas_call(body, out_shape=[(pltpu.HBM if o in pushed and (not INTERP...  33.8 us
    all_to_all x3, starting transfers between devices, swap(): return lax.all_to_all(values, axes, split_axis=0, concat_axis=0, tiled=True)  24 us
    all_to_all x3, waiting for transfers between devices, swap(): return lax.all_to_all(values, axes, split_axis=0, concat_axis=0, tiled=True)  12.3 us
    ppermute x2, waiting for transfers between devices, exchanged(): lax.ppermute(values, GRID, [(i, (i + 1 if i % 2 else i - 1) % count) for...  11.3 us
    ppermute x2, starting transfers between devices, exchanged(): lax.ppermute(values, GRID, [(i, (i + 1 if i % 2 else i - 1) % count) for...  4.97 us
    ppermute x1, waiting for transfers between devices, per_device(): lax.ppermute(sent, 'core', [(0, 1), (1, 0)]).astype(F32)  4.71 us
  transfers between devices with their start and end apart: 9, of which 7 were waited for; matrix products, arithmetic and copies ran while one was open for 4% of the time, Pallas kernels for 4%

profile of v7, /device:TPU:32, one launch (start us, length us, event | category | flops | bytes accessed | tf_op | source)
XLA Modules:
  0.0 163.8 jit_solution(10650981009047231312)
XLA Ops:
  0.6 8.5 %all-to-all-start = ((bf16[16,16,256]{2,1,0:T(8,128)(2,1)}), bf16[16,16,256]{2,1,0:T(8,128)(2,1)S(1)}, u32[]{:S(2)}, u32[]{:S(2)}) async-start(bf16[16,16,256]{2,1,0:T(8,128)(2,1)} %bitcast.30), calls=%async_computation | async-start | bytes 262144 | tf_op jit(solution)/shard_map/all_to_all | solution.py:61
  9.8 1.2 pack.1
  11.0 5.1 %all-to-all-done = bf16[16,16,256]{2,1,0:T(8,128)(2,1)S(1)} async-done(((bf16[16,16,256]{2,1,0:T(8,128)(2,1)}), bf16[16,16,256]{2,1,0:T(8,128)(2,1)S(1)}, u32[]{:S(2)}, u32[]{:S(2)}) %all-to-all-start) | async-done | bytes 131104 | tf_op jit(solution)/shard_map/all_to_all | solution.py:61
  16.1 5.0 %collective-permute-start.1 = (bf16[40,128]{1,0:T(8,128)(2,1)S(1)}, bf16[40,128]{1,0:T(8,128)(2,1)S(1)}, u32[]{:S(2)}, u32[]{:S(2)}) collective-permute-start(bf16[40,128]{1,0:T(8,128)(2,1)S(1)} %pad_maximum_fusion.1), channel_id=1, source_target_pairs={{0,15},{1,2},{2,1},{3,4},{4,3},{5,6},{6,5},{7,8},{8,7},{9,10},{10,... | collective-permute-start | bytes 30728 | tf_op jit(solution)/shard_map/ppermute | solution.py:67
  21.0 0.0 collective-permute-start
  21.0 3.2 %collective-permute-start.2 = (bf16[16,128]{1,0:T(8,128)(2,1)S(1)}, bf16[16,128]{1,0:T(8,128)(2,1)S(1)}, u32[]{:S(2)}, u32[]{:S(2)}) collective-permute-start(bf16[16,128]{1,0:T(8,128)(2,1)S(1)} %slice.45), channel_id=1, source_target_pairs={{0,14},{1,15},{2,0},{3,1},{4,2},{5,3},{6,4},{7,5},{8,6},{9,7},{10,... | collective-permute-start | bytes 12296 | tf_op jit(solution)/shard_map/ppermute | solution.py:575
  24.2 1.0 collective-permute-done.1
  25.2 0.0 collective-permute-done
  25.2 0.3 collective-permute-done.2
  25.6 0.8 broadcast_in_dim.2
  26.4 10.2 %all-to-all-start.1 = ((bf16[16,88,128]{2,1,0:T(8,128)(2,1)}), bf16[16,88,128]{2,1,0:T(8,128)(2,1)S(1)}, u32[]{:S(2)}, u32[]{:S(2)}) async-start(bf16[16,88,128]{2,1,0:T(8,128)(2,1)} %broadcast_in_dim.2), calls=%async_computation.1 | async-start | bytes 720896 | tf_op jit(solution)/shard_map/all_to_all | solution.py:61
  36.6 0.1 multiply_add_fusion
  36.8 0.0 copy-start.1
  36.8 0.2 reshape.101
  37.0 0.8 pad.9.refs_2_
  37.8 1.8 %fusion.3.refs_3_ = bf16[1024,128]{1,0:T(8,128)(2,1)S(1)} fusion(bf16[128,1024]{1,0:T(8,128)(2,1)} %refs_3_.1, s32[1024]{0:T(1024)S(1)} %reshape.101), kind=kOutput, calls=%fused_computation.5 | convolution fusion | flops 269615104 | bytes 528384 | tf_op jit(solution)/shard_map/dot_general | solution.py:52
  39.5 1.7 %fusion.1.refs_4_.refs_8_ = bf16[1024,1024]{1,0:T(8,128)(2,1)} fusion(s32[1024]{0:T(1024)S(1)} %reshape.101), kind=kLoop, calls=%fused_computation.3 | loop fusion | flops 2097152 | bytes 2101248 | tf_op jit(solution)/shard_map/convert_element_type | solution.py:538
  41.3 0.1 reshape.89
  41.4 6.1 %all-to-all-done.1.refs_0_ = bf16[16,88,128]{2,1,0:T(8,128)(2,1)S(1)} async-done(((bf16[16,88,128]{2,1,0:T(8,128)(2,1)}), bf16[16,88,128]{2,1,0:T(8,128)(2,1)S(1)}, u32[]{:S(2)}, u32[]{:S(2)}) %all-to-all-start.1) | async-done | bytes 360480 | tf_op jit(solution)/shard_map/all_to_all | solution.py:61
  47.5 0.0 copy-done.1
  47.5 12.1 %forward.1 = (f32[256,128]{1,0:T(8,128)}, f32[128,1024]{1,0:T(8,128)}, f32[128,1024]{1,0:T(8,128)}, bf16[128,1024]{1,0:T(8,128)(2,1)}, f32[128,1024]{1,0:T(8,128...) custom-call(bf16[16,88,128]{2,1,0:T(8,128)(2,1)S(1)} %all-to-all-don, ...), custom_call_target="tpu_custom_call" | custom-call | tf_op jit(solution)/shard_map/forward/pallas_call | solution.py:479
  59.6 0.0 copy-start
  59.6 5.2 %all-to-all-start.2 = ((f32[16,16,128]{2,1,0:T(8,128)}), f32[16,16,128]{2,1,0:T(8,128)S(1)}, u32[]{:S(2)}, u32[]{:S(2)}) async-start(f32[16,16,128]{2,1,0:T(8,128)} %bitcast.11), calls=%async_computation.2 | async-start | bytes 262144 | tf_op jit(solution)/shard_map/all_to_all | solution.py:61
  64.9 1.1 copy.19
  65.9 4.7 %prepare.1 = (f32[1024,512]{1,0:T(8,128)}, bf16[1024,128]{1,0:T(8,128)(2,1)}, bf16[1024,128]{1,0:T(8,128)(2,1)}, bf16[128,512]{1,0:T(8,128)(2,1)}, bf16[6,256,12...) custom-call(f32[384,128]{1,0:T(8,128)} %get-tuple-element.44.refs_0_, f32[128,384]{1,0:T(8,128)S(1)} %bitcast.25, ...), custom_call_target="tpu_custom_call" | custom-call | tf_op jit(solution)/shard_map/prepare/pallas_call | solution.py:479
  70.6 1.2 all-to-all-done.2.refs_0_
  71.8 0.3 loss.1
  72.1 12.8 %all_to_all.30 = bf16[16,16,128]{2,1,0:T(8,128)(2,1)S(1)} all-to-all(bf16[16,16,128]{2,1,0:T(8,128)(2,1)S(1)} %loss.1), channel_id=1, replica_groups=mesh['zl'=4,'x'=4,'zh'=2,'y'=4,'core'=2] {'zl','x'}, dimensions={0} | all-to-all | bytes 131072 | tf_op jit(solution)/shard_map/all_to_all | solution.py:61
  84.9 0.0 collective-permute-start.4
  84.9 0.0 collective-permute-start.3
  84.9 10.4 %collective-permute-done.4.refs_2_ = bf16[256,128]{1,0:T(8,128)(2,1)S(1)} collective-permute-done((bf16[256,128]{1,0:T(8,128)(2,1)S(1)}, bf16[256,128]{1,0:T(8,128)(2,1)S(1)}, u32[]{:S(2)}, u32[]{:S(2)}) %collective-permute-start.4) | collective-permute-done | bytes 65568 | tf_op jit(solution)/shard_map/ppermute | solution.py:67
  95.3 0.0 collective-permute-done.3.refs_0_
  95.3 0.0 copy-done
  95.3 14.9 %backward.1 = (bf16[512,2432]{1,0:T(8,128)(2,1)S(1)}, bf16[512,2432]{1,0:T(8,128)(2,1)S(1)}) custom-call(bf16[256,128]{1,0:T(8,128)(2,1)S(1)} %collective-permute-done.3.refs_0_, bf16[256,128]{1,0:T(8,128)(2,1)S(1)} %bitcast.28, bf16[256,128]{1,0:T(8,128)(2,1)S(1)} %collective-permute-done.4.refs_2_, bf16[512,128]{1,0:T(8,128)(2,1)S(1)} %copy-done, ...), custom_call_target="tpu_custom_call" | custom-call | tf_op jit(solution)/shard_map/backward/pallas_call | solution.py:479
  110.2 0.1 collective-permute-start.5
  110.3 4.7 %collective-permute-done.5 = bf16[512,2432]{1,0:T(8,128)(2,1)S(1)} collective-permute-done((bf16[512,2432]{1,0:T(8,128)(2,1)S(1)}, bf16[512,2432]{1,0:T(8,128)(2,1)S(1)}, u32[]{:S(2)}, u32[]{:S(2)}) %collective-permute-start.5) | collective-permute-done | bytes 2490400 | tf_op jit(solution)/shard_map/ppermute | solution.py:686
  115.0 0.7 add_convert_fusion
  115.7 35.5 %all_to_all.31 = bf16[16,32,2432]{2,1,0:T(8,128)(2,1)S(1)} all-to-all(bf16[16,32,2432]{2,1,0:T(8,128)(2,1)S(1)} %bitcast.29), channel_id=1, replica_groups=mesh['zl'=4,'x'=4,'zh'=2,'y'=4,'core'=2] {'x','y'}, dimensions={0} | all-to-all | bytes 4980736 | tf_op jit(solution)/shard_map/all_to_all | solution.py:61
  151.2 0.4 reduce_sum.12
  151.6 11.4 %all_to_all.32.refs_0_ = bf16[8,4,2432]{2,1,0:T(4,128)(2,1)S(1)} all-to-all(bf16[8,4,2432]{2,1,0:T(4,128)(2,1)S(1)} %reshape.94), channel_id=1, replica_groups=mesh['zl'=4,'x'=4,'zh'=2,'y'=4,'core'=2] {'zl','zh'}, dimensions={0} | all-to-all | bytes 311296 | tf_op jit(solution)/shard_map/all_to_all | solution.py:61
  163.0 0.6 last.1
  (18 shorter events, 0.2 us)
Async XLA Ops:
  0.6 15.4 %all-to-all-start = ((bf16[16,16,256]{2,1,0:T(8,128)(2,1)}), bf16[16,16,256]{2,1,0:T(8,128)(2,1)S(1)}, u32[]{:S(2)}, u32[]{:S(2)}) async-start(bf16[16,16,256]{2,1,0:T(8,128)(2,1)} %bitcast.30), calls=%async_computation | async-start | bytes 262144 | tf_op jit(solution)/shard_map/all_to_all | solution.py:61
  16.1 9.1 %collective-permute-start.1 = (bf16[40,128]{1,0:T(8,128)(2,1)S(1)}, bf16[40,128]{1,0:T(8,128)(2,1)S(1)}, u32[]{:S(2)}, u32[]{:S(2)}) collective-permute-start(bf16[40,128]{1,0:T(8,128)(2,1)S(1)} %pad_maximum_fusion.1), channel_id=1, source_target_pairs={{0,15},{1,2},{2,1},{3,4},{4,3},{5,6},{6,5},{7,8},{8,7},{9,10},{10,... | collective-permute-start | bytes 30728 | tf_op jit(solution)/shard_map/ppermute | solution.py:67
  21.0 4.1 %collective-permute-start = (bf16[40,128]{1,0:T(8,128)(2,1)S(1)}, bf16[40,128]{1,0:T(8,128)(2,1)S(1)}, u32[]{:S(2)}, u32[]{:S(2)}) collective-permute-start(bf16[40,128]{1,0:T(8,128)(2,1)S(1)} %pad_maximum_fusion.1), channel_id=1, source_target_pairs={{0,1},{1,0},{2,3},{3,2},{4,5},{5,4},{6,7},{7,6},{8,9},{9,8},{10,11... | collective-permute-start | bytes 30728 | tf_op jit(solution)/shard_map/ppermute | solution.py:66
  21.0 4.5 %collective-permute-start.2 = (bf16[16,128]{1,0:T(8,128)(2,1)S(1)}, bf16[16,128]{1,0:T(8,128)(2,1)S(1)}, u32[]{:S(2)}, u32[]{:S(2)}) collective-permute-start(bf16[16,128]{1,0:T(8,128)(2,1)S(1)} %slice.45), channel_id=1, source_target_pairs={{0,14},{1,15},{2,0},{3,1},{4,2},{5,3},{6,4},{7,5},{8,6},{9,7},{10,... | collective-permute-start | bytes 12296 | tf_op jit(solution)/shard_map/ppermute | solution.py:575
  26.4 21.1 %all-to-all-start.1 = ((bf16[16,88,128]{2,1,0:T(8,128)(2,1)}), bf16[16,88,128]{2,1,0:T(8,128)(2,1)S(1)}, u32[]{:S(2)}, u32[]{:S(2)}) async-start(bf16[16,88,128]{2,1,0:T(8,128)(2,1)} %broadcast_in_dim.2), calls=%async_computation.1 | async-start | bytes 720896 | tf_op jit(solution)/shard_map/all_to_all | solution.py:61
  36.8 10.8 %copy-start.1 = (bf16[128,1024]{1,0:T(8,128)(2,1)S(1)}, bf16[128,1024]{1,0:T(8,128)(2,1)}, u32[]{:S(2)}) copy-start(bf16[128,1024]{1,0:T(8,128)(2,1)} %refs_3_.1) | copy-start | bytes 786436
  59.6 35.6 %copy-start = (bf16[512,128]{1,0:T(8,128)(2,1)S(1)}, bf16[512,128]{1,0:T(8,128)(2,1)}, u32[]{:S(2)}) copy-start(bf16[512,128]{1,0:T(8,128)(2,1)} %get-tuple-element.45.refs_2_.refs_3_) | copy-start | bytes 393220
  59.6 12.2 %all-to-all-start.2 = ((f32[16,16,128]{2,1,0:T(8,128)}), f32[16,16,128]{2,1,0:T(8,128)S(1)}, u32[]{:S(2)}, u32[]{:S(2)}) async-start(f32[16,16,128]{2,1,0:T(8,128)} %bitcast.11), calls=%async_computation.2 | async-start | bytes 262144 | tf_op jit(solution)/shard_map/all_to_all | solution.py:61
  84.9 10.4 %collective-permute-start.4 = (bf16[256,128]{1,0:T(8,128)(2,1)S(1)}, bf16[256,128]{1,0:T(8,128)(2,1)S(1)}, u32[]{:S(2)}, u32[]{:S(2)}) collective-permute-start(bf16[256,128]{1,0:T(8,128)(2,1)S(1)} %bitcast.26), channel_id=1, source_target_pairs={{0,15},{1,2},{2,1},{3,4},{4,3},{5,6},{6,5},{7,8},{8,7},{9,10},{10,... | collective-permute-start | bytes 196616 | tf_op jit(solution)/shard_map/ppermute | solution.py:67
  84.9 10.4 %collective-permute-start.3 = (bf16[256,128]{1,0:T(8,128)(2,1)S(1)}, bf16[256,128]{1,0:T(8,128)(2,1)S(1)}, u32[]{:S(2)}, u32[]{:S(2)}) collective-permute-start(bf16[256,128]{1,0:T(8,128)(2,1)S(1)} %bitcast.27), channel_id=1, source_target_pairs={{0,1},{1,0},{2,3},{3,2},{4,5},{5,4},{6,7},{7,6},{8,9},{9,8},{10,11... | collective-permute-start | bytes 196616 | tf_op jit(solution)/shard_map/ppermute | solution.py:66
  110.2 4.8 %collective-permute-start.5 = (bf16[512,2432]{1,0:T(8,128)(2,1)S(1)}, bf16[512,2432]{1,0:T(8,128)(2,1)S(1)}, u32[]{:S(2)}, u32[]{:S(2)}) collective-permute-start(bf16[512,2432]{1,0:T(8,128)(2,1)S(1)} %get-tuple-element.73), channel_id=1, source_target_pairs={{0,1},{1,0},{2,3},{3,2},{4,5},{5,4},{6,7},{7,6},{8,9},{9,8},{10,11... | collective-permute-start | bytes 7471112 | tf_op jit(solution)/shard_map/ppermute | solution.py:686

commit v8 on v7

--- a/solution.py
+++ b/solution.py
@@ -157,8 +157,8 @@
 def forward_kernel(k_enc, k_dec, need, push, *refs):
     got_ref, jitter_ref, wn_ref, we_ref, wq_ref, wo_ref, u_ref = refs[:7]
     (forecast_ref, pooled_ref, state0_ref, normed_ref, raw_ref, qn_ref, kn_ref, v_ref) = refs[7:15]
-    prob_ref, att_ref, state1_ref, dnorm_ref, facts_ref, near_ref = refs[15:21]
-    x_ref, msg_ref, all0_ref, proj_ref = refs[21:]
+    prob_ref, att_ref, state1_ref, dnorm_ref, facts_ref, near_ref, turned_ref = refs[15:22]
+    x_ref, msg_ref, all0_ref, proj_ref = refs[22:]
     attn = wo_ref.shape[0]
     reach = POINTS + 2 * RIM_G
     inv_root = HEAD_DIM ** (-0.5)
@@ -187,7 +187,8 @@
     facts_ref[:, 2 * k_enc : 2 * k_enc + 1] = facts[:, at - 1 : at]
     facts_ref[:, 2 * k_enc + 1 : 2 * k_enc + 1 + each] = facts[:, at : at + each]
     facts_ref[:, 2 * k_enc + 1 + each : 2 * k_enc + 1 + 2 * each] = scale
-    push(12, 13)
+    turned_ref[...] = facts_ref[...].T
+    push(12, 13, 14)
 
     def message_rows(i, carry):
         rows = pl.ds(pl.multiple_of(i * 128, 128), 128)
@@ -271,7 +272,7 @@
         place = interleave(parity, (POINTS, NODES), 0)
         high, low = split2(rest)
         forecast = forecast + dot(place, high, NN) + dot(place, low, NN)
-    forecast_ref[...] = forecast
+    forecast_ref[...] = forecast.astype(BF16)
 
 
 def prepare_kernel(k_enc, k_dec, need, push, *refs):
@@ -283,7 +284,7 @@
         rows = slice(r * quarter, (r + 1) * quarter)
         slope_ref[rows, :] = silu_slope(dot(wet_ref[rows, :], x_ref[...], NT))
     push(0)
-    need(4, 5, 6, 0)
+    need(4, 5, 6, 0, 1)
     for r in range(4):
         rows = slice(r * quarter, (r + 1) * quarter)
         nt_ref[rows, :] = dot(order_ref[rows, :], normed_ref[...], NT).astype(BF16)
@@ -424,7 +425,7 @@
 
 def loss_kernel(scale, need, push, cells_ref, truth_ref, out_ref):
     members = cells_ref.shape[0]
-    cells = [cells_ref[m] for m in range(members)]
+    cells = [cells_ref[m].astype(F32) for m in range(members)]
     fair = [jnp.zeros_like(cells[0]) for _ in range(members)]
     for m in range(members):
         for n in range(m + 1, members):
@@ -595,12 +596,13 @@
         ((ASKED, width), BF16),
         ((3 * nodes, channels), F32),
         ((points + 2 * RIM_G, channels), BF16),
+        ((channels, 3 * nodes), F32),
     ]
     forecast, *saved = call(
         functools.partial(forward_kernel, k_enc, k_dec),
         (got, jitter_all, w_noise, w_enc, w_qkv, w_out, unpacker_linear_map),
         (4, 5, 6),
-        [((points, channels), F32)] + residuals,
+        [((points, channels), BF16)] + residuals,
         tuple(range(1, 1 + len(residuals))),
         [
             ((4 * points, channels), BF16),
@@ -612,11 +614,11 @@
     )
 
     cells = swap(forecast.reshape(members, sub, channels), MEMBER)
-    pooled, state0, normed, raw, query, key, value, prob, attended, state1, dnorm, facts, near = saved
+    pooled, state0, normed, raw, query, key, value, prob, attended, state1, dnorm, facts, near, turn = saved
     prepared = call(
         functools.partial(prepare_kernel, k_enc, k_dec),
-        (facts, facts.T, near, w_enc_turned, reorder, normed, dnorm),
-        (2, 4, 5, 6, 0),
+        (facts, turn, near, w_enc_turned, reorder, normed, dnorm),
+        (2, 4, 5, 6, 0, 1),
         [
             ((width, points + 2 * RIM_G), F32),
             ((width, nodes), BF16),

time: 164 us -> 163 us (level)
  transfers between devices with their start and end apart: 9 -> 9, of which waited for: 7 -> 7; matrix products, arithmetic and copies ran while one was open for 4% -> 3% of each run, Pallas kernels for 4% -> 4%
where the time goes in v8:
time: 163 us
  blocking collectives  58.9 us (36%)
  Pallas kernels  33.9 us (21%)
  starting transfers between devices  32.2 us (20%)
  waiting for transfers between devices  29.4 us (18%)
  other arithmetic  2.98 us (2%)
  local copies, waits for them, and re-layouts  2 us (1%)
  matrix products  1.78 us (1%)
    all_to_all x3, blocking collectives, swap(): return lax.all_to_all(values, axes, split_axis=0, concat_axis=0, tiled=True)  58.9 us
    pallas_call x6, Pallas kernels, call(): pl.pallas_call(body, out_shape=[(pltpu.HBM if o in pushed and (not INTERP...  33.9 us
    all_to_all x3, starting transfers between devices, swap(): return lax.all_to_all(values, axes, split_axis=0, concat_axis=0, tiled=True)  24 us
    all_to_all x3, waiting for transfers between devices, swap(): return lax.all_to_all(values, axes, split_axis=0, concat_axis=0, tiled=True)  13 us
    ppermute x2, waiting for transfers between devices, exchanged(): lax.ppermute(values, GRID, [(i, (i + 1 if i % 2 else i - 1) % count) for...  11.3 us
    ppermute x2, starting transfers between devices, exchanged(): lax.ppermute(values, GRID, [(i, (i + 1 if i % 2 else i - 1) % count) for...  4.97 us
    ppermute x1, waiting for transfers between devices, per_device(): lax.ppermute(sent, 'core', [(0, 1), (1, 0)]).astype(F32)  4.71 us
  transfers between devices with their start and end apart: 9, of which 7 were waited for; matrix products, arithmetic and copies ran while one was open for 3% of the time, Pallas kernels for 4%

profile of v8, /device:TPU:32, one launch (start us, length us, event | category | flops | bytes accessed | tf_op | source)
XLA Modules:
  0.0 162.8 jit_solution(973205598703723668)
XLA Ops:
  0.6 8.5 %all-to-all-start = ((bf16[16,16,256]{2,1,0:T(8,128)(2,1)}), bf16[16,16,256]{2,1,0:T(8,128)(2,1)S(1)}, u32[]{:S(2)}, u32[]{:S(2)}) async-start(bf16[16,16,256]{2,1,0:T(8,128)(2,1)} %bitcast.28), calls=%async_computation | async-start | bytes 262144 | tf_op jit(solution)/shard_map/all_to_all | solution.py:61
  9.8 1.2 pack.1
  11.0 5.1 %all-to-all-done = bf16[16,16,256]{2,1,0:T(8,128)(2,1)S(1)} async-done(((bf16[16,16,256]{2,1,0:T(8,128)(2,1)}), bf16[16,16,256]{2,1,0:T(8,128)(2,1)S(1)}, u32[]{:S(2)}, u32[]{:S(2)}) %all-to-all-start) | async-done | bytes 131104 | tf_op jit(solution)/shard_map/all_to_all | solution.py:61
  16.1 5.0 %collective-permute-start.1 = (bf16[40,128]{1,0:T(8,128)(2,1)S(1)}, bf16[40,128]{1,0:T(8,128)(2,1)S(1)}, u32[]{:S(2)}, u32[]{:S(2)}) collective-permute-start(bf16[40,128]{1,0:T(8,128)(2,1)S(1)} %pad_maximum_fusion.1), channel_id=1, source_target_pairs={{0,15},{1,2},{2,1},{3,4},{4,3},{5,6},{6,5},{7,8},{8,7},{9,10},{10,... | collective-permute-start | bytes 30728 | tf_op jit(solution)/shard_map/ppermute | solution.py:67
  21.0 0.0 collective-permute-start
  21.0 3.2 %collective-permute-start.2 = (bf16[16,128]{1,0:T(8,128)(2,1)S(1)}, bf16[16,128]{1,0:T(8,128)(2,1)S(1)}, u32[]{:S(2)}, u32[]{:S(2)}) collective-permute-start(bf16[16,128]{1,0:T(8,128)(2,1)S(1)} %slice.45), channel_id=1, source_target_pairs={{0,14},{1,15},{2,0},{3,1},{4,2},{5,3},{6,4},{7,5},{8,6},{9,7},{10,... | collective-permute-start | bytes 12296 | tf_op jit(solution)/shard_map/ppermute | solution.py:576
  24.2 1.0 collective-permute-done.1
  25.2 0.0 collective-permute-done
  25.2 0.3 collective-permute-done.2
  25.6 0.8 broadcast_in_dim.2
  26.4 10.2 %all-to-all-start.1 = ((bf16[16,88,128]{2,1,0:T(8,128)(2,1)}), bf16[16,88,128]{2,1,0:T(8,128)(2,1)S(1)}, u32[]{:S(2)}, u32[]{:S(2)}) async-start(bf16[16,88,128]{2,1,0:T(8,128)(2,1)} %broadcast_in_dim.2), calls=%async_computation.1 | async-start | bytes 720896 | tf_op jit(solution)/shard_map/all_to_all | solution.py:61
  36.6 0.1 multiply_add_fusion
  36.8 0.0 copy-start.1
  36.8 0.2 reshape.101
  37.0 0.8 pad.9.refs_2_
  37.8 1.8 %fusion.3.refs_3_ = bf16[1024,128]{1,0:T(8,128)(2,1)S(1)} fusion(bf16[128,1024]{1,0:T(8,128)(2,1)} %refs_3_.1, s32[1024]{0:T(1024)S(1)} %reshape.101), kind=kOutput, calls=%fused_computation.5 | convolution fusion | flops 269615104 | bytes 528384 | tf_op jit(solution)/shard_map/dot_general | solution.py:52
  39.5 1.7 %fusion.1.refs_4_.refs_8_ = bf16[1024,1024]{1,0:T(8,128)(2,1)} fusion(s32[1024]{0:T(1024)S(1)} %reshape.101), kind=kLoop, calls=%fused_computation.3 | loop fusion | flops 2097152 | bytes 2101248 | tf_op jit(solution)/shard_map/convert_element_type | solution.py:539
  41.3 0.1 reshape.89
  41.4 6.1 %all-to-all-done.1.refs_0_ = bf16[16,88,128]{2,1,0:T(8,128)(2,1)S(1)} async-done(((bf16[16,88,128]{2,1,0:T(8,128)(2,1)}), bf16[16,88,128]{2,1,0:T(8,128)(2,1)S(1)}, u32[]{:S(2)}, u32[]{:S(2)}) %all-to-all-start.1) | async-done | bytes 360480 | tf_op jit(solution)/shard_map/all_to_all | solution.py:61
  47.5 0.0 copy-done.1
  47.5 12.2 %forward.1 = (bf16[256,128]{1,0:T(8,128)(2,1)}, f32[128,1024]{1,0:T(8,128)}, f32[128,1024]{1,0:T(8,128)}, bf16[128,1024]{1,0:T(8,128)(2,1)}, f32[128,1024]{1,0:T...) custom-call(bf16[16,88,128]{2,1,0:T(8,128)(2,1)S(1)} %all-to-all-don, ...), custom_call_target="tpu_custom_call" | custom-call | tf_op jit(solution)/shard_map/forward/pallas_call | solution.py:480
  59.7 0.0 copy-start
  59.7 5.2 %all-to-all-start.2 = ((bf16[16,16,128]{2,1,0:T(8,128)(2,1)}), bf16[16,16,128]{2,1,0:T(8,128)(2,1)S(1)}, u32[]{:S(2)}, u32[]{:S(2)}) async-start(bf16[16,16,128]{2,1,0:T(8,128)(2,1)} %bitcast.11), calls=%async_computation.2 | async-start | bytes 131072 | tf_op jit(solution)/shard_map/all_to_all | solution.py:61
  65.0 4.7 %prepare.1 = (f32[1024,512]{1,0:T(8,128)}, bf16[1024,128]{1,0:T(8,128)(2,1)}, bf16[1024,128]{1,0:T(8,128)(2,1)}, bf16[128,512]{1,0:T(8,128)(2,1)}, bf16[6,256,12...) custom-call(f32[384,128]{1,0:T(8,128)} %get-tuple-element.45.refs_0_, f32[128,384]{1,0:T(8,128)} %get-tuple-element.46.refs_1_, ...), custom_call_target="tpu_custom_call" | custom-call | tf_op jit(solution)/shard_map/prepare/pallas_call | solution.py:480
  69.7 1.9 %all-to-all-done.2.refs_0_ = bf16[16,16,128]{2,1,0:T(8,128)(2,1)S(1)} async-done(((bf16[16,16,128]{2,1,0:T(8,128)(2,1)}), bf16[16,16,128]{2,1,0:T(8,128)(2,1)S(1)}, u32[]{:S(2)}, u32[]{:S(2)}) %all-to-all-start.2) | async-done | bytes 65568 | tf_op jit(solution)/shard_map/all_to_all | solution.py:61
  71.6 0.3 loss.1
  71.9 12.0 %all_to_all.30 = bf16[16,16,128]{2,1,0:T(8,128)(2,1)S(1)} all-to-all(bf16[16,16,128]{2,1,0:T(8,128)(2,1)S(1)} %loss.1), channel_id=1, replica_groups=mesh['zl'=4,'x'=4,'zh'=2,'y'=4,'core'=2] {'zl','x'}, dimensions={0} | all-to-all | bytes 131072 | tf_op jit(solution)/shard_map/all_to_all | solution.py:61
  83.9 0.0 collective-permute-start.4
  83.9 0.0 collective-permute-start.3
  83.9 10.4 %collective-permute-done.4.refs_2_ = bf16[256,128]{1,0:T(8,128)(2,1)S(1)} collective-permute-done((bf16[256,128]{1,0:T(8,128)(2,1)S(1)}, bf16[256,128]{1,0:T(8,128)(2,1)S(1)}, u32[]{:S(2)}, u32[]{:S(2)}) %collective-permute-start.4) | collective-permute-done | bytes 65568 | tf_op jit(solution)/shard_map/ppermute | solution.py:67
  94.3 0.0 collective-permute-done.3.refs_0_
  94.3 0.0 copy-done
  94.3 14.9 %backward.1 = (bf16[512,2432]{1,0:T(8,128)(2,1)S(1)}, bf16[512,2432]{1,0:T(8,128)(2,1)S(1)}) custom-call(bf16[256,128]{1,0:T(8,128)(2,1)S(1)} %collective-permute-done.3.refs_0_, bf16[256,128]{1,0:T(8,128)(2,1)S(1)} %bitcast.26, bf16[256,128]{1,0:T(8,128)(2,1)S(1)} %collective-permute-done.4.refs_2_, bf16[512,128]{1,0:T(8,128)(2,1)S(1)} %copy-done, ...), custom_call_target="tpu_custom_call" | custom-call | tf_op jit(solution)/shard_map/backward/pallas_call | solution.py:480
  109.3 0.1 collective-permute-start.5
  109.4 4.7 %collective-permute-done.5 = bf16[512,2432]{1,0:T(8,128)(2,1)S(1)} collective-permute-done((bf16[512,2432]{1,0:T(8,128)(2,1)S(1)}, bf16[512,2432]{1,0:T(8,128)(2,1)S(1)}, u32[]{:S(2)}, u32[]{:S(2)}) %collective-permute-start.5) | collective-permute-done | bytes 2490400 | tf_op jit(solution)/shard_map/ppermute | solution.py:688
  114.1 0.7 add_convert_fusion
  114.8 35.5 %all_to_all.31 = bf16[16,32,2432]{2,1,0:T(8,128)(2,1)S(1)} all-to-all(bf16[16,32,2432]{2,1,0:T(8,128)(2,1)S(1)} %bitcast.27), channel_id=1, replica_groups=mesh['zl'=4,'x'=4,'zh'=2,'y'=4,'core'=2] {'x','y'}, dimensions={0} | all-to-all | bytes 4980736 | tf_op jit(solution)/shard_map/all_to_all | solution.py:61
  150.2 0.4 reduce_sum.12
  150.7 11.4 %all_to_all.32.refs_0_ = bf16[8,4,2432]{2,1,0:T(4,128)(2,1)S(1)} all-to-all(bf16[8,4,2432]{2,1,0:T(4,128)(2,1)S(1)} %reshape.94), channel_id=1, replica_groups=mesh['zl'=4,'x'=4,'zh'=2,'y'=4,'core'=2] {'zl','zh'}, dimensions={0} | all-to-all | bytes 311296 | tf_op jit(solution)/shard_map/all_to_all | solution.py:61
  162.0 0.6 last.1
  (18 shorter events, 0.2 us)
Async XLA Ops:
  0.6 15.4 %all-to-all-start = ((bf16[16,16,256]{2,1,0:T(8,128)(2,1)}), bf16[16,16,256]{2,1,0:T(8,128)(2,1)S(1)}, u32[]{:S(2)}, u32[]{:S(2)}) async-start(bf16[16,16,256]{2,1,0:T(8,128)(2,1)} %bitcast.28), calls=%async_computation | async-start | bytes 262144 | tf_op jit(solution)/shard_map/all_to_all | solution.py:61
  16.1 9.1 %collective-permute-start.1 = (bf16[40,128]{1,0:T(8,128)(2,1)S(1)}, bf16[40,128]{1,0:T(8,128)(2,1)S(1)}, u32[]{:S(2)}, u32[]{:S(2)}) collective-permute-start(bf16[40,128]{1,0:T(8,128)(2,1)S(1)} %pad_maximum_fusion.1), channel_id=1, source_target_pairs={{0,15},{1,2},{2,1},{3,4},{4,3},{5,6},{6,5},{7,8},{8,7},{9,10},{10,... | collective-permute-start | bytes 30728 | tf_op jit(solution)/shard_map/ppermute | solution.py:67
  21.0 4.1 %collective-permute-start = (bf16[40,128]{1,0:T(8,128)(2,1)S(1)}, bf16[40,128]{1,0:T(8,128)(2,1)S(1)}, u32[]{:S(2)}, u32[]{:S(2)}) collective-permute-start(bf16[40,128]{1,0:T(8,128)(2,1)S(1)} %pad_maximum_fusion.1), channel_id=1, source_target_pairs={{0,1},{1,0},{2,3},{3,2},{4,5},{5,4},{6,7},{7,6},{8,9},{9,8},{10,11... | collective-permute-start | bytes 30728 | tf_op jit(solution)/shard_map/ppermute | solution.py:66
  21.0 4.5 %collective-permute-start.2 = (bf16[16,128]{1,0:T(8,128)(2,1)S(1)}, bf16[16,128]{1,0:T(8,128)(2,1)S(1)}, u32[]{:S(2)}, u32[]{:S(2)}) collective-permute-start(bf16[16,128]{1,0:T(8,128)(2,1)S(1)} %slice.45), channel_id=1, source_target_pairs={{0,14},{1,15},{2,0},{3,1},{4,2},{5,3},{6,4},{7,5},{8,6},{9,7},{10,... | collective-permute-start | bytes 12296 | tf_op jit(solution)/shard_map/ppermute | solution.py:576
  26.4 21.1 %all-to-all-start.1 = ((bf16[16,88,128]{2,1,0:T(8,128)(2,1)}), bf16[16,88,128]{2,1,0:T(8,128)(2,1)S(1)}, u32[]{:S(2)}, u32[]{:S(2)}) async-start(bf16[16,88,128]{2,1,0:T(8,128)(2,1)} %broadcast_in_dim.2), calls=%async_computation.1 | async-start | bytes 720896 | tf_op jit(solution)/shard_map/all_to_all | solution.py:61
  36.8 10.8 %copy-start.1 = (bf16[128,1024]{1,0:T(8,128)(2,1)S(1)}, bf16[128,1024]{1,0:T(8,128)(2,1)}, u32[]{:S(2)}) copy-start(bf16[128,1024]{1,0:T(8,128)(2,1)} %refs_3_.1) | copy-start | bytes 786436
  59.7 34.6 %copy-start = (bf16[512,128]{1,0:T(8,128)(2,1)S(1)}, bf16[512,128]{1,0:T(8,128)(2,1)}, u32[]{:S(2)}) copy-start(bf16[512,128]{1,0:T(8,128)(2,1)} %get-tuple-element.47.refs_2_.refs_3_) | copy-start | bytes 393220
  59.7 11.9 %all-to-all-start.2 = ((bf16[16,16,128]{2,1,0:T(8,128)(2,1)}), bf16[16,16,128]{2,1,0:T(8,128)(2,1)S(1)}, u32[]{:S(2)}, u32[]{:S(2)}) async-start(bf16[16,16,128]{2,1,0:T(8,128)(2,1)} %bitcast.11), calls=%async_computation.2 | async-start | bytes 131072 | tf_op jit(solution)/shard_map/all_to_all | solution.py:61
  83.9 10.4 %collective-permute-start.4 = (bf16[256,128]{1,0:T(8,128)(2,1)S(1)}, bf16[256,128]{1,0:T(8,128)(2,1)S(1)}, u32[]{:S(2)}, u32[]{:S(2)}) collective-permute-start(bf16[256,128]{1,0:T(8,128)(2,1)S(1)} %bitcast.24), channel_id=1, source_target_pairs={{0,15},{1,2},{2,1},{3,4},{4,3},{5,6},{6,5},{7,8},{8,7},{9,10},{10,... | collective-permute-start | bytes 196616 | tf_op jit(solution)/shard_map/ppermute | solution.py:67
  83.9 10.4 %collective-permute-start.3 = (bf16[256,128]{1,0:T(8,128)(2,1)S(1)}, bf16[256,128]{1,0:T(8,128)(2,1)S(1)}, u32[]{:S(2)}, u32[]{:S(2)}) collective-permute-start(bf16[256,128]{1,0:T(8,128)(2,1)S(1)} %bitcast.25), channel_id=1, source_target_pairs={{0,1},{1,0},{2,3},{3,2},{4,5},{5,4},{6,7},{7,6},{8,9},{9,8},{10,11... | collective-permute-start | bytes 196616 | tf_op jit(solution)/shard_map/ppermute | solution.py:66
  109.3 4.8 %collective-permute-start.5 = (bf16[512,2432]{1,0:T(8,128)(2,1)S(1)}, bf16[512,2432]{1,0:T(8,128)(2,1)S(1)}, u32[]{:S(2)}, u32[]{:S(2)}) collective-permute-start(bf16[512,2432]{1,0:T(8,128)(2,1)S(1)} %get-tuple-element.75), channel_id=1, source_target_pairs={{0,1},{1,0},{2,3},{3,2},{4,5},{5,4},{6,7},{7,6},{8,9},{9,8},{10,11... | collective-permute-start | bytes 7471112 | tf_op jit(solution)/shard_map/ppermute | solution.py:688
